TPU v7x, 32 devices: a whole 2x2x4 slice. The times are simulated.
32 devices in a mesh: ctx: 2 (over y), fsdp: 4 (over z), rep: 4 (over x, core).
Axes of the slice: x: 2, y: 2, z: 4, core: 2. Of those that a mesh axis runs over, the one named last changes fastest.
Arguments:
- tokens: bfloat16 [16, 256, 2048], P(('fsdp', 'rep'), 'ctx'), may hold values from -6 to 6
- cotangent: bfloat16 [16, 256, 2048], P(('fsdp', 'rep'), 'ctx'), may hold values from -6 to 6
- lengths: int32 [16], P(('fsdp', 'rep')), may hold values from 64 to 256, as said below
- first_gain: bfloat16 [2048], P('fsdp'), may hold values from 0.25 to 1.75
- joint_matrix: bfloat16 [2048, 1920], P('fsdp'), may hold values from -0.125 to 0.125
- query_gain: bfloat16 [64], P('fsdp'), may hold values from 0.25 to 1.75
- key_gain: bfloat16 [64], P('fsdp'), may hold values from 0.25 to 1.75
- out_weight: bfloat16 [1280, 2048], P('fsdp'), may hold values from -2 to 2
- second_gain: bfloat16 [2048], P('fsdp'), may hold values from 0.25 to 1.75
- expand_weight: bfloat16 [2048, 10240], P('fsdp'), may hold values from -0.125 to 0.125
- contract_weight: bfloat16 [5120, 2048], P('fsdp'), may hold values from -0.078125 to 0.078125
Outputs:
- layer_output: bfloat16 [16, 256, 2048], P(('fsdp', 'rep'), 'ctx')
- input_gradient: float32 [16, 256, 2048], P(('fsdp', 'rep'), 'ctx')
- first_gradient: float32 [2048], P('fsdp')
- joint_gradient: float32 [2048, 1920], P('fsdp')
- query_gradient: float32 [64], P('fsdp')
- key_gradient: float32 [64], P('fsdp')
- out_gradient: float32 [1280, 2048], P('fsdp')
- second_gradient: float32 [2048], P('fsdp')
- expand_gradient: float32 [2048, 10240], P('fsdp')
- contract_gradient: float32 [5120, 2048], P('fsdp')
Inputs may be any that keep to these rules, and one draw needn't show every extreme that they name: `lengths`: valid positions count from each slot's start; some slot is full and some slot has 64.
All inputs are finite; a program needn't handle non-finite values.
Results may differ from a plain program's by a relative error of at most 0.012.
Values may be sent and summed in bfloat16 or wider, within the bound.
No kernel may reach another device: no remote copies, remote signals or barrier semaphores. Data moves between devices by JAX's collectives and lax.ppermute only.
A program may use at most 384 MiB of HBM per device.

v0:
```python
import math

import jax
import jax.numpy as jnp
from jax import lax
from jax.sharding import PartitionSpec as P

QUERY_HEADS = 20
KEY_VALUE_HEADS = 5
HEAD_SIZE = 64
FF = 5120


epsilon = 1e-06
masked_fill_value = -1e30


def tables(positions, width):
    steps = jnp.arange(width // 2, dtype=jnp.float32)
    rates = jnp.exp(steps * (-2.0 * math.log(10000.0) / width))
    angles = positions.astype(jnp.float32)[:, None] * rates[None, :]
    return (jnp.cos(angles)[:, None, :], jnp.sin(angles)[:, None, :])


def rotate(field, cosine_table, sine_table):
    half = field.shape[-1] // 2
    first, second = (field[..., :half], field[..., half:])
    return jnp.concatenate(
        [first * cosine_table - second * sine_table, second * cosine_table + first * sine_table],
        axis=-1,
    )


def reverse_rotation(upstream, cosine_table, sine_table):
    half = upstream.shape[-1] // 2
    first, second = (upstream[..., :half], upstream[..., half:])
    return jnp.concatenate(
        [first * cosine_table + second * sine_table, second * cosine_table - first * sine_table],
        axis=-1,
    )


def rms_parts(field):
    inverse = lax.rsqrt(jnp.mean(field * field, axis=-1, keepdims=True) + epsilon)
    return (field * inverse, inverse)


def rms_back(upstream, normed, inverse):
    return inverse * (upstream - normed * jnp.mean(upstream * normed, axis=-1, keepdims=True))


def cross_product(left, right):
    return lax.dot_general(
        left, right, (((0,), (0,)), ((), ())), preferred_element_type=jnp.float32
    )


def against(left, right):
    return lax.dot_general(
        left, right, (((1,), (1,)), ((), ())), preferred_element_type=jnp.float32
    )


def block_scores(grouped_query, pair_all, start, positions, slot_length_value, stretch_factor):
    key_span_width = KEY_VALUE_HEADS * HEAD_SIZE
    block_pairing = lax.dynamic_slice_in_dim(pair_all, start, stretch_factor, 0)
    key_rows = block_pairing[:, :key_span_width].reshape(stretch_factor, KEY_VALUE_HEADS, HEAD_SIZE)
    value_rows = block_pairing[:, key_span_width:].reshape(
        stretch_factor, KEY_VALUE_HEADS, HEAD_SIZE
    )
    scores = jnp.einsum(
        "qgrd,kgd->grqk", grouped_query, key_rows, preferred_element_type=jnp.float32
    ) * HEAD_SIZE ** (-0.5)
    key_pos = start + jnp.arange(stretch_factor, dtype=jnp.int32)
    allowed = (key_pos[None, :] <= positions[:, None]) & (key_pos[None, :] < slot_length_value)
    scores = jnp.where(allowed, scores, masked_fill_value)
    return (scores, allowed, key_rows, value_rows)


def shards(
    tokens,
    cotangent,
    lengths,
    first_gain,
    joint_matrix,
    query_gain,
    key_gain,
    out_weight,
    second_gain,
    expand_weight,
    contract_weight,
):
    stretch_factor = tokens.shape[1]
    place = lax.axis_index("ctx")
    span = stretch_factor * lax.axis_size("ctx")
    slot_length_value = lengths[0]
    positions = place * stretch_factor + jnp.arange(stretch_factor, dtype=jnp.int32)
    valid = (positions < slot_length_value).astype(jnp.float32)[:, None]
    context_block_count = jnp.minimum(place, (slot_length_value - 1) // stretch_factor) + 1
    query_span_width = QUERY_HEADS * HEAD_SIZE
    key_span_width = KEY_VALUE_HEADS * HEAD_SIZE
    head_group = QUERY_HEADS // KEY_VALUE_HEADS
    scale = HEAD_SIZE ** (-0.5)
    gain_one, joint_full, query_scale, key_scale, out_full = (
        lax.all_gather(first_gain, "fsdp", axis=0, tiled=True),
        lax.all_gather(joint_matrix, "fsdp", axis=0, tiled=True),
        lax.all_gather(query_gain, "fsdp", axis=0, tiled=True),
        lax.all_gather(key_gain, "fsdp", axis=0, tiled=True),
        lax.all_gather(out_weight, "fsdp", axis=0, tiled=True),
    )
    rows = tokens[0].astype(jnp.float32)
    normed_one, inverse_one = rms_parts(rows)
    entry_one = (normed_one * gain_one.astype(jnp.float32)).astype(jnp.bfloat16)
    joint_projection = jnp.dot(entry_one, joint_full, preferred_element_type=jnp.float32)
    query_raw = joint_projection[:, :query_span_width].reshape(
        stretch_factor, QUERY_HEADS, HEAD_SIZE
    )
    unnormed_key = joint_projection[
        :, query_span_width : query_span_width + key_span_width
    ].reshape(stretch_factor, KEY_VALUE_HEADS, HEAD_SIZE)
    value_part = joint_projection[:, query_span_width + key_span_width :]
    cosine_table, sine_table = tables(positions, HEAD_SIZE)
    query_normed, query_inverse = rms_parts(query_raw)
    rotated_query = rotate(
        query_normed * query_scale.astype(jnp.float32), cosine_table, sine_table
    ).astype(jnp.bfloat16)
    key_normed, key_inverse = rms_parts(unnormed_key)
    key_rot = rotate(key_normed * key_scale.astype(jnp.float32), cosine_table, sine_table).astype(
        jnp.bfloat16
    )
    local_pair = jnp.concatenate(
        [key_rot.reshape(stretch_factor, key_span_width), value_part.astype(jnp.bfloat16)], axis=1
    )
    pair_all = lax.all_gather(local_pair, "ctx", axis=0, tiled=True)
    grouped_query = rotated_query.reshape(stretch_factor, KEY_VALUE_HEADS, head_group, HEAD_SIZE)

    def largest_step(index, carry):
        running, total = carry
        scores, allowed, key_rows, value_rows = block_scores(
            grouped_query,
            pair_all,
            index * stretch_factor,
            positions,
            slot_length_value,
            stretch_factor,
        )
        newer = jnp.maximum(running, jnp.max(scores, axis=-1))
        total = total * jnp.exp(running - newer) + jnp.sum(
            jnp.exp(scores - newer[..., None]), axis=-1
        )
        return (newer, total)

    largest_start = jnp.full(
        (KEY_VALUE_HEADS, head_group, stretch_factor), masked_fill_value, jnp.float32
    )
    running, total = lax.fori_loop(
        0,
        context_block_count,
        largest_step,
        (largest_start, jnp.zeros((KEY_VALUE_HEADS, head_group, stretch_factor), jnp.float32)),
    )
    log_total = running + jnp.log(total)

    def value_step(index, carry):
        rounded, exact = carry
        scores, allowed, key_rows, value_rows = block_scores(
            grouped_query,
            pair_all,
            index * stretch_factor,
            positions,
            slot_length_value,
            stretch_factor,
        )
        shares = jnp.where(allowed, jnp.exp(scores - log_total[..., None]), 0.0)
        rounded = rounded + jnp.einsum(
            "grqk,kgd->qgrd",
            shares.astype(jnp.bfloat16),
            value_rows,
            preferred_element_type=jnp.float32,
        )
        exact = exact + jnp.einsum(
            "grqk,kgd->qgrd",
            shares,
            value_rows.astype(jnp.float32),
            precision=lax.Precision.HIGHEST,
        )
        return (rounded, exact)

    blank_group = jnp.zeros((stretch_factor, KEY_VALUE_HEADS, head_group, HEAD_SIZE), jnp.float32)
    rounded, exact = lax.fori_loop(0, context_block_count, value_step, (blank_group, blank_group))
    mixed_output = rounded.reshape(stretch_factor, query_span_width).astype(jnp.bfloat16)
    hidden = rows + jnp.dot(mixed_output, out_full, preferred_element_type=jnp.float32)
    gain_two, expand_full, contract_full = (
        lax.all_gather(second_gain, "fsdp", axis=0, tiled=True),
        lax.all_gather(expand_weight, "fsdp", axis=0, tiled=True),
        lax.all_gather(contract_weight, "fsdp", axis=0, tiled=True),
    )
    normed_two, inverse_two = rms_parts(hidden)
    entry_two = (normed_two * gain_two.astype(jnp.float32)).astype(jnp.bfloat16)
    expanded = jnp.dot(entry_two, expand_full, preferred_element_type=jnp.float32)
    gate = expanded[:, :FF]
    upward = expanded[:, FF:]
    sigma = jax.nn.sigmoid(gate)
    activated = gate * sigma
    product = (activated * upward).astype(jnp.bfloat16)
    branch_two = jnp.dot(product, contract_full, preferred_element_type=jnp.float32)
    layer_output = ((hidden + branch_two) * valid).astype(jnp.bfloat16)
    gain_two, expand_full, contract_full = (
        lax.all_gather(second_gain, "fsdp", axis=0, tiled=True),
        lax.all_gather(expand_weight, "fsdp", axis=0, tiled=True),
        lax.all_gather(contract_weight, "fsdp", axis=0, tiled=True),
    )
    upstream = cotangent[0].astype(jnp.float32) * valid
    upstream_b = upstream.astype(jnp.bfloat16)
    contract_grad = cross_product(product, upstream_b)
    back_product = against(upstream_b, contract_full)
    grad_gate = back_product * upward * sigma * (1.0 + gate * (1.0 - sigma))
    grad_upward = back_product * activated
    grad_expanded = jnp.concatenate([grad_gate, grad_upward], axis=1).astype(jnp.bfloat16)
    expand_grad = cross_product(entry_two, grad_expanded)
    back_entry_two = against(grad_expanded, expand_full)
    second_grad = jnp.sum(back_entry_two * normed_two, axis=0)
    back_hidden = upstream + rms_back(
        back_entry_two * gain_two.astype(jnp.float32), normed_two, inverse_two
    )
    second_owned, expand_owned, contract_owned = (
        lax.psum_scatter(second_grad, "fsdp", scatter_dimension=0, tiled=True),
        lax.psum_scatter(expand_grad, "fsdp", scatter_dimension=0, tiled=True),
        lax.psum_scatter(contract_grad, "fsdp", scatter_dimension=0, tiled=True),
    )
    gain_one, joint_full, query_scale, key_scale, out_full = (
        lax.all_gather(first_gain, "fsdp", axis=0, tiled=True),
        lax.all_gather(joint_matrix, "fsdp", axis=0, tiled=True),
        lax.all_gather(query_gain, "fsdp", axis=0, tiled=True),
        lax.all_gather(key_gain, "fsdp", axis=0, tiled=True),
        lax.all_gather(out_weight, "fsdp", axis=0, tiled=True),
    )
    back_hidden_b = back_hidden.astype(jnp.bfloat16)
    out_grad = cross_product(mixed_output, back_hidden_b)
    mixed_backward = against(back_hidden_b, out_full).astype(jnp.bfloat16)
    group_backward = mixed_backward.reshape(stretch_factor, KEY_VALUE_HEADS, head_group, HEAD_SIZE)
    offset = jnp.transpose(jnp.sum(group_backward.astype(jnp.float32) * exact, axis=-1), (1, 2, 0))
    pair_all = lax.all_gather(local_pair, "ctx", axis=0, tiled=True)

    def grad_step(index, carry):
        grad_query, pair_grads = carry
        start = index * stretch_factor
        scores, allowed, key_rows, value_rows = block_scores(
            grouped_query, pair_all, start, positions, slot_length_value, stretch_factor
        )
        shares = jnp.where(allowed, jnp.exp(scores - log_total[..., None]), 0.0)
        back_shares = jnp.einsum(
            "qgrd,kgd->grqk", group_backward, value_rows, preferred_element_type=jnp.float32
        )
        back_scores = (shares * (back_shares - offset[..., None])).astype(jnp.bfloat16)
        grad_query = grad_query + jnp.einsum(
            "grqk,kgd->qgrd", back_scores, key_rows, preferred_element_type=jnp.float32
        )
        grad_keys = (
            jnp.einsum(
                "grqk,qgrd->kgd", back_scores, grouped_query, preferred_element_type=jnp.float32
            )
            * scale
        )
        grad_values = jnp.einsum(
            "grqk,qgrd->kgd",
            shares.astype(jnp.bfloat16),
            group_backward,
            preferred_element_type=jnp.float32,
        )
        block_grad = jnp.concatenate(
            [
                grad_keys.reshape(stretch_factor, key_span_width),
                grad_values.reshape(stretch_factor, key_span_width),
            ],
            axis=1,
        )
        pair_grads = lax.dynamic_update_slice_in_dim(pair_grads, block_grad, start, 0)
        return (grad_query, pair_grads)

    grad_query, pair_grads = lax.fori_loop(
        0,
        context_block_count,
        grad_step,
        (blank_group, jnp.zeros((span, 2 * key_span_width), jnp.float32)),
    )
    local_pairing = lax.psum_scatter(pair_grads, "ctx", scatter_dimension=0, tiled=True)
    back_query_rot = reverse_rotation(
        grad_query.reshape(stretch_factor, QUERY_HEADS, HEAD_SIZE) * scale, cosine_table, sine_table
    )
    query_gain_grad = jnp.sum(back_query_rot * query_normed, axis=(0, 1))
    grad_query_raw = rms_back(
        back_query_rot * query_scale.astype(jnp.float32), query_normed, query_inverse
    )
    rotated_key_backward = reverse_rotation(
        local_pairing[:, :key_span_width].reshape(stretch_factor, KEY_VALUE_HEADS, HEAD_SIZE),
        cosine_table,
        sine_table,
    )
    key_gain_grad = jnp.sum(rotated_key_backward * key_normed, axis=(0, 1))
    grad_key_raw = rms_back(
        rotated_key_backward * key_scale.astype(jnp.float32), key_normed, key_inverse
    )
    grad_joint = jnp.concatenate(
        [
            grad_query_raw.reshape(stretch_factor, query_span_width),
            grad_key_raw.reshape(stretch_factor, key_span_width),
            local_pairing[:, key_span_width:],
        ],
        axis=1,
    ).astype(jnp.bfloat16)
    joint_grad = cross_product(entry_one, grad_joint)
    back_entry_one = against(grad_joint, joint_full)
    first_grad = jnp.sum(back_entry_one * normed_one, axis=0)
    input_gradient = back_hidden + rms_back(
        back_entry_one * gain_one.astype(jnp.float32), normed_one, inverse_one
    )
    first_owned, joint_owned, query_owned, key_owned, out_owned = (
        lax.psum_scatter(first_grad, "fsdp", scatter_dimension=0, tiled=True),
        lax.psum_scatter(joint_grad, "fsdp", scatter_dimension=0, tiled=True),
        lax.psum_scatter(query_gain_grad, "fsdp", scatter_dimension=0, tiled=True),
        lax.psum_scatter(key_gain_grad, "fsdp", scatter_dimension=0, tiled=True),
        lax.psum_scatter(out_grad, "fsdp", scatter_dimension=0, tiled=True),
    )
    summed = lax.psum(
        (
            first_owned,
            joint_owned,
            query_owned,
            key_owned,
            out_owned,
            second_owned,
            expand_owned,
            contract_owned,
        ),
        ("ctx", "rep"),
    )
    return (layer_output[None], input_gradient[None]) + tuple(summed)


def solution(mesh):
    return jax.shard_map(
        shards,
        mesh=mesh,
        in_specs=(
            P(("fsdp", "rep"), "ctx", None),
            P(("fsdp", "rep"), "ctx", None),
            P(("fsdp", "rep")),
            P("fsdp"),
            P("fsdp", None),
            P("fsdp"),
            P("fsdp"),
            P("fsdp", None),
            P("fsdp"),
            P("fsdp", None),
            P("fsdp", None),
        ),
        out_specs=(
            P(("fsdp", "rep"), "ctx", None),
            P(("fsdp", "rep"), "ctx", None),
            P("fsdp"),
            P("fsdp", None),
            P("fsdp"),
            P("fsdp"),
            P("fsdp", None),
            P("fsdp"),
            P("fsdp", None),
            P("fsdp", None),
        ),
        check_vma=False,
    )
```

profile of v0, /device:TPU:0, one launch (start us, length us, event | category | flops | bytes accessed | tf_op | source)
XLA Modules:
  0.0 4372.4 jit_solution(18229859901072036340)
XLA Ops:
  10.8 13.5 all-gather
  26.1 12.9 all-reduce.10
  39.1 13.1 all-gather.1
  52.7 101.0 %all-gather.7.cloned.1.call-done = bf16[2048,1920]{1,0:T(8,128)(2,1)} async-done(((bf16[512,1920]{1,0:T(8,128)(2,1)}), bf16[2048,1920]{1,0:T(8,128)(2,1)}) %all-gather.7.cloned.1.call-update) | async-done | bytes 7864336 | tf_op jit(solution)/shard_map/all_gather | solution.py:106
  153.7 4.5 fusion.59
  160.3 6.8 all_gather.39
  169.5 2.4 while.39
  172.6 4.1 while.40
  174.3 1.2 fusion.135
  176.8 74.9 %all-gather.9.cloned.1.call-done = bf16[1280,2048]{1,0:T(8,128)(2,1)} async-done(((bf16[320,2048]{1,0:T(8,128)(2,1)}), bf16[1280,2048]{1,0:T(8,128)(2,1)}) %all-gather.9.cloned.1.call-update) | async-done | bytes 5242896 | tf_op jit(solution)/shard_map/all_gather | solution.py:109
  251.7 3.4 multiply_reduce_fusion.2
  255.2 696.3 %all-gather.11.cloned.1.call-done = bf16[2048,10240]{1,0:T(8,128)(2,1)} async-done(((bf16[512,10240]{1,0:T(8,128)(2,1)}), bf16[2048,10240]{1,0:T(8,128)(2,1)}) %all-gather.11.cloned.1.call-update) | async-done | bytes 41943056 | tf_op jit(solution)/shard_map/all_gather | solution.py:195
  951.5 21.9 fusion.64
  973.4 334.6 %all-gather.13.cloned.1.call-done = bf16[5120,2048]{1,0:T(8,128)(2,1)} async-done(((bf16[1280,2048]{1,0:T(8,128)(2,1)}), bf16[5120,2048]{1,0:T(8,128)(2,1)}) %all-gather.13.cloned.1.call-update) | async-done | bytes 20971536 | tf_op jit(solution)/shard_map/all_gather | solution.py:196
  1308.0 13.6 multiply_convert_fusion.1
  1321.6 20.5 multiply_reduce_fusion
  1342.5 1.0 copy-done.1
  1343.5 4.3 convolution_convert_fusion
  1349.7 6.1 while.41
  1351.7 1.2 fusion.149
  1352.9 1.1 fusion.150
  1355.9 6.9 fusion.48
  1365.1 2.1 copy.123
  1367.5 1.0 pad_maximum_fusion.4
  1368.5 2.2 copy.120
  1370.7 1.1 copy.122
  1371.8 3.0 multiply_reduce_fusion.3
  1374.8 1.7 reduce-scatter.8.cloned.1.call-done
  1378.6 1.0 slice.125
  1379.8 8.5 fusion.57
  1388.4 1.2 copy-done.5
  1389.6 17.5 fusion.51
  1407.4 30.9 fusion.32
  1438.4 119.1 %reduce-scatter.12.cloned.1.call-done = f32[320,2048]{1,0:T(8,128)} async-done(((f32[1280,2048]{1,0:T(8,128)}), f32[320,2048]{1,0:T(8,128)}) %reduce-scatter.12.cloned.1.call-update) | async-done | bytes 2621456 | tf_op jit(solution)/shard_map/reduce_scatter | solution.py:323
  1557.5 266.8 %reduce-scatter.10.cloned.1.call-done = f32[512,1920]{1,0:T(8,128)} async-done(((f32[2048,1920]{1,0:T(8,128)}), f32[512,1920]{1,0:T(8,128)}) %reduce-scatter.10.cloned.1.call-update) | async-done | bytes 3932176 | tf_op jit(solution)/shard_map/reduce_scatter | solution.py:320
  1824.2 689.9 %reduce-scatter.14.cloned.1.call-done = f32[1280,2048]{1,0:T(8,128)} async-done(((f32[5120,2048]{1,0:T(8,128)}), f32[1280,2048]{1,0:T(8,128)}) %reduce-scatter.14.cloned.1.call-update) | async-done | bytes 10485776 | tf_op jit(solution)/shard_map/reduce_scatter | solution.py:229
  2514.1 1368.5 %reduce-scatter.16.cloned.1.call-done = f32[512,10240]{1,0:T(8,128)} async-done(((f32[2048,10240]{1,0:T(8,128)}), f32[512,10240]{1,0:T(8,128)}) %reduce-scatter.16.cloned.1.call-update) | async-done | bytes 20971536
  3884.6 1.2 reduce_sum.152
  3885.8 10.7 fusion.31
  3896.8 6.1 fusion.44
  3902.9 19.1 all-reduce.9
  3922.3 13.2 all-reduce.7
  3935.5 1.3 fusion.43
  3936.8 400.2 %all-reduce.13.cloned.1.call-done = (f32[512,1920]{1,0:T(8,128)}, f32[320,2048]{1,0:T(8,128)}, f32[512,10240]{1,0:T(8,128)}, f32[1280,2048]{1,0:T(8,128)}) async-done(((f32[512,1920]{1,0:T(8,128)}, f32[320,2048]{1,0:T(8,128)}, f32[512,10240]{1,0:T(8,128)}, f32[1280,2048]{1,0:T(8,128)}), (f32[512,1920]{1,0:T(8,128)}, f32[320,2048]{1,0:T(8,128)}, f32[512,10240]{1,0:T(8,128)}, ...) | async-done | bytes 38010896 | tf_op jit(solution)/shard_map/psum | solution.py:325
  4337.1 4.4 copy.197
  4341.5 1.5 copy.198
  4343.0 18.0 copy.199
  4361.0 4.1 copy.200
  (214 shorter events, 26.4 us)
Async XLA Ops:
  7.2 146.6 %all-gather.7.cloned.1.call-start = ((), (), s32[]{:S(2)}) async-start(), calls=%async_computation.5 | async-start | bytes 9830400 | tf_op jit(solution)/shard_map/all_gather | solution.py:106
  7.9 243.8 %all-gather.9.cloned.1.call-start = ((), (), s32[]{:S(2)}) async-start(), calls=%async_computation.6 | async-start | bytes 6553600 | tf_op jit(solution)/shard_map/all_gather | solution.py:109
  8.7 942.8 %all-gather.11.cloned.1.call-start = ((), (), s32[]{:S(2)}) async-start(), calls=%async_computation.7 | async-start | bytes 52428800 | tf_op jit(solution)/shard_map/all_gather | solution.py:195
  9.4 1.4 copy-start.37
  9.4 15.0 copy-start.35
  9.4 16.2 copy-start.43
  9.4 16.5 copy-start.44
  9.4 29.7 copy-start.38
  9.4 42.9 copy-start
  9.5 1298.5 %all-gather.13.cloned.1.call-start = ((), (), s32[]{:S(2)}) async-start(), calls=%async_computation.8 | async-start | bytes 26214400 | tf_op jit(solution)/shard_map/all_gather | solution.py:196
  10.0 1366.5 %reduce-scatter.8.cloned.1.call-start = ((), (), s32[]{:S(2)}) async-start(), calls=%async_computation.9 | async-start | bytes 983040 | tf_op jit(solution)/shard_map/reduce_scatter | solution.py:287
  39.1 13.2 copy-start.39
  39.1 119.2 %copy-start.41 = (bf16[64]{0:T(256)(128)(2,1)}, bf16[64]{0:T(256)(128)(2,1)S(1)}, u32[]{:S(2)}) copy-start(bf16[64]{0:T(256)(128)(2,1)S(1)} %get-tuple-element.449) | copy-start | bytes 388
  39.1 120.4 %copy-start.31 = (f32[64]{0:T(128)}, f32[64]{0:T(128)S(1)}, u32[]{:S(2)}) copy-start(f32[64]{0:T(128)S(1)} %convert_element_type.96) | copy-start | bytes 772
  39.1 129.2 %copy-start.33 = (f32[64]{0:T(128)}, f32[64]{0:T(128)S(1)}, u32[]{:S(2)}) copy-start(f32[64]{0:T(128)S(1)} %convert_element_type.99) | copy-start | bytes 772
  52.3 1289.8 %copy-start.30 = (f32[128]{0:T(128)}, f32[128]{0:T(128)S(1)}, u32[]{:S(2)}) copy-start(f32[128]{0:T(128)S(1)} %compare_convert_fusion) | copy-start | bytes 1540
  52.5 105.7 %copy-start.26 = (f32[128]{0:T(128)}, f32[128]{0:T(128)S(1)}, u32[]{:S(2)}) copy-start(f32[128]{0:T(128)S(1)} %add_rsqrt_fusion.3) | copy-start | bytes 1540
  52.7 116.6 %copy-start.15 = (f32[128,32]{0,1:T(8,128)}, f32[128,32]{0,1:T(8,128)S(1)}, u32[]{:S(2)}) copy-start(f32[128,32]{0,1:T(8,128)S(1)} %get-tuple-element.481) | copy-start | bytes 49156
  52.7 116.6 %copy-start.17 = (f32[128,32]{0,1:T(8,128)}, f32[128,32]{0,1:T(8,128)S(1)}, u32[]{:S(2)}) copy-start(f32[128,32]{0,1:T(8,128)S(1)} %get-tuple-element.482) | copy-start | bytes 49156
  159.4 7.7 copy-start.8
  176.8 78.4 %copy-start.10 = (bf16[128,5,4,64]{0,3,2,1:T(8,128)(2,1)}, bf16[128,5,4,64]{0,3,2,1:T(8,128)(2,1)S(1)}, u32[]{:S(2)}) copy-start(bf16[128,5,4,64]{0,3,2,1:T(8,128)(2,1)S(1)} %convert_element_type.100) | copy-start | bytes 983044
  255.2 1086.9 %copy-start.23 = (f32[128]{0:T(128)}, f32[128]{0:T(128)S(1)}, u32[]{:S(2)}) copy-start(f32[128]{0:T(128)S(1)} %add_rsqrt_fusion.2) | copy-start | bytes 1540
  951.5 356.5 %copy-start.12 = (bf16[1,128,2048]{2,1,0:T(8,128)(2,1)S(1)}, bf16[1,128,2048]{2,1,0:T(8,128)(2,1)}, u32[]{:S(2)}) copy-start(bf16[1,128,2048]{2,1,0:T(8,128)(2,1)} %param.18) | copy-start | bytes 1572868
  1355.9 201.6 %reduce-scatter.12.cloned.1.call-start = ((), (), s32[]{:S(2)}) async-start(), calls=%async_computation.11 | async-start | bytes 13107200 | tf_op jit(solution)/shard_map/reduce_scatter | solution.py:323
  1362.9 4.4 copy-start.16
  1362.9 4.4 copy-start.18
  1362.9 4.5 copy-start.4
  1362.9 4.5 copy-start.34
  1362.9 461.3 %reduce-scatter.10.cloned.1.call-start = ((), (), s32[]{:S(2)}) async-start(), calls=%async_computation.10 | async-start | bytes 19660800 | tf_op jit(solution)/shard_map/reduce_scatter | solution.py:320
  1367.5 4.3 copy-start.7
  1370.7 6.9 copy-start.9
  1371.8 5.8 copy-start.22
  1371.8 5.9 copy-start.32
  1371.8 6.0 copy-start.29
  1371.8 8.0 copy-start.27
  1374.8 4.9 copy-start.13
  1388.3 1125.8 %reduce-scatter.14.cloned.1.call-start = ((), (), s32[]{:S(2)}) async-start(), calls=%async_computation.12 | async-start | bytes 52428800 | tf_op jit(solution)/shard_map/reduce_scatter | solution.py:229
  1407.1 2475.5 %reduce-scatter.16.cloned.1.call-start = ((), (), s32[]{:S(2)}) async-start(), calls=%async_computation.13 | async-start | bytes 104857600
  1438.3 2898.7 %all-reduce.13.cloned.1.call-start = ((), (), s32[]{:S(2)}) async-start(), calls=%async_computation.14 | async-start | bytes 76021760 | tf_op jit(solution)/shard_map/psum | solution.py:325
  3885.8 10.7 copy-start.14
  3885.8 10.9 copy-start.28
  3896.8 6.1 copy-start.24
  3896.8 6.1 copy-start.36
  3896.8 38.7 copy-start.2
  4337.1 4.4 copy-start.11
  4341.5 19.5 slice-start
  4343.0 18.0 slice-start.1
  4343.0 18.0 slice-start.2
  (10 other events, 9.7 us)
Sparse Core Ops, SparseCore 0:
  9.6 144.1 all-gather.6
  155.3 96.3 all-gather.8
  253.3 698.1 all-gather.10
  952.9 355.0 all-gather.12
  1356.0 20.4 reduce-scatter.7
  1379.4 177.9 reduce-scatter.11
  1560.5 263.6 reduce-scatter.9
  1826.7 687.3 reduce-scatter.13
  2516.5 1366.0 reduce-scatter.15
  3887.3 449.7 all-reduce.12
where the time goes:
time: 4380 us; the launch traced here: 4370 us
  waiting for transfers between devices  4060 us (93%)
  matrix products  155 us (4%)
  blocking collectives  78.7 us (2%)
  local copies, waits for them, and re-layouts  51 us (1%)
    unnamed x11, waiting for transfers between devices  1370 us
    all_gather x1, waiting for transfers between devices, shards(): lax.all_gather(expand_weight, 'fsdp', axis=0, tiled=True)  696 us
    reduce_scatter x1, waiting for transfers between devices, shards(): lax.psum_scatter(contract_grad, 'fsdp', scatter_dimension=0, tiled=True)  690 us
    psum x1, waiting for transfers between devices, shards(): lax.psum((first_owned, joint_owned, query_owned, key_owned, out_owned, se...  400 us
    all_gather x1, waiting for transfers between devices, shards(): lax.all_gather(contract_weight, 'fsdp', axis=0, tiled=True)  335 us
    reduce_scatter x1, waiting for transfers between devices, shards(): lax.psum_scatter(joint_grad, 'fsdp', scatter_dimension=0, tiled=True)  267 us
    reduce_scatter x1, waiting for transfers between devices, shards(): lax.psum_scatter(out_grad, 'fsdp', scatter_dimension=0, tiled=True)  119 us
    all_gather x1, waiting for transfers between devices, shards(): lax.all_gather(joint_matrix, 'fsdp', axis=0, tiled=True)  101 us
  transfers between devices with their start and end apart: 10, of which 10 were waited for; matrix products, arithmetic and copies ran while one was open for 3% of the time, Pallas kernels for 0%

commit v1 on v0

v1 whole, which is shorter than its diff:
```python
import functools
import math

import jax
import jax.numpy as jnp
from jax import lax
from jax.experimental import pallas as pl
from jax.experimental.pallas import tpu as pltpu
from jax.sharding import PartitionSpec as P

QUERY_HEADS = 20
KEY_VALUE_HEADS = 5
HEAD_SIZE = 64
FF = 5120
LANES = 128

epsilon = 1e-06
masked_fill_value = -1e30
PLANE = ("ctx", "rep")
BF = jnp.bfloat16
F32 = jnp.float32


def tables(positions, width):
    steps = jnp.arange(width // 2, dtype=jnp.float32)
    rates = jnp.exp(steps * (-2.0 * math.log(10000.0) / width))
    angles = positions.astype(jnp.float32)[:, None] * rates[None, :]
    return (jnp.cos(angles)[:, None, :], jnp.sin(angles)[:, None, :])


def rotate(field, cosine_table, sine_table):
    half = field.shape[-1] // 2
    first, second = (field[..., :half], field[..., half:])
    return jnp.concatenate(
        [first * cosine_table - second * sine_table, second * cosine_table + first * sine_table],
        axis=-1,
    )


def reverse_rotation(upstream, cosine_table, sine_table):
    half = upstream.shape[-1] // 2
    first, second = (upstream[..., :half], upstream[..., half:])
    return jnp.concatenate(
        [first * cosine_table + second * sine_table, second * cosine_table - first * sine_table],
        axis=-1,
    )


def rms_parts(field):
    inverse = lax.rsqrt(jnp.mean(field * field, axis=-1, keepdims=True) + epsilon)
    return (field * inverse, inverse)


def rms_back(upstream, normed, inverse):
    return inverse * (upstream - normed * jnp.mean(upstream * normed, axis=-1, keepdims=True))


def dot(left, right, dims, out=F32):
    got = lax.dot_general(left, right, (dims, ((), ())), preferred_element_type=F32)
    return got.astype(out)


def cross_product(left, right, out=F32):
    return dot(left, right, ((0,), (0,)), out)


def against(left, right, out=F32):
    return dot(left, right, ((1,), (1,)), out)


class Plane:
    def __init__(self):
        self.c, self.r, self.z = (lax.axis_size(a) for a in ("ctx", "rep", "fsdp"))
        self.size = self.c * self.r
        self.cube = self.c == 2 and self.r == 4
        self.y = lax.axis_index("ctx")
        rep = lax.axis_index("rep")
        self.x, self.core = rep // 2, rep % 2
        self.rank = self.y * self.r + rep
        self.layer = lax.axis_index("fsdp")

    def over_x(self, v):
        return lax.ppermute(v, "rep", [(i, i ^ 2) for i in range(4)])

    def over_core(self, v):
        return lax.ppermute(v, "rep", [(i, i ^ 1) for i in range(4)])

    def over_y(self, v):
        return lax.ppermute(v, "ctx", [(0, 1), (1, 0)])

    def gather(self, v, axis=0):
        if not self.cube:
            return lax.all_gather(v, PLANE, axis=axis, tiled=False)
        half = v.shape[0] // 2
        from_x, from_y = self.over_x(v), self.over_y(v)
        far_a = self.over_y(from_x[:half])
        far_b = self.over_x(from_y[half:])
        far = jnp.concatenate([far_a, far_b], axis=0)
        x, y = self.x, self.y
        near = place(
            [(v, 2 * y + x), (from_x, 2 * y + 1 - x), (from_y, 2 * (1 - y) + x), (far, 2 * (1 - y) + 1 - x)],
            4,
            axis,
        )
        other = self.over_core(near)
        both = place([(near, self.core), (other, 1 - self.core)], 2, axis + 1)
        return both.reshape(both.shape[:axis] + (8,) + both.shape[axis + 2 :])

    def scatter(self, v, axis=0):
        if not self.cube:
            moved = jnp.moveaxis(v, axis, 0)
            return lax.psum_scatter(moved.astype(BF), PLANE, scatter_dimension=0, tiled=False).astype(F32)
        v = v.reshape(v.shape[:axis] + (2, 2, 2) + v.shape[axis + 1 :])
        pick = lambda a, i, ax: lax.dynamic_index_in_dim(a, i, ax, keepdims=False)
        x, y, core = self.x, self.y, self.core
        got = self.over_core(pick(v, 1 - core, axis + 2).astype(BF))
        v = pick(v, core, axis + 2).astype(F32) + got.astype(F32)
        row, away = pick(v, y, axis), pick(v, 1 - y, axis)
        far = pick(away, 1 - x, axis).astype(BF)
        near_y, near_x, mine = pick(away, x, axis), pick(row, 1 - x, axis), pick(row, x, axis)
        half = far.shape[0] // 2
        got_x, got_y = self.over_x(far[:half]), self.over_y(far[half:])
        near_y = jnp.concatenate([near_y[:half] + got_x.astype(F32), near_y[half:]], axis=0)
        near_x = jnp.concatenate([near_x[:half], near_x[half:] + got_y.astype(F32)], axis=0)
        in_x, in_y = self.over_x(near_x.astype(BF)), self.over_y(near_y.astype(BF))
        return mine + in_x.astype(F32) + in_y.astype(F32)

    def layers_gather(self, v):
        z = self.z
        parts = [(v, self.layer)]
        for d in range(1, z):
            got = lax.ppermute(v, "fsdp", [(i, (i + d) % z) for i in range(z)])
            parts.append((got, (self.layer - d) % z))
        return place(parts, z, 0)

    def layers_scatter(self, v):
        z = self.z
        total = lax.dynamic_index_in_dim(v, self.layer, 0, keepdims=False).astype(F32)
        for d in range(1, z):
            out = lax.dynamic_index_in_dim(v, (self.layer + d) % z, 0, keepdims=False).astype(BF)
            total = total + lax.ppermute(out, "fsdp", [(i, (i + d) % z) for i in range(z)]).astype(F32)
        return total


def place(parts, count, axis):
    first = parts[0][0]
    shape = first.shape[:axis] + (count,) + first.shape[axis:]
    total = jnp.zeros(shape, first.dtype)
    for part, index in parts:
        total = lax.dynamic_update_index_in_dim(total, jnp.expand_dims(part, axis), index, axis)
    return total


def column_slices(matrix, rank, groups, width):
    rows, columns = matrix.shape
    span = columns // groups
    last = columns // LANES - 1
    block = min(128, rows)
    window = -(-(LANES - 1 + width) // LANES)
    if width % 32 == 0:
        window = -(-(LANES - 32 + width) // LANES)

    def body(rank_ref, *refs):
        out = refs[-1]
        for g in range(groups):
            parts = [refs[g * window + w][...].astype(F32) for w in range(window)]
            wide = jnp.concatenate(parts, axis=1)
            shift = (g * span + rank_ref[0] * width) % LANES
            wide = pltpu.roll(wide, (window * LANES - shift) % (window * LANES), 1)
            out[:, g * width : (g + 1) * width] = wide[:, :width].astype(out.dtype)

    def spec(g, w):
        def index(i, rank_ref):
            return (i, jnp.minimum((g * span + rank_ref[0] * width) // LANES + w, last))

        return pl.BlockSpec((block, LANES), index)

    return pl.pallas_call(
        body,
        out_shape=jax.ShapeDtypeStruct((rows, groups * width), matrix.dtype),
        grid_spec=pltpu.PrefetchScalarGridSpec(
            num_scalar_prefetch=1,
            grid=(rows // block,),
            in_specs=[spec(g, w) for g in range(groups) for w in range(window)],
            out_specs=pl.BlockSpec((block, groups * width), lambda i, rank_ref: (i, 0)),
        ),
        name="column_slices",
    )(rank[None].astype(jnp.int32), *([matrix] * (groups * window)))


def column_merge(parts, groups):
    ranks, rows, columns = parts.shape
    width = columns // groups
    block = 32

    def body(part_ref, out):
        for g in range(groups):
            pieces = [part_ref[k, :, g * width : (g + 1) * width].astype(F32) for k in range(ranks)]
            out[:, g * ranks * width : (g + 1) * ranks * width] = jnp.concatenate(pieces, axis=1)

    return pl.pallas_call(
        body,
        out_shape=jax.ShapeDtypeStruct((rows, ranks * columns), F32),
        grid=(rows // block,),
        in_specs=[pl.BlockSpec((ranks, block, columns), lambda i: (0, i, 0))],
        out_specs=pl.BlockSpec((block, ranks * columns), lambda i: (i, 0)),
        name="column_merge",
    )(parts)


def shards(
    tokens,
    cotangent,
    lengths,
    first_gain,
    joint_matrix,
    query_gain,
    key_gain,
    out_weight,
    second_gain,
    expand_weight,
    contract_weight,
):
    plane = Plane()
    members, layers, rank = plane.size, plane.z, plane.rank
    rows_here = tokens.shape[1]
    model = tokens.shape[2]
    place_ctx = lax.axis_index("ctx")
    contexts = lax.axis_size("ctx")
    span = rows_here * contexts
    slot_length_value = lengths[0]
    positions = place_ctx * rows_here + jnp.arange(rows_here, dtype=jnp.int32)
    valid = (positions < slot_length_value).astype(F32)[:, None]
    query_width = QUERY_HEADS * HEAD_SIZE
    key_width = KEY_VALUE_HEADS * HEAD_SIZE
    head_group = QUERY_HEADS // KEY_VALUE_HEADS
    scale = HEAD_SIZE ** (-0.5)
    joint_columns = joint_matrix.shape[1]

    sizes = [first_gain.shape[0], second_gain.shape[0], query_gain.shape[0], key_gain.shape[0]]
    packed = plane.layers_gather(jnp.concatenate([first_gain, second_gain, query_gain, key_gain]))
    gains, at = [], 0
    for size in sizes:
        gains.append(packed[:, at : at + size].reshape(-1).astype(F32))
        at += size
    gain_one, gain_two, query_scale, key_scale = gains

    joint_rows = joint_matrix.shape[0] // members
    out_rows = out_weight.shape[0] // members
    joint_share = plane.layers_gather(lax.dynamic_slice_in_dim(joint_matrix, rank * joint_rows, joint_rows, 0))
    joint_full = plane.gather(joint_share, axis=1).reshape(model, joint_columns)
    out_share = plane.layers_gather(lax.dynamic_slice_in_dim(out_weight, rank * out_rows, out_rows, 0))
    out_full = plane.gather(out_share, axis=1).reshape(query_width, model)

    units = contract_weight.shape[0] // members
    expand_share = column_slices(expand_weight, rank, 2 * layers, units)
    expand_part = lax.all_gather(expand_share, "fsdp", axis=0, tiled=True)
    contract_share = lax.dynamic_slice_in_dim(contract_weight, rank * units, units, 0)
    contract_part = lax.all_gather(contract_share, "fsdp", axis=0, tiled=True)
    width = units * layers

    upstream = cotangent[0].astype(F32) * valid
    upstream_all = plane.gather(upstream.astype(BF)).reshape(members * rows_here, model)

    rows = tokens[0].astype(F32)
    normed_one, inverse_one = rms_parts(rows)
    entry_one = (normed_one * gain_one).astype(BF)
    joint_projection = dot(entry_one, joint_full, ((1,), (0,)))
    query_raw = joint_projection[:, :query_width].reshape(rows_here, QUERY_HEADS, HEAD_SIZE)
    key_raw = joint_projection[:, query_width : query_width + key_width].reshape(
        rows_here, KEY_VALUE_HEADS, HEAD_SIZE
    )
    value_part = joint_projection[:, query_width + key_width :]
    cosine_table, sine_table = tables(positions, HEAD_SIZE)
    query_normed, query_inverse = rms_parts(query_raw)
    rotated_query = rotate(query_normed * query_scale, cosine_table, sine_table).astype(BF)
    key_normed, key_inverse = rms_parts(key_raw)
    key_rot = rotate(key_normed * key_scale, cosine_table, sine_table).astype(BF)
    local_pair = jnp.concatenate([key_rot.reshape(rows_here, key_width), value_part.astype(BF)], axis=1)
    if contexts == 2:
        earlier = lax.ppermute(local_pair, "ctx", [(0, 1)])
        first = place_ctx == 0
        pair_all = jnp.concatenate(
            [jnp.where(first, local_pair, earlier), jnp.where(first, 0, local_pair).astype(BF)], axis=0
        )
    else:
        pair_all = lax.all_gather(local_pair, "ctx", axis=0, tiled=True)
    key_all = pair_all[:, :key_width].reshape(span, KEY_VALUE_HEADS, HEAD_SIZE)
    value_all = pair_all[:, key_width:].reshape(span, KEY_VALUE_HEADS, HEAD_SIZE)
    grouped_query = rotated_query.reshape(rows_here, KEY_VALUE_HEADS, head_group, HEAD_SIZE)
    key_pos = jnp.arange(span, dtype=jnp.int32)
    allowed = (key_pos[None, :] <= positions[:, None]) & (key_pos[None, :] < slot_length_value)
    scores = jnp.einsum("qgrd,kgd->grqk", grouped_query, key_all, preferred_element_type=F32) * scale
    scores = jnp.where(allowed, scores, masked_fill_value)
    powers = jnp.where(allowed, jnp.exp(scores - jnp.max(scores, axis=-1, keepdims=True)), 0.0)
    shares = powers / jnp.sum(powers, axis=-1, keepdims=True)
    shares_b = shares.astype(BF)
    mixed = jnp.einsum("grqk,kgd->qgrd", shares_b, value_all, preferred_element_type=F32)
    mixed_output = mixed.reshape(rows_here, query_width).astype(BF)
    hidden = rows + dot(mixed_output, out_full, ((1,), (0,)))

    normed_two, inverse_two = rms_parts(hidden)
    entry_two = (normed_two * gain_two).astype(BF)
    entry_all = plane.gather(entry_two).reshape(members * rows_here, model)
    expanded = dot(entry_all, expand_part, ((1,), (0,)))
    gate, upward = expanded[:, :width], expanded[:, width:]
    sigma = jax.nn.sigmoid(gate)
    activated = gate * sigma
    product = (activated * upward).astype(BF)
    back_product = against(upstream_all, contract_part)
    grad_gate = back_product * upward * sigma * (1.0 + gate * (1.0 - sigma))
    grad_upward = back_product * activated
    grad_expanded = jnp.concatenate([grad_gate, grad_upward], axis=1).astype(BF)
    back_entry_share = against(grad_expanded, expand_part, BF)
    back_entry_two = plane.scatter(back_entry_share.reshape(members, rows_here, model))
    contract_grad = cross_product(product, upstream_all, BF)
    contract_owned = lax.psum_scatter(contract_grad, "fsdp", scatter_dimension=0, tiled=True)
    expand_grad = cross_product(entry_all, grad_expanded, BF)
    expand_owned = lax.psum_scatter(expand_grad, "fsdp", scatter_dimension=0, tiled=True)
    branch_share = dot(product, contract_part, ((1,), (0,)), BF)
    branch_two = plane.scatter(branch_share.reshape(members, rows_here, model))
    layer_output = ((hidden + branch_two) * valid).astype(BF)

    second_grad = jnp.sum(back_entry_two * normed_two, axis=0)
    back_hidden = upstream + rms_back(back_entry_two * gain_two, normed_two, inverse_two)

    back_hidden_b = back_hidden.astype(BF)
    out_grad = cross_product(mixed_output, back_hidden_b, BF)
    out_mine = plane.scatter(out_grad.reshape(layers, members, out_rows, model), axis=1)
    mixed_backward = against(back_hidden_b, out_full, BF)
    group_backward = mixed_backward.reshape(rows_here, KEY_VALUE_HEADS, head_group, HEAD_SIZE)
    back_shares = jnp.einsum("qgrd,kgd->grqk", group_backward, value_all, preferred_element_type=F32)
    offset = jnp.sum(shares * back_shares, axis=-1, keepdims=True)
    back_scores = (shares * (back_shares - offset)).astype(BF)
    grad_query = jnp.einsum("grqk,kgd->qgrd", back_scores, key_all, preferred_element_type=F32)
    grad_keys = jnp.einsum("grqk,qgrd->kgd", back_scores, grouped_query, preferred_element_type=F32) * scale
    grad_values = jnp.einsum("grqk,qgrd->kgd", shares_b, group_backward, preferred_element_type=F32)
    pair_grads = jnp.concatenate(
        [grad_keys.reshape(span, key_width), grad_values.reshape(span, key_width)], axis=1
    )
    if contexts == 2:
        later = lax.ppermute(pair_grads[:rows_here], "ctx", [(1, 0)])
        pair_mine = jnp.where(first, pair_grads[:rows_here] + later, pair_grads[rows_here:])
    else:
        pair_mine = lax.psum_scatter(pair_grads, "ctx", scatter_dimension=0, tiled=True)
    back_query_rot = reverse_rotation(
        grad_query.reshape(rows_here, QUERY_HEADS, HEAD_SIZE) * scale, cosine_table, sine_table
    )
    query_gain_grad = jnp.sum(back_query_rot * query_normed, axis=(0, 1))
    grad_query_raw = rms_back(back_query_rot * query_scale, query_normed, query_inverse)
    back_key_rot = reverse_rotation(
        pair_mine[:, :key_width].reshape(rows_here, KEY_VALUE_HEADS, HEAD_SIZE), cosine_table, sine_table
    )
    key_gain_grad = jnp.sum(back_key_rot * key_normed, axis=(0, 1))
    grad_key_raw = rms_back(back_key_rot * key_scale, key_normed, key_inverse)
    grad_joint = jnp.concatenate(
        [
            grad_query_raw.reshape(rows_here, query_width),
            grad_key_raw.reshape(rows_here, key_width),
            pair_mine[:, key_width:],
        ],
        axis=1,
    ).astype(BF)
    joint_grad = cross_product(entry_one, grad_joint, BF)
    joint_mine = plane.scatter(joint_grad.reshape(layers, members, joint_rows, joint_columns), axis=1)
    back_entry_one = against(grad_joint, joint_full)
    first_grad = jnp.sum(back_entry_one * normed_one, axis=0)
    input_gradient = back_hidden + rms_back(back_entry_one * gain_one, normed_one, inverse_one)

    out_owned = plane.layers_scatter(out_mine).astype(BF)
    joint_owned = plane.layers_scatter(joint_mine).astype(BF)
    out_gradient = plane.gather(out_owned).reshape(members * out_rows, model).astype(F32)
    joint_gradient = plane.gather(joint_owned).reshape(members * joint_rows, joint_columns).astype(F32)
    contract_gradient = plane.gather(contract_owned).reshape(members * units, model).astype(F32)
    expand_gradient = column_merge(plane.gather(expand_owned), 2 * layers)
    small = lax.psum(
        jnp.concatenate([first_grad, second_grad, query_gain_grad, key_gain_grad]), ("ctx", "fsdp", "rep")
    )
    owned, at = [], 0
    for size in sizes:
        owned.append(lax.dynamic_slice_in_dim(small, at + plane.layer * size, size))
        at += size * layers
    return (
        layer_output[None],
        input_gradient[None],
        owned[0],
        joint_gradient,
        owned[2],
        owned[3],
        out_gradient,
        owned[1],
        expand_gradient,
        contract_gradient,
    )


def solution(mesh):
    return jax.shard_map(
        shards,
        mesh=mesh,
        in_specs=(
            P(("fsdp", "rep"), "ctx", None),
            P(("fsdp", "rep"), "ctx", None),
            P(("fsdp", "rep")),
            P("fsdp"),
            P("fsdp", None),
            P("fsdp"),
            P("fsdp"),
            P("fsdp", None),
            P("fsdp"),
            P("fsdp", None),
            P("fsdp", None),
        ),
        out_specs=(
            P(("fsdp", "rep"), "ctx", None),
            P(("fsdp", "rep"), "ctx", None),
            P("fsdp"),
            P("fsdp", None),
            P("fsdp"),
            P("fsdp"),
            P("fsdp", None),
            P("fsdp"),
            P("fsdp", None),
            P("fsdp", None),
        ),
        check_vma=False,
    )
```

time: 4380 us -> 679 us (0.16)
  waiting for transfers between devices: 4060 us -> 272 us
  matrix products: 155 us -> 74.4 us
  starting transfers between devices: 0.65 us -> 79.7 us
  local copies, waits for them, and re-layouts: 51 us -> 114 us
    unnamed x11 -> x4, waiting for transfers between devices: 1370 us -> 0.07 us
    all_gather x4 -> x2, waiting for transfers between devices: 1210 us -> 38.4 us  [the longest x1 38.4 us: shards(): contract_part = lax.all_gather(contract_share, 'fsdp', axis=0, tiled=True)]
    reduce_scatter x1, waiting for transfers between devices: 690 us -> 0.01 us  [shards(): lax.psum_scatter(contract_grad, 'fsdp', scatter_dimension=0, tiled=True)]
    psum x1 -> x0, waiting for transfers between devices: 400 us -> none  [shards(): lax.psum((first_owned, joint_owned, query_owned, key_owned, out_owned, se...]
    reduce_scatter x3 -> x1, waiting for transfers between devices: 388 us -> 0.01 us  [shards(): lax.psum_scatter(expand_grad, 'fsdp', scatter_dimension=0, tiled=True)]
    ppermute x0 -> x77, waiting for transfers between devices: none -> 233 us  [the longest x24 134 us: over_y(): return lax.ppermute(v, 'ctx', [(0, 1), (1, 0)])]
    dot_general x21 -> x17, matrix products: 155 us -> 71.8 us  [the longest x12 64.2 us: dot(): lax.dot_general(left, right, (dims, ((), ())), preferred_element_type=F32)]
    ppermute x0 -> x77, starting transfers between devices: none -> 79.2 us  [the longest x24 25.3 us: over_y(): return lax.ppermute(v, 'ctx', [(0, 1), (1, 0)])]
  transfers between devices with their start and end apart: 10 -> 81, of which waited for: 10 -> 41; matrix products, arithmetic and copies ran while one was open for 3% -> 30% of each run, Pallas kernels for 0% -> 1%
where the time goes in v1:
time: 679 us; the launch traced here: 668 us
  waiting for transfers between devices  272 us (40%)
  local copies, waits for them, and re-layouts  114 us (17%)
  starting transfers between devices  79.7 us (12%)
  matrix products  74.4 us (11%)
  other arithmetic  46.7 us (7%)
  blocking collectives  43.2 us (6%)
  Pallas kernels  21.5 us (3%)
  between operations  16.9 us (2%)
    ppermute x24, waiting for transfers between devices, over_y(): return lax.ppermute(v, 'ctx', [(0, 1), (1, 0)])  134 us
    dot_general x12, matrix products, dot(): lax.dot_general(left, right, (dims, ((), ())), preferred_element_type=F32)  64.2 us
    dynamic_update_slice x49, local copies, waits for them, and re-layouts, place(): lax.dynamic_update_index_in_dim(total, jnp.expand_dims(part, axis), index...  45.5 us
    ppermute x9, waiting for transfers between devices, layers_gather(): got = lax.ppermute(v, 'fsdp', [(i, (i + d) % z) for i in range(z)])  43.5 us
    psum x1, blocking collectives, shards(): lax.psum(jnp.concatenate([first_grad, second_grad, query_gain_grad, key_g...  43.2 us
    all_gather x1, waiting for transfers between devices, shards(): contract_part = lax.all_gather(contract_share, 'fsdp', axis=0, tiled=True)  38.4 us
    ppermute x24, waiting for transfers between devices, over_x(): return lax.ppermute(v, 'rep', [(i, i ^ 2) for i in range(4)])  35.9 us
    ppermute x24, starting transfers between devices, over_y(): return lax.ppermute(v, 'ctx', [(0, 1), (1, 0)])  25.3 us
  transfers between devices with their start and end apart: 81, of which 41 were waited for; matrix products, arithmetic and copies ran while one was open for 30% of the time, Pallas kernels for 1%

profile of v1, /device:TPU:0, one launch (start us, length us, event | category | flops | bytes accessed | tf_op | source)
XLA Modules:
  0.0 668.4 jit_solution(9665672172217191534)
XLA Ops:
  8.3 3.1 collective-permute-start.3
  18.0 5.2 column_slices.1
  29.0 5.5 collective-permute-done.12
  34.5 37.2 %collective-permute-done.13 = bf16[40,2048]{1,0:T(8,128)(2,1)S(1)} collective-permute-done((bf16[40,2048]{1,0:T(8,128)(2,1)}, bf16[40,2048]{1,0:T(8,128)(2,1)S(1)}, u32[]{:S(2)}, u32[]{:S(2)}) %collective-permute-start.13) | collective-permute-done | bytes 163872 | tf_op jit(solution)/shard_map/ppermute | solution.py:132
  71.7 7.1 %collective-permute-start = (bf16[1056]{0:T(1024)(128)(2,1)}, bf16[1056]{0:T(1024)(128)(2,1)}, u32[]{:S(2)}, u32[]{:S(2)}) collective-permute-start(bf16[1056]{0:T(1024)(128)(2,1)} %concatenate.102), channel_id=1, source_target_pairs={{0,4},{4,8},{8,12},{12,0},{1,5},{5,9},{9,13},{13,1},{2,6},{6,10},{... | collective-permute-start | bytes 6344 | tf_op jit(solution)/shard_map/ppermute | solution.py:132
  89.3 8.8 %collective-permute-done.16 = bf16[4,40,2048]{2,1,0:T(8,128)(2,1)S(1)} collective-permute-done((bf16[4,40,2048]{2,1,0:T(8,128)(2,1)S(1)}, bf16[4,40,2048]{2,1,0:T(8,128)(2,1)S(1)}, u32[]{:S(2)}, u32[]{:S(2)}) %collective-permute-start.16) | collective-permute-done | bytes 655392 | tf_op jit(solution)/shard_map/ppermute | solution.py:89
  98.1 3.7 collective-permute-start.1
  103.3 12.5 %collective-permute-done.7 = bf16[4,64,1920]{2,1,0:T(8,128)(2,1)S(1)} collective-permute-done((bf16[4,64,1920]{2,1,0:T(8,128)(2,1)S(1)}, bf16[4,64,1920]{2,1,0:T(8,128)(2,1)S(1)}, u32[]{:S(2)}, u32[]{:S(2)}) %collective-permute-start.7) | collective-permute-done | bytes 983072 | tf_op jit(solution)/shard_map/ppermute | solution.py:89
  121.3 5.5 collective-permute-done.9
  132.0 3.2 collective-permute-start.2
  144.2 8.4 %collective-permute-done.31 = bf16[128,2048]{1,0:T(8,128)(2,1)S(1)} collective-permute-done((bf16[128,2048]{1,0:T(8,128)(2,1)S(1)}, bf16[128,2048]{1,0:T(8,128)(2,1)S(1)}, u32[]{:S(2)}, u32[]{:S(2)}) %collective-permute-start.31) | collective-permute-done | bytes 524320 | tf_op jit(solution)/shard_map/ppermute | solution.py:89
  165.7 4.6 bitcast_dynamic-update-slice_fusion.3
  196.6 6.9 %collective-permute-done.21 = bf16[128,2048]{1,0:T(8,128)(2,1)S(1)} collective-permute-done((bf16[128,2048]{1,0:T(8,128)(2,1)S(1)}, bf16[128,2048]{1,0:T(8,128)(2,1)S(1)}, u32[]{:S(2)}, u32[]{:S(2)}) %collective-permute-start.21) | collective-permute-done | bytes 524320 | tf_op jit(solution)/shard_map/ppermute | solution.py:89
  215.6 3.1 bitcast_dynamic-update-slice_fusion.9
  221.2 3.1 bitcast_dynamic-update-slice_fusion.10
  224.3 4.8 bitcast_dynamic-update-slice_fusion.8
  229.1 10.8 %fusion.120 = f32[1024,1280]{1,0:T(8,128)} fusion(bf16[1024,2048]{1,0:T(8,128)(2,1)} %bitcast.54, bf16[2048,1280]{1,0:T(8,128)(2,1)} %all-gather.3.cloned.1.call-done), kind=kOutput, calls=%fused_computation.319 | convolution fusion | flops 5368709120 | bytes 14680064 | tf_op jit(solution)/shard_map/dot_general | solution.py:59
  239.9 38.4 %all-gather.5.cloned.1.call-done = bf16[640,2048]{1,0:T(8,128)(2,1)} async-done(((bf16[160,2048]{1,0:T(8,128)(2,1)}), bf16[640,2048]{1,0:T(8,128)(2,1)}) %all-gather.5.cloned.1.call-update) | async-done | bytes 2621456 | tf_op jit(solution)/shard_map/all_gather | solution.py:259
  278.3 10.1 %multiply_convert_fusion.1 = (bf16[1024,640]{1,0:T(8,128)(2,1)}, bf16[1024,640]{1,0:T(8,128)(2,1)}, bf16[1024,640]{1,0:T(8,128)(2,1)S(1)}) fusion(f32[1024,1280]{1,0:T(8,128)} %fusion.120, bf16[1024,2048]{1,0:T(8,128)(2,1)} %bitcast.75, bf16[640,2048]{1,0:T(8,128)(2,1)} %all-gather.5.cloned.1.call-done), kind=kOutput, calls=%fused_computation.32 | convolution fusion | flops 2694184960 | bytes 15990784 | tf_op jit(solution)/shard_map/dot_general | solution.py:59
  289.5 6.6 convolution_convert_fusion.5
  299.3 8.8 %convolution_convert_fusion.3 = bf16[1024,2048]{1,0:T(8,128)(2,1)S(1)} fusion(bf16[2048,1280]{1,0:T(8,128)(2,1)} %all-gather.3.cloned.1.call-done, bf16[1024,640]{1,0:T(8,128)(2,1)} %get-tuple-element.34, bf16[1024,640]{1,0:T(8,128)(2,1)} %get-tuple-element.33), kind=kOutput, calls=%fused_computation.15 | convolution fusion | flops 5376049152 | bytes 12058624 | tf_op jit(solution)/shard_map/dot_general | solution.py:59
  312.4 3.6 convolution_convert_fusion.4
  319.9 11.1 %convolution_convert_fusion = bf16[2048,1280]{1,0:T(8,128)(2,1)} fusion(bf16[1024,2048]{1,0:T(8,128)(2,1)} %bitcast.54, bf16[1024,640]{1,0:T(8,128)(2,1)S(1)} %copy-done.63, bf16[1024,640]{1,0:T(8,128)(2,1)S(1)} %copy-done.62), kind=kOutput, calls=%fused_computation.2 | convolution fusion | flops 5376573440 | bytes 12058624 | tf_op jit(solution)/shard_map/dot_general | solution.py:59
  331.0 3.2 convert_add_fusion.2
  352.9 7.5 %collective-permute-done.39 = bf16[128,2048]{1,0:T(8,128)(2,1)S(1)} collective-permute-done((bf16[128,2048]{1,0:T(8,128)(2,1)S(1)}, bf16[128,2048]{1,0:T(8,128)(2,1)S(1)}, u32[]{:S(2)}, u32[]{:S(2)}) %collective-permute-start.39) | collective-permute-done | bytes 524320 | tf_op jit(solution)/shard_map/ppermute | solution.py:89
  362.8 8.4 %collective-permute-done.29 = bf16[128,2048]{1,0:T(8,128)(2,1)S(1)} collective-permute-done((bf16[128,2048]{1,0:T(8,128)(2,1)S(1)}, bf16[128,2048]{1,0:T(8,128)(2,1)S(1)}, u32[]{:S(2)}, u32[]{:S(2)}) %collective-permute-start.29) | collective-permute-done | bytes 524320 | tf_op jit(solution)/shard_map/ppermute | solution.py:89
  382.2 3.9 convolution_convert_fusion.1
  395.6 4.8 constant_dynamic-slice_fusion.1
  407.6 4.0 constant_dynamic-slice_fusion.3
  411.6 4.6 copy.209
  419.2 43.2 %psum.7 = f32[4224]{0:T(1024)S(1)} all-reduce(f32[4224]{0:T(1024)S(1)} %concatenate.124), channel_id=1, replica_groups=mesh['ctx'=2,'fsdp'=4,'rep'=4] {'ctx','fsdp','rep'}, use_global_device_ids=true, to_apply=%region_17.18 | all-reduce | flops 4224 | bytes 33792 | tf_op jit(solution)/shard_map/psum | solution.py:376
  467.3 3.6 convert_add_fusion.1
  473.7 15.1 %collective-permute-done.55 = bf16[2,40,2048]{2,1,0:T(8,128)(2,1)S(1)} collective-permute-done((bf16[2,40,2048]{2,1,0:T(8,128)(2,1)S(1)}, bf16[2,40,2048]{2,1,0:T(8,128)(2,1)S(1)}, u32[]{:S(2)}, u32[]{:S(2)}) %collective-permute-start.55) | collective-permute-done | bytes 327712 | tf_op jit(solution)/shard_map/ppermute | solution.py:89
  493.6 13.2 %collective-permute-done.58 = bf16[4,40,2048]{2,1,0:T(8,128)(2,1)S(1)} collective-permute-done((bf16[4,40,2048]{2,1,0:T(8,128)(2,1)S(1)}, bf16[4,40,2048]{2,1,0:T(8,128)(2,1)S(1)}, u32[]{:S(2)}, u32[]{:S(2)}) %collective-permute-start.58) | collective-permute-done | bytes 655392 | tf_op jit(solution)/shard_map/ppermute | solution.py:89
  514.3 7.2 %collective-permute-done.60 = bf16[40,2048]{1,0:T(8,128)(2,1)S(1)} collective-permute-done((bf16[40,2048]{1,0:T(8,128)(2,1)S(1)}, bf16[40,2048]{1,0:T(8,128)(2,1)S(1)}, u32[]{:S(2)}, u32[]{:S(2)}) %collective-permute-start.60) | collective-permute-done | bytes 163872 | tf_op jit(solution)/shard_map/ppermute | solution.py:141
  523.5 5.3 collective-permute-done.63
  530.5 3.0 convert_add_fusion
  536.5 9.3 %collective-permute-done.42 = bf16[2,64,1920]{2,1,0:T(8,128)(2,1)S(1)} collective-permute-done((bf16[2,64,1920]{2,1,0:T(8,128)(2,1)S(1)}, bf16[2,64,1920]{2,1,0:T(8,128)(2,1)S(1)}, u32[]{:S(2)}, u32[]{:S(2)}) %collective-permute-start.42) | collective-permute-done | bytes 491552 | tf_op jit(solution)/shard_map/ppermute | solution.py:89
  550.8 13.0 %collective-permute-done.45 = bf16[4,64,1920]{2,1,0:T(8,128)(2,1)S(1)} collective-permute-done((bf16[4,64,1920]{2,1,0:T(8,128)(2,1)S(1)}, bf16[4,64,1920]{2,1,0:T(8,128)(2,1)S(1)}, u32[]{:S(2)}, u32[]{:S(2)}) %collective-permute-start.45) | collective-permute-done | bytes 983072 | tf_op jit(solution)/shard_map/ppermute | solution.py:89
  571.2 4.1 collective-permute-done.48
  575.9 3.1 bitcast_convert_fusion.2
  579.0 4.9 collective-permute-done.47
  587.4 17.9 %collective-permute-done.68 = bf16[512,1280]{1,0:T(8,128)(2,1)S(1)} collective-permute-done((bf16[512,1280]{1,0:T(8,128)(2,1)}, bf16[512,1280]{1,0:T(8,128)(2,1)S(1)}, u32[]{:S(2)}, u32[]{:S(2)}) %collective-permute-start.68) | collective-permute-done | bytes 1310752 | tf_op jit(solution)/shard_map/ppermute | solution.py:89
  606.8 9.2 %collective-permute-done.70 = bf16[256,1280]{1,0:T(8,128)(2,1)S(1)} collective-permute-done((bf16[256,1280]{1,0:T(8,128)(2,1)S(1)}, bf16[256,1280]{1,0:T(8,128)(2,1)S(1)}, u32[]{:S(2)}, u32[]{:S(2)}) %collective-permute-start.70) | collective-permute-done | bytes 655392 | tf_op jit(solution)/shard_map/ppermute | solution.py:83
  621.7 3.4 collective-permute-done.52
  626.2 5.9 bitcast_convert_fusion
  635.1 4.6 broadcast_in_dim.324
  645.1 16.3 %column_merge.1 = f32[512,10240]{1,0:T(8,128)} custom-call(bf16[8,512,1280]{2,1,0:T(8,128)(2,1)} %bitcast.163.part_ref), custom_call_target="tpu_custom_call" | custom-call | tf_op jit(solution)/shard_map/column_merge/pallas_call | solution.py:201
  (508 shorter events, 220.9 us)
Async XLA Ops:
  7.2 221.9 %all-gather.3.cloned.1.call-start = ((), (), s32[]{:S(2)}) async-start(), calls=%async_computation.2 | async-start | bytes 6553600 | tf_op jit(solution)/shard_map/all_gather | solution.py:257
  8.3 72.1 %collective-permute-start.3 = (bf16[64,1920]{1,0:T(8,128)(2,1)S(1)}, bf16[64,1920]{1,0:T(8,128)(2,1)S(1)}, u32[]{:S(2)}, u32[]{:S(2)}) collective-permute-start(bf16[64,1920]{1,0:T(8,128)(2,1)S(1)} %get-tuple-element.26), channel_id=1, source_target_pairs={{0,4},{4,8},{8,12},{12,0},{1,5},{5,9},{9,13},{13,1},{2,6},{6,10},{... | collective-permute-start | bytes 737288 | tf_op jit(solution)/shard_map/ppermute | solution.py:132
  11.4 70.6 %collective-permute-start.4 = (bf16[64,1920]{1,0:T(8,128)(2,1)S(1)}, bf16[64,1920]{1,0:T(8,128)(2,1)S(1)}, u32[]{:S(2)}, u32[]{:S(2)}) collective-permute-start(bf16[64,1920]{1,0:T(8,128)(2,1)S(1)} %get-tuple-element.26), channel_id=1, source_target_pairs={{0,8},{4,12},{8,0},{12,4},{1,9},{5,13},{9,1},{13,5},{2,10},{6,14},... | collective-permute-start | bytes 737288 | tf_op jit(solution)/shard_map/ppermute | solution.py:132
  14.0 68.0 %collective-permute-start.5 = (bf16[64,1920]{1,0:T(8,128)(2,1)S(1)}, bf16[64,1920]{1,0:T(8,128)(2,1)S(1)}, u32[]{:S(2)}, u32[]{:S(2)}) collective-permute-start(bf16[64,1920]{1,0:T(8,128)(2,1)S(1)} %get-tuple-element.26), channel_id=1, source_target_pairs={{0,12},{4,0},{8,4},{12,8},{1,13},{5,1},{9,5},{13,9},{2,14},{6,2},{... | collective-permute-start | bytes 737288 | tf_op jit(solution)/shard_map/ppermute | solution.py:132
  17.0 17.4 %collective-permute-start.12 = (bf16[40,2048]{1,0:T(8,128)(2,1)}, bf16[40,2048]{1,0:T(8,128)(2,1)S(1)}, u32[]{:S(2)}, u32[]{:S(2)}) collective-permute-start(bf16[40,2048]{1,0:T(8,128)(2,1)} %get-tuple-element.22), channel_id=1, source_target_pairs={{0,4},{4,8},{8,12},{12,0},{1,5},{5,9},{9,13},{13,1},{2,6},{6,10},{... | collective-permute-start | bytes 491528 | tf_op jit(solution)/shard_map/ppermute | solution.py:132
  17.7 54.0 %collective-permute-start.13 = (bf16[40,2048]{1,0:T(8,128)(2,1)}, bf16[40,2048]{1,0:T(8,128)(2,1)S(1)}, u32[]{:S(2)}, u32[]{:S(2)}) collective-permute-start(bf16[40,2048]{1,0:T(8,128)(2,1)} %get-tuple-element.22), channel_id=1, source_target_pairs={{0,8},{4,12},{8,0},{12,4},{1,9},{5,13},{9,1},{13,5},{2,10},{6,14},... | collective-permute-start | bytes 491528 | tf_op jit(solution)/shard_map/ppermute | solution.py:132
  23.3 255.0 %all-gather.5.cloned.1.call-start = ((), (), s32[]{:S(2)}) async-start(), calls=%async_computation.3 | async-start | bytes 3276800 | tf_op jit(solution)/shard_map/all_gather | solution.py:259
  34.4 44.4 %collective-permute-start.14 = (bf16[40,2048]{1,0:T(8,128)(2,1)}, bf16[40,2048]{1,0:T(8,128)(2,1)S(1)}, u32[]{:S(2)}, u32[]{:S(2)}) collective-permute-start(bf16[40,2048]{1,0:T(8,128)(2,1)} %get-tuple-element.22), channel_id=1, source_target_pairs={{0,12},{4,0},{8,4},{12,8},{1,13},{5,1},{9,5},{13,9},{2,14},{6,2},{... | collective-permute-start | bytes 491528 | tf_op jit(solution)/shard_map/ppermute | solution.py:132
  71.7 65.5 %collective-permute-start = (bf16[1056]{0:T(1024)(128)(2,1)}, bf16[1056]{0:T(1024)(128)(2,1)}, u32[]{:S(2)}, u32[]{:S(2)}) collective-permute-start(bf16[1056]{0:T(1024)(128)(2,1)} %concatenate.102), channel_id=1, source_target_pairs={{0,4},{4,8},{8,12},{12,0},{1,5},{5,9},{9,13},{13,1},{2,6},{6,10},{... | collective-permute-start | bytes 6344 | tf_op jit(solution)/shard_map/ppermute | solution.py:132
  78.8 23.0 %collective-permute-start.15 = (bf16[4,40,2048]{2,1,0:T(8,128)(2,1)S(1)}, bf16[4,40,2048]{2,1,0:T(8,128)(2,1)S(1)}, u32[]{:S(2)}, u32[]{:S(2)}) collective-permute-start(bf16[4,40,2048]{2,1,0:T(8,128)(2,1)S(1)} %bitcast_dynamic-update-slice_fusion.43), channel_id=1, source_target_pairs={{0,2},{1,3},{2,0},{3,1},{4,6},{5,7},{6,4},{7,5},{8,10},{9,11},{10,... | collective-permute-start | bytes 1966088 | tf_op jit(solution)/shard_map/ppermute | solution.py:83
  80.4 17.7 %collective-permute-start.16 = (bf16[4,40,2048]{2,1,0:T(8,128)(2,1)S(1)}, bf16[4,40,2048]{2,1,0:T(8,128)(2,1)S(1)}, u32[]{:S(2)}, u32[]{:S(2)}) collective-permute-start(bf16[4,40,2048]{2,1,0:T(8,128)(2,1)S(1)} %bitcast_dynamic-update-slice_fusion.43), channel_id=1, source_target_pairs={{0,16},{16,0},{1,17},{17,1},{2,18},{18,2},{3,19},{19,3},{4,20},{20... | collective-permute-start | bytes 1966088 | tf_op jit(solution)/shard_map/ppermute | solution.py:89
  82.0 35.6 %collective-permute-start.6 = (bf16[4,64,1920]{2,1,0:T(8,128)(2,1)S(1)}, bf16[4,64,1920]{2,1,0:T(8,128)(2,1)S(1)}, u32[]{:S(2)}, u32[]{:S(2)}) collective-permute-start(bf16[4,64,1920]{2,1,0:T(8,128)(2,1)S(1)} %bitcast_dynamic-update-slice_fusion.36), channel_id=1, source_target_pairs={{0,2},{1,3},{2,0},{3,1},{4,6},{5,7},{6,4},{7,5},{8,10},{9,11},{10,... | collective-permute-start | bytes 2949128 | tf_op jit(solution)/shard_map/ppermute | solution.py:83
  82.6 33.2 %collective-permute-start.7 = (bf16[4,64,1920]{2,1,0:T(8,128)(2,1)S(1)}, bf16[4,64,1920]{2,1,0:T(8,128)(2,1)S(1)}, u32[]{:S(2)}, u32[]{:S(2)}) collective-permute-start(bf16[4,64,1920]{2,1,0:T(8,128)(2,1)S(1)} %bitcast_dynamic-update-slice_fusion.36), channel_id=1, source_target_pairs={{0,16},{16,0},{1,17},{17,1},{2,18},{18,2},{3,19},{19,3},{4,20},{20... | collective-permute-start | bytes 2949128 | tf_op jit(solution)/shard_map/ppermute | solution.py:89
  98.1 40.7 %collective-permute-start.1 = (bf16[1056]{0:T(1024)(128)(2,1)}, bf16[1056]{0:T(1024)(128)(2,1)S(1)}, u32[]{:S(2)}, u32[]{:S(2)}) collective-permute-start(bf16[1056]{0:T(1024)(128)(2,1)} %concatenate.102), channel_id=1, source_target_pairs={{0,8},{4,12},{8,0},{12,4},{1,9},{5,13},{9,1},{13,5},{2,10},{6,14},... | collective-permute-start | bytes 6344 | tf_op jit(solution)/shard_map/ppermute | solution.py:132
  101.8 30.2 %collective-permute-start.18 = (bf16[2,40,2048]{2,1,0:T(8,128)(2,1)S(1)}, bf16[2,40,2048]{2,1,0:T(8,128)(2,1)S(1)}, u32[]{:S(2)}, u32[]{:S(2)}) collective-permute-start(bf16[2,40,2048]{2,1,0:T(8,128)(2,1)S(1)} %slice.374), channel_id=1, source_target_pairs={{0,2},{1,3},{2,0},{3,1},{4,6},{5,7},{6,4},{7,5},{8,10},{9,11},{10,... | collective-permute-start | bytes 983048 | tf_op jit(solution)/shard_map/ppermute | solution.py:83
  131.1 34.6 %collective-permute-start.10 = (bf16[4,4,64,1920]{3,2,1,0:T(8,128)(2,1)}, bf16[4,4,64,1920]{3,2,1,0:T(8,128)(2,1)}, u32[]{:S(2)}, u32[]{:S(2)}) collective-permute-start(bf16[4,4,64,1920]{3,2,1,0:T(8,128)(2,1)} %fusion.42), channel_id=1, source_target_pairs={{0,1},{1,0},{2,3},{3,2},{4,5},{5,4},{6,7},{7,6},{8,9},{9,8},{10,11... | collective-permute-start | bytes 11796488 | tf_op jit(solution)/shard_map/ppermute | solution.py:86
  136.0 27.5 %collective-permute-start.19 = (bf16[4,4,40,2048]{3,2,1,0:T(8,128)(2,1)}, bf16[4,4,40,2048]{3,2,1,0:T(8,128)(2,1)}, u32[]{:S(2)}, u32[]{:S(2)}) collective-permute-start(bf16[4,4,40,2048]{3,2,1,0:T(8,128)(2,1)} %fusion.47), channel_id=1, source_target_pairs={{0,1},{1,0},{2,3},{3,2},{4,5},{5,4},{6,7},{7,6},{8,9},{9,8},{10,11... | collective-permute-start | bytes 7864328 | tf_op jit(solution)/shard_map/ppermute | solution.py:86
  137.2 16.7 %collective-permute-start.30 = (bf16[128,2048]{1,0:T(8,128)(2,1)S(1)}, bf16[128,2048]{1,0:T(8,128)(2,1)S(1)}, u32[]{:S(2)}, u32[]{:S(2)}) collective-permute-start(bf16[128,2048]{1,0:T(8,128)(2,1)S(1)} %copy-done.31), channel_id=1, source_target_pairs={{0,2},{1,3},{2,0},{3,1},{4,6},{5,7},{6,4},{7,5},{8,10},{9,11},{10,... | collective-permute-start | bytes 1572872 | tf_op jit(solution)/shard_map/ppermute | solution.py:83
  153.3 41.4 %collective-permute-start.33 = (bf16[64,2048]{1,0:T(8,128)(2,1)}, bf16[64,2048]{1,0:T(8,128)(2,1)}, u32[]{:S(2)}, u32[]{:S(2)}) collective-permute-start(bf16[64,2048]{1,0:T(8,128)(2,1)} %slice.383), channel_id=1, source_target_pairs={{0,2},{1,3},{2,0},{3,1},{4,6},{5,7},{6,4},{7,5},{8,10},{9,11},{10,... | collective-permute-start | bytes 786440 | tf_op jit(solution)/shard_map/ppermute | solution.py:83
  154.6 40.1 %collective-permute-start.32 = (bf16[64,2048]{1,0:T(8,128)(2,1)}, bf16[64,2048]{1,0:T(8,128)(2,1)}, u32[]{:S(2)}, u32[]{:S(2)}) collective-permute-start(bf16[64,2048]{1,0:T(8,128)(2,1)} %slice.382), channel_id=1, source_target_pairs={{0,16},{16,0},{1,17},{17,1},{2,18},{18,2},{3,19},{19,3},{4,20},{20... | collective-permute-start | bytes 786440 | tf_op jit(solution)/shard_map/ppermute | solution.py:89
  196.6 27.7 %collective-permute-start.34 = (bf16[4,128,2048]{2,1,0:T(8,128)(2,1)}, bf16[4,128,2048]{2,1,0:T(8,128)(2,1)}, u32[]{:S(2)}, u32[]{:S(2)}) collective-permute-start(bf16[4,128,2048]{2,1,0:T(8,128)(2,1)} %fusion.67), channel_id=1, source_target_pairs={{0,1},{1,0},{2,3},{3,2},{4,5},{5,4},{6,7},{7,6},{8,9},{9,8},{10,11... | collective-permute-start | bytes 6291464 | tf_op jit(solution)/shard_map/ppermute | solution.py:86
  213.0 251.9 %reduce-scatter.5.cloned.1.call-start = ((), (), s32[]{:S(2)}) async-start(), calls=%async_computation.5 | async-start | bytes 3276800 | tf_op jit(solution)/shard_map/reduce_scatter | solution.py:317
  296.2 273.9 %reduce-scatter.3.cloned.1.call-start = ((), (), s32[]{:S(2)}) async-start(), calls=%async_computation.4 | async-start | bytes 6553600 | tf_op jit(solution)/shard_map/reduce_scatter | solution.py:319
  309.7 21.3 %collective-permute-start.35 = (bf16[2,2,128,2048]{3,2,1,0:T(8,128)(2,1)}, bf16[2,2,128,2048]{3,2,1,0:T(8,128)(2,1)}, u32[]{:S(2)}, u32[]{:S(2)}) collective-permute-start(bf16[2,2,128,2048]{3,2,1,0:T(8,128)(2,1)} %dynamic-slice_bitcast_fusion), channel_id=1, source_target_pairs={{0,1},{1,0},{2,3},{3,2},{4,5},{5,4},{6,7},{7,6},{8,9},{9,8},{10,11... | collective-permute-start | bytes 6291464 | tf_op jit(solution)/shard_map/ppermute | solution.py:86
  319.9 17.3 %collective-permute-start.25 = (bf16[2,2,128,2048]{3,2,1,0:T(8,128)(2,1)}, bf16[2,2,128,2048]{3,2,1,0:T(8,128)(2,1)}, u32[]{:S(2)}, u32[]{:S(2)}) collective-permute-start(bf16[2,2,128,2048]{3,2,1,0:T(8,128)(2,1)} %dynamic-slice_bitcast_fusion.1), channel_id=1, source_target_pairs={{0,1},{1,0},{2,3},{3,2},{4,5},{5,4},{6,7},{7,6},{8,9},{9,8},{10,11... | collective-permute-start | bytes 6291464 | tf_op jit(solution)/shard_map/ppermute | solution.py:86
  345.9 15.9 %collective-permute-start.37 = (bf16[128,2048]{1,0:T(8,128)(2,1)S(1)}, bf16[128,2048]{1,0:T(8,128)(2,1)S(1)}, u32[]{:S(2)}, u32[]{:S(2)}) collective-permute-start(bf16[128,2048]{1,0:T(8,128)(2,1)S(1)} %pad_maximum_fusion.10), channel_id=1, source_target_pairs={{0,2},{1,3},{2,0},{3,1},{4,6},{5,7},{6,4},{7,5},{8,10},{9,11},{10,... | collective-permute-start | bytes 1572872 | tf_op jit(solution)/shard_map/ppermute | solution.py:83
  350.7 20.5 %collective-permute-start.29 = (bf16[128,2048]{1,0:T(8,128)(2,1)S(1)}, bf16[128,2048]{1,0:T(8,128)(2,1)S(1)}, u32[]{:S(2)}, u32[]{:S(2)}) collective-permute-start(bf16[128,2048]{1,0:T(8,128)(2,1)S(1)} %pad_maximum_fusion.9), channel_id=1, source_target_pairs={{0,16},{16,0},{1,17},{17,1},{2,18},{18,2},{3,19},{19,3},{4,20},{20... | collective-permute-start | bytes 1572872 | tf_op jit(solution)/shard_map/ppermute | solution.py:89
  351.5 20.7 %collective-permute-start.27 = (bf16[128,2048]{1,0:T(8,128)(2,1)S(1)}, bf16[128,2048]{1,0:T(8,128)(2,1)S(1)}, u32[]{:S(2)}, u32[]{:S(2)}) collective-permute-start(bf16[128,2048]{1,0:T(8,128)(2,1)S(1)} %pad_maximum_fusion.8), channel_id=1, source_target_pairs={{0,2},{1,3},{2,0},{3,1},{4,6},{5,7},{6,4},{7,5},{8,10},{9,11},{10,... | collective-permute-start | bytes 1572872 | tf_op jit(solution)/shard_map/ppermute | solution.py:83
  402.2 65.1 %collective-permute-start.54 = (bf16[4,2,2,40,2048]{4,3,0,2,1:T(8,128)(2,1)}, bf16[4,2,2,40,2048]{4,3,0,2,1:T(8,128)(2,1)}, u32[]{:S(2)}, u32[]{:S(2)}) collective-permute-start(bf16[4,2,2,40,2048]{4,3,0,2,1:T(8,128)(2,1)} %bitcast.489), channel_id=1, source_target_pairs={{0,1},{1,0},{2,3},{3,2},{4,5},{5,4},{6,7},{7,6},{8,9},{9,8},{10,11... | collective-permute-start | bytes 7864328 | tf_op jit(solution)/shard_map/ppermute | solution.py:86
  416.2 114.3 %collective-permute-start.41 = (bf16[4,2,2,64,1920]{4,3,0,2,1:T(8,128)(2,1)}, bf16[4,2,2,64,1920]{4,3,0,2,1:T(8,128)(2,1)}, u32[]{:S(2)}, u32[]{:S(2)}) collective-permute-start(bf16[4,2,2,64,1920]{4,3,0,2,1:T(8,128)(2,1)} %bitcast.488), channel_id=1, source_target_pairs={{0,1},{1,0},{2,3},{3,2},{4,5},{5,4},{6,7},{7,6},{8,9},{9,8},{10,11... | collective-permute-start | bytes 11796488 | tf_op jit(solution)/shard_map/ppermute | solution.py:86
  465.0 28.1 %collective-permute-start.72 = (bf16[160,2048]{1,0:T(8,128)(2,1)}, bf16[160,2048]{1,0:T(8,128)(2,1)S(1)}, u32[]{:S(2)}, u32[]{:S(2)}) collective-permute-start(bf16[160,2048]{1,0:T(8,128)(2,1)} %reduce-scatter.5.cloned.1.call-done), channel_id=1, source_target_pairs={{0,2},{1,3},{2,0},{3,1},{4,6},{5,7},{6,4},{7,5},{8,10},{9,11},{10,... | collective-permute-start | bytes 1966088 | tf_op jit(solution)/shard_map/ppermute | solution.py:83
  467.2 24.0 %collective-permute-start.73 = (bf16[160,2048]{1,0:T(8,128)(2,1)}, bf16[160,2048]{1,0:T(8,128)(2,1)S(1)}, u32[]{:S(2)}, u32[]{:S(2)}) collective-permute-start(bf16[160,2048]{1,0:T(8,128)(2,1)} %reduce-scatter.5.cloned.1.call-done), channel_id=1, source_target_pairs={{0,16},{16,0},{1,17},{17,1},{2,18},{18,2},{3,19},{19,3},{4,20},{20... | collective-permute-start | bytes 1966088 | tf_op jit(solution)/shard_map/ppermute | solution.py:89
  471.0 17.7 %collective-permute-start.55 = (bf16[2,40,2048]{2,1,0:T(8,128)(2,1)S(1)}, bf16[2,40,2048]{2,1,0:T(8,128)(2,1)S(1)}, u32[]{:S(2)}, u32[]{:S(2)}) collective-permute-start(bf16[2,40,2048]{2,1,0:T(8,128)(2,1)S(1)} %get-tuple-element.66), channel_id=1, source_target_pairs={{0,16},{16,0},{1,17},{17,1},{2,18},{18,2},{3,19},{19,3},{4,20},{20... | collective-permute-start | bytes 983048 | tf_op jit(solution)/shard_map/ppermute | solution.py:89
  489.0 17.7 %collective-permute-start.58 = (bf16[4,40,2048]{2,1,0:T(8,128)(2,1)S(1)}, bf16[4,40,2048]{2,1,0:T(8,128)(2,1)S(1)}, u32[]{:S(2)}, u32[]{:S(2)}) collective-permute-start(bf16[4,40,2048]{2,1,0:T(8,128)(2,1)S(1)} %pad_maximum_fusion.7), channel_id=1, source_target_pairs={{0,16},{16,0},{1,17},{17,1},{2,18},{18,2},{3,19},{19,3},{4,20},{20... | collective-permute-start | bytes 1966088 | tf_op jit(solution)/shard_map/ppermute | solution.py:89
  490.9 17.7 %collective-permute-start.56 = (bf16[4,40,2048]{2,1,0:T(8,128)(2,1)S(1)}, bf16[4,40,2048]{2,1,0:T(8,128)(2,1)S(1)}, u32[]{:S(2)}, u32[]{:S(2)}) collective-permute-start(bf16[4,40,2048]{2,1,0:T(8,128)(2,1)S(1)} %pad_maximum_fusion.6), channel_id=1, source_target_pairs={{0,2},{1,3},{2,0},{3,1},{4,6},{5,7},{6,4},{7,5},{8,10},{9,11},{10,... | collective-permute-start | bytes 1966088 | tf_op jit(solution)/shard_map/ppermute | solution.py:83
  491.2 21.5 %collective-permute-start.75 = (bf16[80,2048]{1,0:T(8,128)(2,1)S(1)}, bf16[80,2048]{1,0:T(8,128)(2,1)S(1)}, u32[]{:S(2)}, u32[]{:S(2)}) collective-permute-start(bf16[80,2048]{1,0:T(8,128)(2,1)S(1)} %slice.405), channel_id=1, source_target_pairs={{0,2},{1,3},{2,0},{3,1},{4,6},{5,7},{6,4},{7,5},{8,10},{9,11},{10,... | collective-permute-start | bytes 983048 | tf_op jit(solution)/shard_map/ppermute | solution.py:83
  493.1 19.9 %collective-permute-start.74 = (bf16[80,2048]{1,0:T(8,128)(2,1)S(1)}, bf16[80,2048]{1,0:T(8,128)(2,1)S(1)}, u32[]{:S(2)}, u32[]{:S(2)}) collective-permute-start(bf16[80,2048]{1,0:T(8,128)(2,1)S(1)} %slice.404), channel_id=1, source_target_pairs={{0,16},{16,0},{1,17},{17,1},{2,18},{18,2},{3,19},{19,3},{4,20},{20... | collective-permute-start | bytes 983048 | tf_op jit(solution)/shard_map/ppermute | solution.py:89
  513.0 104.2 %collective-permute-start.76 = (bf16[4,160,2048]{2,1,0:T(8,128)(2,1)S(1)}, bf16[4,160,2048]{2,1,0:T(8,128)(2,1)}, u32[]{:S(2)}, u32[]{:S(2)}) collective-permute-start(bf16[4,160,2048]{2,1,0:T(8,128)(2,1)S(1)} %fusion.48), channel_id=1, source_target_pairs={{0,1},{1,0},{2,3},{3,2},{4,5},{5,4},{6,7},{7,6},{8,9},{9,8},{10,11... | collective-permute-start | bytes 7864328 | tf_op jit(solution)/shard_map/ppermute | solution.py:86
  528.8 20.4 %collective-permute-start.65 = (bf16[20,2048]{1,0:T(8,128)(2,1)S(1)}, bf16[20,2048]{1,0:T(8,128)(2,1)S(1)}, u32[]{:S(2)}, u32[]{:S(2)}) collective-permute-start(bf16[20,2048]{1,0:T(8,128)(2,1)S(1)} %slice.401), channel_id=1, source_target_pairs={{0,2},{1,3},{2,0},{3,1},{4,6},{5,7},{6,4},{7,5},{8,10},{9,11},{10,... | collective-permute-start | bytes 245768 | tf_op jit(solution)/shard_map/ppermute | solution.py:83
  530.2 19.1 %collective-permute-start.64 = (bf16[20,2048]{1,0:T(8,128)(2,1)S(1)}, bf16[20,2048]{1,0:T(8,128)(2,1)S(1)}, u32[]{:S(2)}, u32[]{:S(2)}) collective-permute-start(bf16[20,2048]{1,0:T(8,128)(2,1)S(1)} %slice.400), channel_id=1, source_target_pairs={{0,16},{16,0},{1,17},{17,1},{2,18},{18,2},{3,19},{19,3},{4,20},{20... | collective-permute-start | bytes 245768 | tf_op jit(solution)/shard_map/ppermute | solution.py:89
  548.9 16.6 %collective-permute-start.43 = (bf16[4,64,1920]{2,1,0:T(8,128)(2,1)S(1)}, bf16[4,64,1920]{2,1,0:T(8,128)(2,1)S(1)}, u32[]{:S(2)}, u32[]{:S(2)}) collective-permute-start(bf16[4,64,1920]{2,1,0:T(8,128)(2,1)S(1)} %pad_maximum_fusion.3), channel_id=1, source_target_pairs={{0,2},{1,3},{2,0},{3,1},{4,6},{5,7},{6,4},{7,5},{8,10},{9,11},{10,... | collective-permute-start | bytes 2949128 | tf_op jit(solution)/shard_map/ppermute | solution.py:83
  549.3 17.9 %collective-permute-start.66 = (bf16[4,40,2048]{2,1,0:T(8,128)(2,1)S(1)}, bf16[4,40,2048]{2,1,0:T(8,128)(2,1)S(1)}, u32[]{:S(2)}, u32[]{:S(2)}) collective-permute-start(bf16[4,40,2048]{2,1,0:T(8,128)(2,1)S(1)} %fusion.101), channel_id=1, source_target_pairs={{0,1},{1,0},{2,3},{3,2},{4,5},{5,4},{6,7},{7,6},{8,9},{9,8},{10,11... | collective-permute-start | bytes 1966088 | tf_op jit(solution)/shard_map/ppermute | solution.py:86
  568.1 15.8 %collective-permute-start.47 = (bf16[64,1920]{1,0:T(8,128)(2,1)S(1)}, bf16[64,1920]{1,0:T(8,128)(2,1)}, u32[]{:S(2)}, u32[]{:S(2)}) collective-permute-start(bf16[64,1920]{1,0:T(8,128)(2,1)S(1)} %get-tuple-element.54), channel_id=1, source_target_pairs={{0,8},{4,12},{8,0},{12,4},{1,9},{5,13},{9,1},{13,5},{2,10},{6,14},... | collective-permute-start | bytes 737288 | tf_op jit(solution)/shard_map/ppermute | solution.py:141
  570.1 36.2 %collective-permute-start.67 = (bf16[512,1280]{1,0:T(8,128)(2,1)}, bf16[512,1280]{1,0:T(8,128)(2,1)S(1)}, u32[]{:S(2)}, u32[]{:S(2)}) collective-permute-start(bf16[512,1280]{1,0:T(8,128)(2,1)} %reduce-scatter.3.cloned.1.call-done), channel_id=1, source_target_pairs={{0,2},{1,3},{2,0},{3,1},{4,6},{5,7},{6,4},{7,5},{8,10},{9,11},{10,... | collective-permute-start | bytes 3932168 | tf_op jit(solution)/shard_map/ppermute | solution.py:83
  575.3 30.1 %collective-permute-start.68 = (bf16[512,1280]{1,0:T(8,128)(2,1)}, bf16[512,1280]{1,0:T(8,128)(2,1)S(1)}, u32[]{:S(2)}, u32[]{:S(2)}) collective-permute-start(bf16[512,1280]{1,0:T(8,128)(2,1)} %reduce-scatter.3.cloned.1.call-done), channel_id=1, source_target_pairs={{0,16},{16,0},{1,17},{17,1},{2,18},{18,2},{3,19},{19,3},{4,20},{20... | collective-permute-start | bytes 3932168 | tf_op jit(solution)/shard_map/ppermute | solution.py:89
  585.5 35.1 %collective-permute-start.49 = (bf16[64,1920]{1,0:T(8,128)(2,1)S(1)}, bf16[64,1920]{1,0:T(8,128)(2,1)S(1)}, u32[]{:S(2)}, u32[]{:S(2)}) collective-permute-start(bf16[64,1920]{1,0:T(8,128)(2,1)S(1)} %get-tuple-element.17), channel_id=1, source_target_pairs={{0,2},{1,3},{2,0},{3,1},{4,6},{5,7},{6,4},{7,5},{8,10},{9,11},{10,... | collective-permute-start | bytes 737288 | tf_op jit(solution)/shard_map/ppermute | solution.py:83
  586.2 33.1 %collective-permute-start.50 = (bf16[64,1920]{1,0:T(8,128)(2,1)S(1)}, bf16[64,1920]{1,0:T(8,128)(2,1)S(1)}, u32[]{:S(2)}, u32[]{:S(2)}) collective-permute-start(bf16[64,1920]{1,0:T(8,128)(2,1)S(1)} %get-tuple-element.17), channel_id=1, source_target_pairs={{0,16},{16,0},{1,17},{17,1},{2,18},{18,2},{3,19},{19,3},{4,20},{20... | collective-permute-start | bytes 737288 | tf_op jit(solution)/shard_map/ppermute | solution.py:89
  617.1 25.4 %collective-permute-start.71 = (bf16[4,512,1280]{2,1,0:T(8,128)(2,1)S(1)}, bf16[4,512,1280]{2,1,0:T(8,128)(2,1)S(1)}, u32[]{:S(2)}, u32[]{:S(2)}) collective-permute-start(bf16[4,512,1280]{2,1,0:T(8,128)(2,1)S(1)} %fusion.13), channel_id=1, source_target_pairs={{0,1},{1,0},{2,3},{3,2},{4,5},{5,4},{6,7},{7,6},{8,9},{9,8},{10,11... | collective-permute-start | bytes 15728648 | tf_op jit(solution)/shard_map/ppermute | solution.py:86
  (105 other events, 872.7 us)
Sparse Core Ops, SparseCore 0:
  23.4 110.9 all-gather.2
  213.2 65.0 all-gather.4
  296.3 50.8 reduce-scatter.4
  349.4 93.8 reduce-scatter.2

commit v2 on v1

--- a/solution.py
+++ b/solution.py
@@ -125,6 +125,73 @@
         in_x, in_y = self.over_x(near_x.astype(BF)), self.over_y(near_y.astype(BF))
         return mine + in_x.astype(F32) + in_y.astype(F32)
 
+    def gather_near(self, v):
+        half = v.shape[0] // 2
+        from_x, from_y = self.over_x(v), self.over_y(v)
+        far_a = self.over_y(from_x[:half])
+        far_b = self.over_x(from_y[half:])
+        near = jnp.concatenate([v, from_x, from_y, far_a, far_b], axis=0)
+        return near, self.over_core(near)
+
+    def gather_rows(self, v):
+        if not self.cube:
+            return lax.all_gather(v, PLANE, axis=0, tiled=True)
+        return jnp.concatenate(self.gather_near(v), axis=0)
+
+    def scatter_rows(self, v):
+        if not self.cube:
+            return lax.psum_scatter(v.astype(BF), PLANE, scatter_dimension=0, tiled=True).astype(F32)
+        n = v.shape[0] // 8
+        got = self.over_core(v[4 * n :].astype(BF)).astype(F32)
+        part = lambda k: v[k * n : (k + 1) * n].astype(F32) + got[k * n : (k + 1) * n]
+        half = n // 2
+        far = part(3).astype(BF)
+        got_x, got_y = self.over_x(far[:half]), self.over_y(far[half:])
+        near_x, near_y = part(1), part(2)
+        near_y = jnp.concatenate([near_y[:half] + got_x.astype(F32), near_y[half:]], axis=0)
+        near_x = jnp.concatenate([near_x[:half], near_x[half:] + got_y.astype(F32)], axis=0)
+        in_x, in_y = self.over_x(near_x.astype(BF)), self.over_y(near_y.astype(BF))
+        return part(0) + in_x.astype(F32) + in_y.astype(F32)
+
+    def reorder(self, v):
+        if not self.cube:
+            return v
+        n = v.shape[0] // 8
+        tail = v.shape[1:]
+        v = v.reshape((2, 2, 2, n) + tail)
+        for axis, bit in ((0, self.y), (1, self.x), (2, self.core)):
+            v = jnp.where(bit == 1, jnp.flip(v, axis), v)
+        return v.reshape((8 * n,) + tail)
+
+    def to_ranks(self, v):
+        if not self.cube:
+            return v
+        n = v.shape[0] // 8
+        v = jnp.swapaxes(v.reshape((2, 4, n) + v.shape[1:]), 0, 1).reshape(v.shape)
+        return self.reorder(v)
+
+    def from_ranks(self, v):
+        if not self.cube:
+            return v
+        n = v.shape[0] // 8
+        v = self.reorder(v)
+        return jnp.swapaxes(v.reshape((4, 2, n) + v.shape[1:]), 0, 1).reshape(v.shape)
+
+    def exchange(self, v):
+        return lax.all_to_all(v, PLANE, split_axis=0, concat_axis=0, tiled=True)
+
+    def total(self, v):
+        if not self.cube:
+            return lax.psum(v, ("ctx", "fsdp", "rep"))
+        v = v + self.over_core(v)
+        v = v + self.over_x(v)
+        v = v + self.over_y(v)
+        z = self.z
+        parts = [lax.ppermute(v, "fsdp", [(i, (i + d) % z) for i in range(z)]) for d in range(1, z)]
+        for part in parts:
+            v = v + part
+        return v
+
     def layers_gather(self, v):
         z = self.z
         parts = [(v, self.layer)]
@@ -151,23 +218,26 @@
     return total
 
 
-def column_slices(matrix, rank, groups, width):
+def column_slices(matrix, rank, groups, splits):
     rows, columns = matrix.shape
+    width = sum(splits)
     span = columns // groups
     last = columns // LANES - 1
     block = min(128, rows)
-    window = -(-(LANES - 1 + width) // LANES)
-    if width % 32 == 0:
-        window = -(-(LANES - 32 + width) // LANES)
+    unit = math.gcd(math.gcd(width, span), LANES)
+    window = -(-(LANES - unit + width) // LANES)
 
     def body(rank_ref, *refs):
-        out = refs[-1]
+        outs = refs[groups * window :]
         for g in range(groups):
             parts = [refs[g * window + w][...].astype(F32) for w in range(window)]
-            wide = jnp.concatenate(parts, axis=1)
+            wide = parts[0] if window == 1 else jnp.concatenate(parts, axis=1)
             shift = (g * span + rank_ref[0] * width) % LANES
             wide = pltpu.roll(wide, (window * LANES - shift) % (window * LANES), 1)
-            out[:, g * width : (g + 1) * width] = wide[:, :width].astype(out.dtype)
+            at = 0
+            for out, size in zip(outs, splits):
+                out[:, g * size : (g + 1) * size] = wide[:, at : at + size].astype(out.dtype)
+                at += size
 
     def spec(g, w):
         def index(i, rank_ref):
@@ -177,35 +247,56 @@
 
     return pl.pallas_call(
         body,
-        out_shape=jax.ShapeDtypeStruct((rows, groups * width), matrix.dtype),
+        out_shape=[jax.ShapeDtypeStruct((rows, groups * size), matrix.dtype) for size in splits],
         grid_spec=pltpu.PrefetchScalarGridSpec(
             num_scalar_prefetch=1,
             grid=(rows // block,),
             in_specs=[spec(g, w) for g in range(groups) for w in range(window)],
-            out_specs=pl.BlockSpec((block, groups * width), lambda i, rank_ref: (i, 0)),
+            out_specs=[pl.BlockSpec((block, groups * size), lambda i, rank_ref: (i, 0)) for size in splits],
         ),
         name="column_slices",
     )(rank[None].astype(jnp.int32), *([matrix] * (groups * window)))
 
 
-def column_merge(parts, groups):
-    ranks, rows, columns = parts.shape
-    width = columns // groups
-    block = 32
-
-    def body(part_ref, out):
+def column_merge(parts, groups, rank, rows):
+    cube = isinstance(parts[0], tuple)
+    flat = [a for part in parts for a in (part if cube else (part,))]
+    sizes = [(part[0] if cube else part).shape[-1] // groups for part in parts]
+    ranks = flat[0].shape[0] * (2 if cube else 1)
+    span = ranks * sum(sizes)
+    block = math.gcd(rows, 32)
+
+    def body(rank_ref, *refs):
+        out = refs[-1]
+        core = rank_ref[0] % 2
+
+        def load(s, k, g):
+            cut = slice(g * sizes[s], (g + 1) * sizes[s])
+            if not cube:
+                return refs[s][k, :, cut].astype(F32)
+            near, other = refs[2 * s], refs[2 * s + 1]
+            index = lax.shift_right_logical(jnp.bitwise_xor(rank_ref[0], k), 1)
+            mine = core == k % 2
+            return jnp.where(mine, near[index, :, cut].astype(F32), other[index, :, cut].astype(F32))
+
         for g in range(groups):
-            pieces = [part_ref[k, :, g * width : (g + 1) * width].astype(F32) for k in range(ranks)]
-            out[:, g * ranks * width : (g + 1) * ranks * width] = jnp.concatenate(pieces, axis=1)
+            pieces = [load(s, k, g) for k in range(ranks) for s in range(len(sizes))]
+            out[:, g * span : (g + 1) * span] = jnp.concatenate(pieces, axis=1)
+
+    def spec(a):
+        return pl.BlockSpec((a.shape[0], block, a.shape[2]), lambda i, rank_ref: (0, i, 0))
 
     return pl.pallas_call(
         body,
-        out_shape=jax.ShapeDtypeStruct((rows, ranks * columns), F32),
-        grid=(rows // block,),
-        in_specs=[pl.BlockSpec((ranks, block, columns), lambda i: (0, i, 0))],
-        out_specs=pl.BlockSpec((block, ranks * columns), lambda i: (i, 0)),
+        out_shape=jax.ShapeDtypeStruct((rows, groups * span), F32),
+        grid_spec=pltpu.PrefetchScalarGridSpec(
+            num_scalar_prefetch=1,
+            grid=(rows // block,),
+            in_specs=[spec(a) for a in flat],
+            out_specs=pl.BlockSpec((block, groups * span), lambda i, rank_ref: (i, 0)),
+        ),
         name="column_merge",
-    )(parts)
+    )(rank[None].astype(jnp.int32), *flat)
 
 
 def shards(
@@ -245,27 +336,36 @@
         at += size
     gain_one, gain_two, query_scale, key_scale = gains
 
-    joint_rows = joint_matrix.shape[0] // members
+    rows = tokens[0].astype(F32)
+    tokens_all = plane.gather_rows(tokens[0])
+    joint_width = joint_columns // members
+    (joint_share,) = column_slices(joint_matrix, rank, 1, (joint_width,))
+    joint_part = plane.layers_gather(joint_share).reshape(model, joint_width)
     out_rows = out_weight.shape[0] // members
-    joint_share = plane.layers_gather(lax.dynamic_slice_in_dim(joint_matrix, rank * joint_rows, joint_rows, 0))
-    joint_full = plane.gather(joint_share, axis=1).reshape(model, joint_columns)
     out_share = plane.layers_gather(lax.dynamic_slice_in_dim(out_weight, rank * out_rows, out_rows, 0))
     out_full = plane.gather(out_share, axis=1).reshape(query_width, model)
 
     units = contract_weight.shape[0] // members
-    expand_share = column_slices(expand_weight, rank, 2 * layers, units)
-    expand_part = lax.all_gather(expand_share, "fsdp", axis=0, tiled=True)
-    contract_share = lax.dynamic_slice_in_dim(contract_weight, rank * units, units, 0)
-    contract_part = lax.all_gather(contract_share, "fsdp", axis=0, tiled=True)
-    width = units * layers
+    splits = (units * 3 // 5, units - units * 3 // 5)
+    groups = 2 * layers
+    expand_shares = column_slices(expand_weight, rank, groups, splits)
+    parts, at = [], rank * units
+    for share, size in zip(expand_shares, splits):
+        contract_share = lax.dynamic_slice_in_dim(contract_weight, at, size, 0)
+        at = at + size
+        sent = jnp.concatenate([share, contract_share.reshape(-1, groups * size)], axis=0)
+        got = lax.all_gather(sent, "fsdp", axis=0, tiled=False)
+        rows_in = share.shape[0]
+        parts.append((got[:, :rows_in].reshape(model, groups * size), got[:, rows_in:].reshape(size * layers, model)))
 
     upstream = cotangent[0].astype(F32) * valid
-    upstream_all = plane.gather(upstream.astype(BF)).reshape(members * rows_here, model)
-
-    rows = tokens[0].astype(F32)
+    upstream_all = plane.gather_rows(upstream.astype(BF))
+
+    entry_one_all = (rms_parts(tokens_all.astype(F32))[0] * gain_one).astype(BF)
     normed_one, inverse_one = rms_parts(rows)
-    entry_one = (normed_one * gain_one).astype(BF)
-    joint_projection = dot(entry_one, joint_full, ((1,), (0,)))
+    joint_columns_all = plane.to_ranks(dot(entry_one_all, joint_part, ((1,), (0,)), BF))
+    joint_projection = plane.exchange(joint_columns_all).reshape(members, rows_here, joint_width)
+    joint_projection = jnp.swapaxes(joint_projection, 0, 1).reshape(rows_here, joint_columns).astype(F32)
     query_raw = joint_projection[:, :query_width].reshape(rows_here, QUERY_HEADS, HEAD_SIZE)
     key_raw = joint_projection[:, query_width : query_width + key_width].reshape(
         rows_here, KEY_VALUE_HEADS, HEAD_SIZE
@@ -301,24 +401,28 @@
 
     normed_two, inverse_two = rms_parts(hidden)
     entry_two = (normed_two * gain_two).astype(BF)
-    entry_all = plane.gather(entry_two).reshape(members * rows_here, model)
-    expanded = dot(entry_all, expand_part, ((1,), (0,)))
-    gate, upward = expanded[:, :width], expanded[:, width:]
-    sigma = jax.nn.sigmoid(gate)
-    activated = gate * sigma
-    product = (activated * upward).astype(BF)
-    back_product = against(upstream_all, contract_part)
-    grad_gate = back_product * upward * sigma * (1.0 + gate * (1.0 - sigma))
-    grad_upward = back_product * activated
-    grad_expanded = jnp.concatenate([grad_gate, grad_upward], axis=1).astype(BF)
-    back_entry_share = against(grad_expanded, expand_part, BF)
-    back_entry_two = plane.scatter(back_entry_share.reshape(members, rows_here, model))
-    contract_grad = cross_product(product, upstream_all, BF)
-    contract_owned = lax.psum_scatter(contract_grad, "fsdp", scatter_dimension=0, tiled=True)
-    expand_grad = cross_product(entry_all, grad_expanded, BF)
-    expand_owned = lax.psum_scatter(expand_grad, "fsdp", scatter_dimension=0, tiled=True)
-    branch_share = dot(product, contract_part, ((1,), (0,)), BF)
-    branch_two = plane.scatter(branch_share.reshape(members, rows_here, model))
+    entry_all = plane.gather_rows(entry_two)
+    back_entry_share = branch_share = 0.0
+    reduced = []
+    for size, (expand_part, contract_part) in zip(splits, parts):
+        width = size * layers
+        expanded = dot(entry_all, expand_part, ((1,), (0,)))
+        gate, upward = expanded[:, :width], expanded[:, width:]
+        sigma = jax.nn.sigmoid(gate)
+        activated = gate * sigma
+        product = (activated * upward).astype(BF)
+        back_product = against(upstream_all, contract_part)
+        grad_gate = back_product * upward * sigma * (1.0 + gate * (1.0 - sigma))
+        grad_upward = back_product * activated
+        grad_expanded = jnp.concatenate([grad_gate, grad_upward], axis=1).astype(BF)
+        contract_grad = cross_product(product, upstream_all, BF).reshape(layers, -1, groups * size)
+        expand_grad = cross_product(entry_all, grad_expanded, BF).reshape(layers, -1, groups * size)
+        sent = jnp.concatenate([expand_grad, contract_grad], axis=1)
+        reduced.append(lax.psum_scatter(sent, "fsdp", scatter_dimension=0, tiled=False))
+        back_entry_share = back_entry_share + against(grad_expanded, expand_part)
+        branch_share = branch_share + dot(product, contract_part, ((1,), (0,)))
+    back_entry_two = plane.scatter_rows(back_entry_share)
+    branch_two = plane.scatter_rows(branch_share)
     layer_output = ((hidden + branch_two) * valid).astype(BF)
 
     second_grad = jnp.sum(back_entry_two * normed_two, axis=0)
@@ -361,21 +465,36 @@
         ],
         axis=1,
     ).astype(BF)
-    joint_grad = cross_product(entry_one, grad_joint, BF)
-    joint_mine = plane.scatter(joint_grad.reshape(layers, members, joint_rows, joint_columns), axis=1)
-    back_entry_one = against(grad_joint, joint_full)
+    grad_joint = jnp.swapaxes(grad_joint.reshape(rows_here, members, joint_width), 0, 1)
+    grad_columns = plane.from_ranks(plane.exchange(grad_joint.reshape(members * rows_here, joint_width)))
+    joint_grad = cross_product(entry_one_all, grad_columns, BF).reshape(layers, -1, joint_width)
+    back_entry_one = plane.scatter_rows(against(grad_columns, joint_part))
     first_grad = jnp.sum(back_entry_one * normed_one, axis=0)
     input_gradient = back_hidden + rms_back(back_entry_one * gain_one, normed_one, inverse_one)
 
     out_owned = plane.layers_scatter(out_mine).astype(BF)
-    joint_owned = plane.layers_scatter(joint_mine).astype(BF)
     out_gradient = plane.gather(out_owned).reshape(members * out_rows, model).astype(F32)
-    joint_gradient = plane.gather(joint_owned).reshape(members * joint_rows, joint_columns).astype(F32)
-    contract_gradient = plane.gather(contract_owned).reshape(members * units, model).astype(F32)
-    expand_gradient = column_merge(plane.gather(expand_owned), 2 * layers)
-    small = lax.psum(
-        jnp.concatenate([first_grad, second_grad, query_gain_grad, key_gain_grad]), ("ctx", "fsdp", "rep")
-    )
+    joint_owned = plane.layers_scatter(joint_grad).astype(BF)
+    wide, tall = [], []
+    for size, mine in zip(splits, reduced):
+        rows_in = model // layers
+        if plane.cube:
+            halves = [h.reshape((4,) + mine.shape) for h in plane.gather_near(mine)]
+            wide.append(tuple(halves))
+            both = jnp.concatenate([h[:, rows_in:] for h in halves], axis=0)
+        else:
+            both = lax.all_gather(mine, PLANE, axis=0, tiled=False)
+            wide.append(both)
+            both = both[:, rows_in:]
+        tall.append(plane.to_ranks(both.reshape(members * size, model)).reshape(members, size, model))
+    expand_gradient = column_merge(wide, groups, rank, rows_in)
+    contract_gradient = jnp.concatenate(tall, axis=1).reshape(members * units, model).astype(F32)
+    if plane.cube:
+        joint_pair = tuple(h.reshape((4,) + joint_owned.shape) for h in plane.gather_near(joint_owned))
+        joint_gradient = column_merge([joint_pair], 1, rank, rows_in)
+    else:
+        joint_gradient = column_merge([lax.all_gather(joint_owned, PLANE, axis=0, tiled=False)], 1, rank, rows_in)
+    small = plane.total(jnp.concatenate([first_grad, second_grad, query_gain_grad, key_gain_grad]))
     owned, at = [], 0
     for size in sizes:
         owned.append(lax.dynamic_slice_in_dim(small, at + plane.layer * size, size))

time: 679 us -> 668 us (0.984)
  waiting for transfers between devices: 272 us -> 228 us
  blocking collectives: 43.2 us -> 0 us
  starting transfers between devices: 79.7 us -> 105 us
  local copies, waits for them, and re-layouts: 114 us -> 132 us
  Pallas kernels: 21.5 us -> 38.9 us
  other arithmetic: 46.7 us -> 63.2 us
    ppermute x24 -> x25, waiting for transfers between devices: 134 us -> 84.5 us  [over_y(): return lax.ppermute(v, 'ctx', [(0, 1), (1, 0)])]
    psum x1 -> x0, blocking collectives: 43.2 us -> none  [shards(): lax.psum(jnp.concatenate([first_grad, second_grad, query_gain_grad, key_g...]
    all_gather x2, waiting for transfers between devices: 38.4 us -> 0.01 us  [shards(): got = lax.all_gather(sent, 'fsdp', axis=0, tiled=False)]
    dynamic_update_slice x49 -> x22, local copies, waits for them, and re-layouts: 45.5 us -> 16.1 us  [place(): lax.dynamic_update_index_in_dim(total, jnp.expand_dims(part, axis), index...]
    unnamed x147 -> x150, local copies, waits for them, and re-layouts: 12.1 us -> 36.7 us
    slice x2 -> x32, local copies, waits for them, and re-layouts: 0.26 us -> 23.1 us  [the longest x2 6.8 us: shards(): got[:, :rows_in].reshape(model, groups * size)]
    ppermute x24 -> x25, waiting for transfers between devices: 35.9 us -> 57.6 us  [over_x(): return lax.ppermute(v, 'rep', [(i, i ^ 2) for i in range(4)])]
    pallas_call x2 -> x4, Pallas kernels: 21.5 us -> 38.9 us  [the longest x2 29.3 us: column_merge(): pl.pallas_call(body, out_shape=jax.ShapeDtypeStruct((rows, groups * span)...]
  transfers between devices with their start and end apart: 81 -> 89, of which waited for: 41 -> 43; matrix products, arithmetic and copies ran while one was open for 30% -> 35% of each run, Pallas kernels for 1% -> 2%
where the time goes in v2:
time: 668 us; the launch traced here: 662 us
  waiting for transfers between devices  228 us (34%)
  local copies, waits for them, and re-layouts  132 us (20%)
  starting transfers between devices  105 us (16%)
  matrix products  76.9 us (12%)
  other arithmetic  63.2 us (9%)
  Pallas kernels  38.9 us (6%)
  between operations  16.8 us (3%)
    ppermute x25, waiting for transfers between devices, over_y(): return lax.ppermute(v, 'ctx', [(0, 1), (1, 0)])  84.5 us
    dot_general x18, matrix products, dot(): lax.dot_general(left, right, (dims, ((), ())), preferred_element_type=F32)  68.4 us
    ppermute x25, waiting for transfers between devices, over_x(): return lax.ppermute(v, 'rep', [(i, i ^ 2) for i in range(4)])  57.6 us
    ppermute x9, waiting for transfers between devices, layers_gather(): got = lax.ppermute(v, 'fsdp', [(i, (i + d) % z) for i in range(z)])  53.4 us
    unnamed x150, local copies, waits for them, and re-layouts  36.7 us
    pallas_call x2, Pallas kernels, column_merge(): pl.pallas_call(body, out_shape=jax.ShapeDtypeStruct((rows, groups * span)...  29.3 us
    ppermute x25, starting transfers between devices, over_x(): return lax.ppermute(v, 'rep', [(i, i ^ 2) for i in range(4)])  24.8 us
    ppermute x25, starting transfers between devices, over_y(): return lax.ppermute(v, 'ctx', [(0, 1), (1, 0)])  24.2 us
  transfers between devices with their start and end apart: 89, of which 43 were waited for; matrix products, arithmetic and copies ran while one was open for 35% of the time, Pallas kernels for 2%

profile of v2, /device:TPU:0, one launch (start us, length us, event | category | flops | bytes accessed | tf_op | source)
XLA Modules:
  0.0 661.6 jit_solution(9817828255964747517)
XLA Ops:
  8.4 6.5 column_slices.3
  38.2 5.2 collective-permute-done.5
  43.5 18.3 %collective-permute-done.6 = bf16[1056]{0:T(1024)(128)(2,1)S(1)} collective-permute-done((bf16[1056]{0:T(1024)(128)(2,1)S(1)}, bf16[1056]{0:T(1024)(128)(2,1)S(1)}, u32[]{:S(2)}, u32[]{:S(2)}) %collective-permute-start.6) | collective-permute-done | bytes 2144 | tf_op jit(solution)/shard_map/ppermute | solution.py:199
  61.8 7.3 %collective-permute-start.12 = (bf16[40,2048]{1,0:T(8,128)(2,1)}, bf16[40,2048]{1,0:T(8,128)(2,1)}, u32[]{:S(2)}, u32[]{:S(2)}) collective-permute-start(bf16[40,2048]{1,0:T(8,128)(2,1)} %get-tuple-element.29), channel_id=1, source_target_pairs={{0,4},{4,8},{8,12},{12,0},{1,5},{5,9},{9,13},{13,1},{2,6},{6,10},{... | collective-permute-start | bytes 491528 | tf_op jit(solution)/shard_map/ppermute | solution.py:199
  69.1 3.9 collective-permute-start.13
  73.3 15.4 %collective-permute-done.12 = bf16[40,2048]{1,0:T(8,128)(2,1)} collective-permute-done((bf16[40,2048]{1,0:T(8,128)(2,1)}, bf16[40,2048]{1,0:T(8,128)(2,1)}, u32[]{:S(2)}, u32[]{:S(2)}) %collective-permute-start.12) | collective-permute-done | bytes 163872 | tf_op jit(solution)/shard_map/ppermute | solution.py:199
  89.9 14.4 %collective-permute-done.13 = bf16[40,2048]{1,0:T(8,128)(2,1)} collective-permute-done((bf16[40,2048]{1,0:T(8,128)(2,1)}, bf16[40,2048]{1,0:T(8,128)(2,1)}, u32[]{:S(2)}, u32[]{:S(2)}) %collective-permute-start.13) | collective-permute-done | bytes 163872 | tf_op jit(solution)/shard_map/ppermute | solution.py:199
  111.5 7.6 %collective-permute-done = bf16[128,2048]{1,0:T(8,128)(2,1)S(1)} collective-permute-done((bf16[128,2048]{1,0:T(8,128)(2,1)S(1)}, bf16[128,2048]{1,0:T(8,128)(2,1)S(1)}, u32[]{:S(2)}, u32[]{:S(2)}) %collective-permute-start) | collective-permute-done | bytes 524320 | tf_op jit(solution)/shard_map/ppermute | solution.py:83
  127.1 6.1 collective-permute-done.3
  143.2 10.2 %collective-permute-done.16 = bf16[4,40,2048]{2,1,0:T(8,128)(2,1)S(1)} collective-permute-done((bf16[4,40,2048]{2,1,0:T(8,128)(2,1)S(1)}, bf16[4,40,2048]{2,1,0:T(8,128)(2,1)S(1)}, u32[]{:S(2)}, u32[]{:S(2)}) %collective-permute-start.16) | collective-permute-done | bytes 655392 | tf_op jit(solution)/shard_map/ppermute | solution.py:89
  157.4 5.1 collective-permute-done.18
  171.7 3.5 all-to-all-start
  178.3 3.6 bitcast_dynamic-update-slice_fusion
  185.0 13.8 %collective-permute-start.11 = (bf16[128,640]{0,1:T(8,128)(2,1)S(1)}, bf16[128,640]{0,1:T(8,128)(2,1)S(1)}, u32[]{:S(2)}, u32[]{:S(2)}) collective-permute-start(bf16[128,640]{0,1:T(8,128)(2,1)S(1)} %get-tuple-element.113), channel_id=1, source_target_pairs={{0,16},{1,17},{2,18},{3,19},{4,20},{5,21},{6,22},{7,23},{8,24},{9,... | collective-permute-start | bytes 491528 | tf_op jit(solution)/shard_map/ppermute | solution.py:381
  204.0 3.8 bitcast_dynamic-update-slice_fusion.1
  207.8 3.6 multiply_reduce_fusion.2
  216.4 8.4 %collective-permute-done.20 = bf16[128,2048]{1,0:T(8,128)(2,1)S(1)} collective-permute-done((bf16[128,2048]{1,0:T(8,128)(2,1)S(1)}, bf16[128,2048]{1,0:T(8,128)(2,1)S(1)}, u32[]{:S(2)}, u32[]{:S(2)}) %collective-permute-start.20) | collective-permute-done | bytes 524320 | tf_op jit(solution)/shard_map/ppermute | solution.py:83
  247.7 4.6 fusion.107
  252.3 4.8 multiply_convert_fusion.4
  258.0 4.4 convolution_convert_fusion.4
  264.9 4.9 convolution_convert_fusion.2
  272.0 3.8 slice.457
  278.6 4.2 reshape.354
  282.8 6.8 %fusion.105 = f32[1024,768]{0,1:T(8,128)S(1)} fusion(bf16[1024,2048]{1,0:T(8,128)(2,1)} %constant_dynamic-update-slice_fusion.16, bf16[2048,768]{1,0:T(8,128)(2,1)} %bitcast.347), kind=kOutput, calls=%fused_computation.348 | convolution fusion | flops 3221225472 | bytes 10485760 | tf_op jit(solution)/shard_map/dot_general | solution.py:59
  289.6 4.8 multiply_convert_fusion.1
  295.3 3.5 fusion.41
  314.1 5.4 convolution_convert_fusion.3
  319.4 4.2 reshape.368
  323.7 6.1 convolution_convert_fusion.1
  354.3 9.9 %collective-permute-done.39 = bf16[128,2048]{1,0:T(8,128)(2,1)S(1)} collective-permute-done((bf16[128,2048]{1,0:T(8,128)(2,1)S(1)}, bf16[128,2048]{1,0:T(8,128)(2,1)S(1)}, u32[]{:S(2)}, u32[]{:S(2)}) %collective-permute-start.39) | collective-permute-done | bytes 524320 | tf_op jit(solution)/shard_map/ppermute | solution.py:89
  366.0 8.8 %collective-permute-done.29 = bf16[128,2048]{1,0:T(8,128)(2,1)S(1)} collective-permute-done((bf16[128,2048]{1,0:T(8,128)(2,1)S(1)}, bf16[128,2048]{1,0:T(8,128)(2,1)S(1)}, u32[]{:S(2)}, u32[]{:S(2)}) %collective-permute-start.29) | collective-permute-done | bytes 524320 | tf_op jit(solution)/shard_map/ppermute | solution.py:89
  376.5 4.4 convolution_convert_fusion.6
  388.5 8.8 %collective-permute-done.40 = f32[128,640]{0,1:T(8,128)S(1)} collective-permute-done((f32[128,640]{0,1:T(8,128)S(1)}, f32[128,640]{0,1:T(8,128)S(1)}, u32[]{:S(2)}, u32[]{:S(2)}) %collective-permute-start.40) | collective-permute-done | bytes 327712 | tf_op jit(solution)/shard_map/ppermute | solution.py:446
  398.4 3.5 all-to-all-start.1
  412.2 4.5 convolution_convert_fusion.5
  430.3 15.0 %collective-permute-done.53 = bf16[512,240]{0,1:T(8,128)(2,1)} collective-permute-done((bf16[512,240]{0,1:T(8,128)(2,1)}, bf16[512,240]{0,1:T(8,128)(2,1)}, u32[]{:S(2)}, u32[]{:S(2)}) %collective-permute-start.53) | collective-permute-done | bytes 245792 | tf_op jit(solution)/shard_map/ppermute | solution.py:208
  472.9 3.6 collective-permute-done.61
  492.3 10.1 %column_merge.2 = f32[512,1920]{1,0:T(8,128)} custom-call(s32[1]{0:T(128)} %bitcast.1.rank_ref, bf16[4,512,240]{2,1,0:T(8,128)(2,1)} %bitcast.343, bf16[4,512,240]{2,1,0:T(8,128)(2,1)} %bitcast.344), custom_call_target="tpu_custom_call" | custom-call | tf_op jit(solution)/shard_map/column_merge/pallas_call | solution.py:289
  510.2 3.4 collective-permute-done.62
  518.7 10.2 %collective-permute-done.47 = f32[4224]{0:T(1024)S(1)} collective-permute-done((f32[4224]{0:T(1024)S(1)}, f32[4224]{0:T(1024)S(1)}, u32[]{:S(2)}, u32[]{:S(2)}) %collective-permute-start.47) | collective-permute-done | bytes 16928 | tf_op jit(solution)/shard_map/ppermute | solution.py:83
  537.6 3.8 collective-permute-start.51
  545.8 21.3 %collective-permute-done.80 = bf16[384,512]{1,0:T(8,128)(2,1)S(1)} collective-permute-done((bf16[384,512]{1,0:T(8,128)(2,1)S(1)}, bf16[384,512]{1,0:T(8,128)(2,1)S(1)}, u32[]{:S(2)}, u32[]{:S(2)}) %collective-permute-start.80) | collective-permute-done | bytes 393248 | tf_op jit(solution)/shard_map/ppermute | solution.py:89
  577.2 4.7 collective-permute-done.75
  586.7 5.7 collective-permute-done.69
  614.6 19.2 %column_merge.3 = f32[512,10240]{1,0:T(8,128)} custom-call(s32[1]{0:T(128)} %bitcast.1.rank_ref, bf16[4,768,768]{2,1,0:T(8,128)(2,1)} %bitcast.110.refs_0_, bf16[4,768,768]{2,1,0:T(8,128)(2,1)} %bitcast.111.refs_1_, bf16[4,768,512]{2,1,0:T(8,128)(2,1)} %bitcast.338, bf16[4,768,512]{2,1,0:T(8,128)(2,1)} %bitcast.340), custom_call_target="tpu_custom_call" | custom-call | tf_op jit(solution)/shard_map/column_merge/pallas_call | solution.py:289
  635.9 4.4 reshape_reshape.35
  640.3 4.4 reverse_select_fusion.2
  649.0 5.9 bitcast_convert_fusion
  (537 shorter events, 298.8 us)
Async XLA Ops:
  7.2 230.2 %all-gather.7.cloned.1.call-start = ((), (), s32[]{:S(2)}) async-start(), calls=%async_computation.7 | async-start | bytes 3932160 | tf_op jit(solution)/shard_map/all_gather | solution.py:357
  16.9 255.1 %all-gather.5.cloned.1.call-start = ((), (), s32[]{:S(2)}) async-start(), calls=%async_computation.6 | async-start | bytes 5898240 | tf_op jit(solution)/shard_map/all_gather | solution.py:357
  20.2 90.9 %collective-permute-start.8 = (bf16[512,240]{1,0:T(8,128)(2,1)}, bf16[512,240]{1,0:T(8,128)(2,1)S(1)}, u32[]{:S(2)}, u32[]{:S(2)}) collective-permute-start(bf16[512,240]{1,0:T(8,128)(2,1)} %column_slices.2), channel_id=1, source_target_pairs={{0,4},{4,8},{8,12},{12,0},{1,5},{5,9},{9,13},{13,1},{2,6},{6,10},{... | collective-permute-start | bytes 737288 | tf_op jit(solution)/shard_map/ppermute | solution.py:199
  23.2 111.5 %collective-permute-start.9 = (bf16[512,240]{1,0:T(8,128)(2,1)}, bf16[512,240]{1,0:T(8,128)(2,1)}, u32[]{:S(2)}, u32[]{:S(2)}) collective-permute-start(bf16[512,240]{1,0:T(8,128)(2,1)} %column_slices.2), channel_id=1, source_target_pairs={{0,8},{4,12},{8,0},{12,4},{1,9},{5,13},{9,1},{13,5},{2,10},{6,14},... | collective-permute-start | bytes 737288 | tf_op jit(solution)/shard_map/ppermute | solution.py:199
  25.9 17.6 %collective-permute-start.5 = (bf16[1056]{0:T(1024)(128)(2,1)S(1)}, bf16[1056]{0:T(1024)(128)(2,1)S(1)}, u32[]{:S(2)}, u32[]{:S(2)}) collective-permute-start(bf16[1056]{0:T(1024)(128)(2,1)S(1)} %concatenate.141), channel_id=1, source_target_pairs={{0,4},{4,8},{8,12},{12,0},{1,5},{5,9},{9,13},{13,1},{2,6},{6,10},{... | collective-permute-start | bytes 6344 | tf_op jit(solution)/shard_map/ppermute | solution.py:199
  25.9 35.9 %collective-permute-start.6 = (bf16[1056]{0:T(1024)(128)(2,1)S(1)}, bf16[1056]{0:T(1024)(128)(2,1)S(1)}, u32[]{:S(2)}, u32[]{:S(2)}) collective-permute-start(bf16[1056]{0:T(1024)(128)(2,1)S(1)} %concatenate.141), channel_id=1, source_target_pairs={{0,8},{4,12},{8,0},{12,4},{1,9},{5,13},{9,1},{13,5},{2,10},{6,14},... | collective-permute-start | bytes 6344 | tf_op jit(solution)/shard_map/ppermute | solution.py:199
  27.8 41.3 %collective-permute-start.7 = (bf16[1056]{0:T(1024)(128)(2,1)S(1)}, bf16[1056]{0:T(1024)(128)(2,1)S(1)}, u32[]{:S(2)}, u32[]{:S(2)}) collective-permute-start(bf16[1056]{0:T(1024)(128)(2,1)S(1)} %concatenate.141), channel_id=1, source_target_pairs={{0,12},{4,0},{8,4},{12,8},{1,13},{5,1},{9,5},{13,9},{2,14},{6,2},{... | collective-permute-start | bytes 6344 | tf_op jit(solution)/shard_map/ppermute | solution.py:199
  43.5 92.3 %collective-permute-start.10 = (bf16[512,240]{1,0:T(8,128)(2,1)S(1)}, bf16[512,240]{1,0:T(8,128)(2,1)}, u32[]{:S(2)}, u32[]{:S(2)}) collective-permute-start(bf16[512,240]{1,0:T(8,128)(2,1)S(1)} %copy-done.33), channel_id=1, source_target_pairs={{0,12},{4,0},{8,4},{12,8},{1,13},{5,1},{9,5},{13,9},{2,14},{6,2},{... | collective-permute-start | bytes 737288 | tf_op jit(solution)/shard_map/ppermute | solution.py:199
  61.8 27.0 %collective-permute-start.12 = (bf16[40,2048]{1,0:T(8,128)(2,1)}, bf16[40,2048]{1,0:T(8,128)(2,1)}, u32[]{:S(2)}, u32[]{:S(2)}) collective-permute-start(bf16[40,2048]{1,0:T(8,128)(2,1)} %get-tuple-element.29), channel_id=1, source_target_pairs={{0,4},{4,8},{8,12},{12,0},{1,5},{5,9},{9,13},{13,1},{2,6},{6,10},{... | collective-permute-start | bytes 491528 | tf_op jit(solution)/shard_map/ppermute | solution.py:199
  69.1 35.2 %collective-permute-start.13 = (bf16[40,2048]{1,0:T(8,128)(2,1)}, bf16[40,2048]{1,0:T(8,128)(2,1)}, u32[]{:S(2)}, u32[]{:S(2)}) collective-permute-start(bf16[40,2048]{1,0:T(8,128)(2,1)} %get-tuple-element.29), channel_id=1, source_target_pairs={{0,8},{4,12},{8,0},{12,4},{1,9},{5,13},{9,1},{13,5},{2,10},{6,14},... | collective-permute-start | bytes 491528 | tf_op jit(solution)/shard_map/ppermute | solution.py:199
  88.8 17.9 %collective-permute-start.14 = (bf16[40,2048]{1,0:T(8,128)(2,1)}, bf16[40,2048]{1,0:T(8,128)(2,1)S(1)}, u32[]{:S(2)}, u32[]{:S(2)}) collective-permute-start(bf16[40,2048]{1,0:T(8,128)(2,1)} %get-tuple-element.29), channel_id=1, source_target_pairs={{0,12},{4,0},{8,4},{12,8},{1,13},{5,1},{9,5},{13,9},{2,14},{6,2},{... | collective-permute-start | bytes 491528 | tf_op jit(solution)/shard_map/ppermute | solution.py:199
  111.0 27.4 %collective-permute-start.30 = (bf16[128,2048]{1,0:T(8,128)(2,1)S(1)}, bf16[128,2048]{1,0:T(8,128)(2,1)S(1)}, u32[]{:S(2)}, u32[]{:S(2)}) collective-permute-start(bf16[128,2048]{1,0:T(8,128)(2,1)S(1)} %get-tuple-element.25), channel_id=1, source_target_pairs={{0,2},{1,3},{2,0},{3,1},{4,6},{5,7},{6,4},{7,5},{8,10},{9,11},{10,... | collective-permute-start | bytes 1572872 | tf_op jit(solution)/shard_map/ppermute | solution.py:83
  133.2 20.9 %collective-permute-start.15 = (bf16[4,40,2048]{2,1,0:T(8,128)(2,1)S(1)}, bf16[4,40,2048]{2,1,0:T(8,128)(2,1)S(1)}, u32[]{:S(2)}, u32[]{:S(2)}) collective-permute-start(bf16[4,40,2048]{2,1,0:T(8,128)(2,1)S(1)} %bitcast_dynamic-update-slice_fusion.14), channel_id=1, source_target_pairs={{0,2},{1,3},{2,0},{3,1},{4,6},{5,7},{6,4},{7,5},{8,10},{9,11},{10,... | collective-permute-start | bytes 1966088 | tf_op jit(solution)/shard_map/ppermute | solution.py:83
  134.7 31.8 %collective-permute-start.4 = (bf16[512,2048]{1,0:T(8,128)(2,1)S(1)}, bf16[512,2048]{1,0:T(8,128)(2,1)S(1)}, u32[]{:S(2)}, u32[]{:S(2)}) collective-permute-start(bf16[512,2048]{1,0:T(8,128)(2,1)S(1)} %get-tuple-element.102), channel_id=1, source_target_pairs={{0,1},{1,0},{2,3},{3,2},{4,5},{5,4},{6,7},{7,6},{8,9},{9,8},{10,11... | collective-permute-start | bytes 6291464 | tf_op jit(solution)/shard_map/ppermute | solution.py:86
  135.8 17.6 %collective-permute-start.16 = (bf16[4,40,2048]{2,1,0:T(8,128)(2,1)S(1)}, bf16[4,40,2048]{2,1,0:T(8,128)(2,1)S(1)}, u32[]{:S(2)}, u32[]{:S(2)}) collective-permute-start(bf16[4,40,2048]{2,1,0:T(8,128)(2,1)S(1)} %bitcast_dynamic-update-slice_fusion.14), channel_id=1, source_target_pairs={{0,16},{16,0},{1,17},{17,1},{2,18},{18,2},{3,19},{19,3},{4,20},{20... | collective-permute-start | bytes 1966088 | tf_op jit(solution)/shard_map/ppermute | solution.py:89
  139.2 73.7 %collective-permute-start.32 = (bf16[64,2048]{1,0:T(8,128)(2,1)}, bf16[64,2048]{1,0:T(8,128)(2,1)}, u32[]{:S(2)}, u32[]{:S(2)}) collective-permute-start(bf16[64,2048]{1,0:T(8,128)(2,1)} %slice.480), channel_id=1, source_target_pairs={{0,16},{16,0},{1,17},{17,1},{2,18},{18,2},{3,19},{19,3},{4,20},{20... | collective-permute-start | bytes 786440 | tf_op jit(solution)/shard_map/ppermute | solution.py:89
  140.4 74.2 %collective-permute-start.33 = (bf16[64,2048]{1,0:T(8,128)(2,1)}, bf16[64,2048]{1,0:T(8,128)(2,1)}, u32[]{:S(2)}, u32[]{:S(2)}) collective-permute-start(bf16[64,2048]{1,0:T(8,128)(2,1)} %slice.481), channel_id=1, source_target_pairs={{0,2},{1,3},{2,0},{3,1},{4,6},{5,7},{6,4},{7,5},{8,10},{9,11},{10,... | collective-permute-start | bytes 786440 | tf_op jit(solution)/shard_map/ppermute | solution.py:83
  166.5 37.5 %collective-permute-start.19 = (bf16[4,4,40,2048]{3,2,1,0:T(8,128)(2,1)}, bf16[4,4,40,2048]{3,2,1,0:T(8,128)(2,1)}, u32[]{:S(2)}, u32[]{:S(2)}) collective-permute-start(bf16[4,4,40,2048]{3,2,1,0:T(8,128)(2,1)} %fusion.47), channel_id=1, source_target_pairs={{0,1},{1,0},{2,3},{3,2},{4,5},{5,4},{6,7},{7,6},{8,9},{9,8},{10,11... | collective-permute-start | bytes 7864328 | tf_op jit(solution)/shard_map/ppermute | solution.py:86
  175.2 327.2 %reduce-scatter.5.cloned.1.call-start = ((), (), s32[]{:S(2)}) async-start(), calls=%async_computation.5 | async-start | bytes 3932160 | tf_op jit(solution)/shard_map/reduce_scatter | solution.py:421
  216.3 17.7 %collective-permute-start.34 = (bf16[512,2048]{1,0:T(8,128)(2,1)S(1)}, bf16[512,2048]{1,0:T(8,128)(2,1)S(1)}, u32[]{:S(2)}, u32[]{:S(2)}) collective-permute-start(bf16[512,2048]{1,0:T(8,128)(2,1)S(1)} %get-tuple-element.94), channel_id=1, source_target_pairs={{0,1},{1,0},{2,3},{3,2},{4,5},{5,4},{6,7},{7,6},{8,9},{9,8},{10,11... | collective-permute-start | bytes 6291464 | tf_op jit(solution)/shard_map/ppermute | solution.py:86
  271.7 261.0 %reduce-scatter.3.cloned.1.call-start = ((), (), s32[]{:S(2)}) async-start(), calls=%async_computation.4 | async-start | bytes 5898240 | tf_op jit(solution)/shard_map/reduce_scatter | solution.py:421
  303.1 29.1 %collective-permute-start.35 = (bf16[512,2048]{1,0:T(8,128)(2,1)}, bf16[512,2048]{1,0:T(8,128)(2,1)}, u32[]{:S(2)}, u32[]{:S(2)}) collective-permute-start(bf16[512,2048]{1,0:T(8,128)(2,1)} %slice.669), channel_id=1, source_target_pairs={{0,1},{1,0},{2,3},{3,2},{4,5},{5,4},{6,7},{7,6},{8,9},{9,8},{10,11... | collective-permute-start | bytes 6291464 | tf_op jit(solution)/shard_map/ppermute | solution.py:86
  314.1 25.0 %collective-permute-start.25 = (bf16[512,2048]{1,0:T(8,128)(2,1)}, bf16[512,2048]{1,0:T(8,128)(2,1)}, u32[]{:S(2)}, u32[]{:S(2)}) collective-permute-start(bf16[512,2048]{1,0:T(8,128)(2,1)} %slice.670), channel_id=1, source_target_pairs={{0,1},{1,0},{2,3},{3,2},{4,5},{5,4},{6,7},{7,6},{8,9},{9,8},{10,11... | collective-permute-start | bytes 6291464 | tf_op jit(solution)/shard_map/ppermute | solution.py:86
  346.4 17.8 %collective-permute-start.39 = (bf16[128,2048]{1,0:T(8,128)(2,1)S(1)}, bf16[128,2048]{1,0:T(8,128)(2,1)S(1)}, u32[]{:S(2)}, u32[]{:S(2)}) collective-permute-start(bf16[128,2048]{1,0:T(8,128)(2,1)S(1)} %pad_maximum_fusion.19), channel_id=1, source_target_pairs={{0,16},{16,0},{1,17},{17,1},{2,18},{18,2},{3,19},{19,3},{4,20},{20... | collective-permute-start | bytes 1572872 | tf_op jit(solution)/shard_map/ppermute | solution.py:89
  347.5 16.8 %collective-permute-start.37 = (bf16[128,2048]{1,0:T(8,128)(2,1)S(1)}, bf16[128,2048]{1,0:T(8,128)(2,1)S(1)}, u32[]{:S(2)}, u32[]{:S(2)}) collective-permute-start(bf16[128,2048]{1,0:T(8,128)(2,1)S(1)} %pad_maximum_fusion.18), channel_id=1, source_target_pairs={{0,2},{1,3},{2,0},{3,1},{4,6},{5,7},{6,4},{7,5},{8,10},{9,11},{10,... | collective-permute-start | bytes 1572872 | tf_op jit(solution)/shard_map/ppermute | solution.py:83
  352.1 22.8 %collective-permute-start.29 = (bf16[128,2048]{1,0:T(8,128)(2,1)S(1)}, bf16[128,2048]{1,0:T(8,128)(2,1)S(1)}, u32[]{:S(2)}, u32[]{:S(2)}) collective-permute-start(bf16[128,2048]{1,0:T(8,128)(2,1)S(1)} %pad_maximum_fusion.17), channel_id=1, source_target_pairs={{0,16},{16,0},{1,17},{17,1},{2,18},{18,2},{3,19},{19,3},{4,20},{20... | collective-permute-start | bytes 1572872 | tf_op jit(solution)/shard_map/ppermute | solution.py:89
  353.2 21.7 %collective-permute-start.27 = (bf16[128,2048]{1,0:T(8,128)(2,1)S(1)}, bf16[128,2048]{1,0:T(8,128)(2,1)S(1)}, u32[]{:S(2)}, u32[]{:S(2)}) collective-permute-start(bf16[128,2048]{1,0:T(8,128)(2,1)S(1)} %pad_maximum_fusion.16), channel_id=1, source_target_pairs={{0,2},{1,3},{2,0},{3,1},{4,6},{5,7},{6,4},{7,5},{8,10},{9,11},{10,... | collective-permute-start | bytes 1572872 | tf_op jit(solution)/shard_map/ppermute | solution.py:83
  407.5 55.6 %collective-permute-start.60 = (bf16[4,2,2,40,2048]{4,3,0,2,1:T(8,128)(2,1)}, bf16[4,2,2,40,2048]{4,3,0,2,1:T(8,128)(2,1)}, u32[]{:S(2)}, u32[]{:S(2)}) collective-permute-start(bf16[4,2,2,40,2048]{4,3,0,2,1:T(8,128)(2,1)} %bitcast.316), channel_id=1, source_target_pairs={{0,1},{1,0},{2,3},{3,2},{4,5},{5,4},{6,7},{7,6},{8,9},{9,8},{10,11... | collective-permute-start | bytes 7864328 | tf_op jit(solution)/shard_map/ppermute | solution.py:86
  424.0 21.3 %collective-permute-start.53 = (bf16[512,240]{0,1:T(8,128)(2,1)}, bf16[512,240]{0,1:T(8,128)(2,1)}, u32[]{:S(2)}, u32[]{:S(2)}) collective-permute-start(bf16[512,240]{0,1:T(8,128)(2,1)} %bitcast.319), channel_id=1, source_target_pairs={{0,8},{4,12},{8,0},{12,4},{1,9},{5,13},{9,1},{13,5},{2,10},{6,14},... | collective-permute-start | bytes 737288 | tf_op jit(solution)/shard_map/ppermute | solution.py:208
  427.0 18.2 %collective-permute-start.52 = (bf16[512,240]{0,1:T(8,128)(2,1)}, bf16[512,240]{0,1:T(8,128)(2,1)}, u32[]{:S(2)}, u32[]{:S(2)}) collective-permute-start(bf16[512,240]{0,1:T(8,128)(2,1)} %bitcast.320), channel_id=1, source_target_pairs={{0,4},{4,8},{8,12},{12,0},{1,5},{5,9},{9,13},{13,1},{2,6},{6,10},{... | collective-permute-start | bytes 737288 | tf_op jit(solution)/shard_map/ppermute | solution.py:208
  463.1 27.0 %collective-permute-start.59 = (bf16[2048,240]{0,1:T(8,128)(2,1)}, bf16[2048,240]{0,1:T(8,128)(2,1)}, u32[]{:S(2)}, u32[]{:S(2)}) collective-permute-start(bf16[2048,240]{0,1:T(8,128)(2,1)} %constant_dynamic-update-slice_fusion.33), channel_id=1, source_target_pairs={{0,1},{1,0},{2,3},{3,2},{4,5},{5,4},{6,7},{7,6},{8,9},{9,8},{10,11... | collective-permute-start | bytes 2949128 | tf_op jit(solution)/shard_map/ppermute | solution.py:86
  478.3 32.0 %collective-permute-start.64 = (bf16[4,40,2048]{2,1,0:T(8,128)(2,1)}, bf16[4,40,2048]{2,1,0:T(8,128)(2,1)}, u32[]{:S(2)}, u32[]{:S(2)}) collective-permute-start(bf16[4,40,2048]{2,1,0:T(8,128)(2,1)} %pad_maximum_fusion.15), channel_id=1, source_target_pairs={{0,16},{16,0},{1,17},{17,1},{2,18},{18,2},{3,19},{19,3},{4,20},{20... | collective-permute-start | bytes 1966088 | tf_op jit(solution)/shard_map/ppermute | solution.py:89
  483.0 24.1 %collective-permute-start.45 = (bf16[128,2048]{1,0:T(8,128)(2,1)}, bf16[128,2048]{1,0:T(8,128)(2,1)}, u32[]{:S(2)}, u32[]{:S(2)}) collective-permute-start(bf16[128,2048]{1,0:T(8,128)(2,1)} %pad_maximum_fusion.21), channel_id=1, source_target_pairs={{0,16},{16,0},{1,17},{17,1},{2,18},{18,2},{3,19},{19,3},{4,20},{20... | collective-permute-start | bytes 1572872 | tf_op jit(solution)/shard_map/ppermute | solution.py:89
  484.6 23.2 %collective-permute-start.43 = (bf16[128,2048]{1,0:T(8,128)(2,1)S(1)}, bf16[128,2048]{1,0:T(8,128)(2,1)}, u32[]{:S(2)}, u32[]{:S(2)}) collective-permute-start(bf16[128,2048]{1,0:T(8,128)(2,1)S(1)} %pad_maximum_fusion.20), channel_id=1, source_target_pairs={{0,2},{1,3},{2,0},{3,1},{4,6},{5,7},{6,4},{7,5},{8,10},{9,11},{10,... | collective-permute-start | bytes 1572872 | tf_op jit(solution)/shard_map/ppermute | solution.py:83
  486.5 27.2 %collective-permute-start.62 = (bf16[4,40,2048]{2,1,0:T(8,128)(2,1)}, bf16[4,40,2048]{2,1,0:T(8,128)(2,1)}, u32[]{:S(2)}, u32[]{:S(2)}) collective-permute-start(bf16[4,40,2048]{2,1,0:T(8,128)(2,1)} %pad_maximum_fusion.14), channel_id=1, source_target_pairs={{0,2},{1,3},{2,0},{3,1},{4,6},{5,7},{6,4},{7,5},{8,10},{9,11},{10,... | collective-permute-start | bytes 1966088 | tf_op jit(solution)/shard_map/ppermute | solution.py:83
  502.4 30.3 %collective-permute-start.78 = (bf16[768,512]{1,0:T(8,128)(2,1)}, bf16[768,512]{1,0:T(8,128)(2,1)S(1)}, u32[]{:S(2)}, u32[]{:S(2)}) collective-permute-start(bf16[768,512]{1,0:T(8,128)(2,1)} %bitcast.372), channel_id=1, source_target_pairs={{0,2},{1,3},{2,0},{3,1},{4,6},{5,7},{6,4},{7,5},{8,10},{9,11},{10,... | collective-permute-start | bytes 2359304 | tf_op jit(solution)/shard_map/ppermute | solution.py:83
  507.2 26.6 %collective-permute-start.79 = (bf16[768,512]{1,0:T(8,128)(2,1)}, bf16[768,512]{1,0:T(8,128)(2,1)}, u32[]{:S(2)}, u32[]{:S(2)}) collective-permute-start(bf16[768,512]{1,0:T(8,128)(2,1)} %bitcast.373), channel_id=1, source_target_pairs={{0,16},{16,0},{1,17},{17,1},{2,18},{18,2},{3,19},{19,3},{4,20},{20... | collective-permute-start | bytes 2359304 | tf_op jit(solution)/shard_map/ppermute | solution.py:89
  517.5 20.1 %collective-permute-start.67 = (bf16[40,2048]{1,0:T(8,128)(2,1)}, bf16[40,2048]{1,0:T(8,128)(2,1)}, u32[]{:S(2)}, u32[]{:S(2)}) collective-permute-start(bf16[40,2048]{1,0:T(8,128)(2,1)} %get-tuple-element.54), channel_id=1, source_target_pairs={{0,12},{4,0},{8,4},{12,8},{1,13},{5,1},{9,5},{13,9},{2,14},{6,2},{... | collective-permute-start | bytes 491528 | tf_op jit(solution)/shard_map/ppermute | solution.py:208
  517.5 23.9 %collective-permute-start.66 = (bf16[40,2048]{1,0:T(8,128)(2,1)}, bf16[40,2048]{1,0:T(8,128)(2,1)}, u32[]{:S(2)}, u32[]{:S(2)}) collective-permute-start(bf16[40,2048]{1,0:T(8,128)(2,1)} %get-tuple-element.55), channel_id=1, source_target_pairs={{0,8},{4,12},{8,0},{12,4},{1,9},{5,13},{9,1},{13,5},{2,10},{6,14},... | collective-permute-start | bytes 491528 | tf_op jit(solution)/shard_map/ppermute | solution.py:208
  532.7 35.6 %collective-permute-start.73 = (bf16[768,768]{1,0:T(8,128)(2,1)}, bf16[768,768]{1,0:T(8,128)(2,1)S(1)}, u32[]{:S(2)}, u32[]{:S(2)}) collective-permute-start(bf16[768,768]{1,0:T(8,128)(2,1)} %bitcast.370), channel_id=1, source_target_pairs={{0,2},{1,3},{2,0},{3,1},{4,6},{5,7},{6,4},{7,5},{8,10},{9,11},{10,... | collective-permute-start | bytes 3538952 | tf_op jit(solution)/shard_map/ppermute | solution.py:83
  533.8 39.4 %collective-permute-start.74 = (bf16[768,768]{1,0:T(8,128)(2,1)}, bf16[768,768]{1,0:T(8,128)(2,1)S(1)}, u32[]{:S(2)}, u32[]{:S(2)}) collective-permute-start(bf16[768,768]{1,0:T(8,128)(2,1)} %bitcast.371), channel_id=1, source_target_pairs={{0,16},{16,0},{1,17},{17,1},{2,18},{18,2},{3,19},{19,3},{4,20},{20... | collective-permute-start | bytes 3538952 | tf_op jit(solution)/shard_map/ppermute | solution.py:89
  537.6 48.2 %collective-permute-start.51 = (f32[4224]{0:T(1024)S(1)}, f32[4224]{0:T(1024)S(1)}, u32[]{:S(2)}, u32[]{:S(2)}) collective-permute-start(f32[4224]{0:T(1024)S(1)} %add.517), channel_id=1, source_target_pairs={{0,12},{4,0},{8,4},{12,8},{1,13},{5,1},{9,5},{13,9},{2,14},{6,2},{... | collective-permute-start | bytes 50696 | tf_op jit(solution)/shard_map/ppermute | solution.py:190
  541.4 25.8 %collective-permute-start.80 = (bf16[384,512]{1,0:T(8,128)(2,1)S(1)}, bf16[384,512]{1,0:T(8,128)(2,1)S(1)}, u32[]{:S(2)}, u32[]{:S(2)}) collective-permute-start(bf16[384,512]{1,0:T(8,128)(2,1)S(1)} %slice.528), channel_id=1, source_target_pairs={{0,16},{16,0},{1,17},{17,1},{2,18},{18,2},{3,19},{19,3},{4,20},{20... | collective-permute-start | bytes 1179656 | tf_op jit(solution)/shard_map/ppermute | solution.py:89
  542.0 29.6 %collective-permute-start.81 = (bf16[384,512]{1,0:T(8,128)(2,1)S(1)}, bf16[384,512]{1,0:T(8,128)(2,1)S(1)}, u32[]{:S(2)}, u32[]{:S(2)}) collective-permute-start(bf16[384,512]{1,0:T(8,128)(2,1)S(1)} %slice.529), channel_id=1, source_target_pairs={{0,2},{1,3},{2,0},{3,1},{4,6},{5,7},{6,4},{7,5},{8,10},{9,11},{10,... | collective-permute-start | bytes 1179656 | tf_op jit(solution)/shard_map/ppermute | solution.py:83
  567.2 19.3 %collective-permute-start.50 = (f32[4224]{0:T(1024)S(1)}, f32[4224]{0:T(1024)S(1)}, u32[]{:S(2)}, u32[]{:S(2)}) collective-permute-start(f32[4224]{0:T(1024)S(1)} %add.517), channel_id=1, source_target_pairs={{0,8},{4,12},{8,0},{12,4},{1,9},{5,13},{9,1},{13,5},{2,10},{6,14},... | collective-permute-start | bytes 50696 | tf_op jit(solution)/shard_map/ppermute | solution.py:190
  568.4 18.3 %collective-permute-start.49 = (f32[4224]{0:T(1024)S(1)}, f32[4224]{0:T(1024)S(1)}, u32[]{:S(2)}, u32[]{:S(2)}) collective-permute-start(f32[4224]{0:T(1024)S(1)} %add.517), channel_id=1, source_target_pairs={{0,4},{4,8},{8,12},{12,0},{1,5},{5,9},{9,13},{13,1},{2,6},{6,10},{... | collective-permute-start | bytes 50696 | tf_op jit(solution)/shard_map/ppermute | solution.py:190
  584.9 16.9 %collective-permute-start.82 = (bf16[3072,512]{1,0:T(8,128)(2,1)S(1)}, bf16[3072,512]{1,0:T(8,128)(2,1)S(1)}, u32[]{:S(2)}, u32[]{:S(2)}) collective-permute-start(bf16[3072,512]{1,0:T(8,128)(2,1)S(1)} %constant_dynamic-update-slice_fusion.43), channel_id=1, source_target_pairs={{0,1},{1,0},{2,3},{3,2},{4,5},{5,4},{6,7},{7,6},{8,9},{9,8},{10,11... | collective-permute-start | bytes 9437192 | tf_op jit(solution)/shard_map/ppermute | solution.py:86
  586.4 28.1 %collective-permute-start.77 = (bf16[3072,768]{1,0:T(8,128)(2,1)}, bf16[3072,768]{1,0:T(8,128)(2,1)}, u32[]{:S(2)}, u32[]{:S(2)}) collective-permute-start(bf16[3072,768]{1,0:T(8,128)(2,1)} %constant_dynamic-update-slice_fusion.38), channel_id=1, source_target_pairs={{0,1},{1,0},{2,3},{3,2},{4,5},{5,4},{6,7},{7,6},{8,9},{9,8},{10,11... | collective-permute-start | bytes 14155784 | tf_op jit(solution)/shard_map/ppermute | solution.py:86
  (102 other events, 966.1 us)
Sparse Core Ops, SparseCore 0:
  17.0 97.0 all-gather.6
  115.6 88.5 all-gather.4
  271.9 58.2 reduce-scatter.4
  332.3 85.2 reduce-scatter.2

commit v3 on v1

v3 whole, which is shorter than its diff:
```python
import functools
import math

import jax
import jax.numpy as jnp
from jax import lax
from jax.experimental import pallas as pl
from jax.experimental.pallas import tpu as pltpu
from jax.sharding import PartitionSpec as P

QUERY_HEADS = 20
KEY_VALUE_HEADS = 5
HEAD_SIZE = 64
FF = 5120
LANES = 128

epsilon = 1e-06
masked_fill_value = -1e30
PLANE = ("ctx", "rep")
BF = jnp.bfloat16
F32 = jnp.float32


def tables(positions, width):
    steps = jnp.arange(width // 2, dtype=jnp.float32)
    rates = jnp.exp(steps * (-2.0 * math.log(10000.0) / width))
    angles = positions.astype(jnp.float32)[:, None] * rates[None, :]
    return (jnp.cos(angles)[:, None, :], jnp.sin(angles)[:, None, :])


def rotate(field, cosine_table, sine_table):
    half = field.shape[-1] // 2
    first, second = (field[..., :half], field[..., half:])
    return jnp.concatenate(
        [first * cosine_table - second * sine_table, second * cosine_table + first * sine_table],
        axis=-1,
    )


def reverse_rotation(upstream, cosine_table, sine_table):
    half = upstream.shape[-1] // 2
    first, second = (upstream[..., :half], upstream[..., half:])
    return jnp.concatenate(
        [first * cosine_table + second * sine_table, second * cosine_table - first * sine_table],
        axis=-1,
    )


def rms_parts(field):
    inverse = lax.rsqrt(jnp.mean(field * field, axis=-1, keepdims=True) + epsilon)
    return (field * inverse, inverse)


def rms_back(upstream, normed, inverse):
    return inverse * (upstream - normed * jnp.mean(upstream * normed, axis=-1, keepdims=True))


def dot(left, right, dims, out=F32):
    got = lax.dot_general(left, right, (dims, ((), ())), preferred_element_type=F32)
    return got.astype(out)


def cross_product(left, right, out=F32):
    return dot(left, right, ((0,), (0,)), out)


def against(left, right, out=F32):
    return dot(left, right, ((1,), (1,)), out)


class Plane:
    def __init__(self):
        self.c, self.r, self.z = (lax.axis_size(a) for a in ("ctx", "rep", "fsdp"))
        self.size = self.c * self.r
        self.cube = self.c == 2 and self.r == 4 and self.z == 4
        rep = lax.axis_index("rep")
        self.y, self.x, self.core = lax.axis_index("ctx"), rep // 2, rep % 2
        self.rank = lax.axis_index("ctx") * self.r + rep
        self.layer = lax.axis_index("fsdp")
        self.place = jnp.stack([self.rank, self.layer]).astype(jnp.int32)

    def over_x(self, v):
        return lax.ppermute(v, "rep", [(i, i ^ 2) for i in range(4)])

    def over_core(self, v):
        return lax.ppermute(v, "rep", [(i, i ^ 1) for i in range(4)])

    def over_y(self, v):
        return lax.ppermute(v, "ctx", [(0, 1), (1, 0)])

    def gather_pair(self, v):
        half = v.shape[0] // 2
        from_x, from_y = self.over_x(v), self.over_y(v)
        far_a = self.over_y(from_x[:half])
        far_b = self.over_x(from_y[half:])
        near = jnp.concatenate([v, from_x, from_y, far_a, far_b], axis=0)
        other = self.over_core(near)
        shape = (4,) + v.shape
        return near.reshape(shape), other.reshape(shape)

    def gather_rows(self, v):
        if not self.cube:
            return lax.all_gather(v, PLANE, axis=0, tiled=True)
        near, other = self.gather_pair(v)
        return jnp.concatenate([near, other], axis=0).reshape(8 * v.shape[0], *v.shape[1:])

    def scatter_rows(self, v):
        if not self.cube:
            return lax.psum_scatter(v.astype(BF), PLANE, scatter_dimension=0, tiled=True).astype(F32)
        n = v.shape[0] // 8
        got = self.over_core(v[4 * n :].astype(BF)).astype(F32)
        part = lambda k: v[k * n : (k + 1) * n].astype(F32) + got[k * n : (k + 1) * n]
        return self.scatter_four(part(0), part(1), part(2), part(3))

    def scatter_four(self, mine, near_x, near_y, far):
        far = far.astype(BF)
        half = far.shape[0] // 2
        got_x, got_y = self.over_x(far[:half]), self.over_y(far[half:])
        near_y = jnp.concatenate([near_y[:half] + got_x.astype(F32), near_y[half:]], axis=0)
        near_x = jnp.concatenate([near_x[:half], near_x[half:] + got_y.astype(F32)], axis=0)
        in_x, in_y = self.over_x(near_x.astype(BF)), self.over_y(near_y.astype(BF))
        return mine + in_x.astype(F32) + in_y.astype(F32)

    def scatter(self, v):
        if not self.cube:
            moved = jnp.moveaxis(v, 1, 0)
            return lax.psum_scatter(moved.astype(BF), PLANE, scatter_dimension=0, tiled=False).astype(F32)
        v = v.reshape(v.shape[:1] + (2, 2, 2) + v.shape[2:])
        pick = lambda a, i, ax: lax.dynamic_index_in_dim(a, i, ax, keepdims=False)
        x, y, core = self.x, self.y, self.core
        got = self.over_core(pick(v, 1 - core, 3).astype(BF))
        v = pick(v, core, 3).astype(F32) + got.astype(F32)
        row, away = pick(v, y, 1), pick(v, 1 - y, 1)
        return self.scatter_four(pick(row, x, 1), pick(row, 1 - x, 1), pick(away, x, 1), pick(away, 1 - x, 1))

    def to_ranks(self, v):
        if not self.cube:
            return v
        n = v.shape[0] // 8
        v = v.reshape((2, 2, 2, n) + v.shape[1:])
        for axis, bit in ((1, self.y), (2, self.x), (0, self.core)):
            v = jnp.where(bit == 1, jnp.flip(v, axis), v)
        return jnp.moveaxis(v, 0, 2).reshape((8 * n,) + v.shape[4:])

    def from_ranks(self, v):
        if not self.cube:
            return v
        n = v.shape[0] // 8
        v = jnp.moveaxis(v.reshape((2, 2, 2, n) + v.shape[1:]), 2, 0)
        for axis, bit in ((1, self.y), (2, self.x), (0, self.core)):
            v = jnp.where(bit == 1, jnp.flip(v, axis), v)
        return v.reshape((8 * n,) + v.shape[4:])

    def exchange(self, v):
        return lax.all_to_all(v, PLANE, split_axis=0, concat_axis=0, tiled=True)

    def total(self, v):
        if not self.cube:
            return lax.psum(v, ("ctx", "fsdp", "rep"))
        v = v + self.over_core(v)
        v = v + self.over_x(v)
        v = v + self.over_y(v)
        for part in self.from_layers(lambda d: v):
            v = v + part
        return v

    def from_layers(self, get):
        z = self.z
        return [lax.ppermute(get(d), "fsdp", [(i, (i + d) % z) for i in range(z)]) for d in range(1, z)]

    def layers_gather(self, v):
        return jnp.stack([v] + self.from_layers(lambda d: v))

    def layers_scatter(self, v):
        pick = lambda d: lax.dynamic_index_in_dim(v, (self.layer + d) % self.z, 0, keepdims=False)
        total = pick(0).astype(F32)
        for part in self.from_layers(lambda d: pick(d).astype(BF)):
            total = total + part.astype(F32)
        return total


def call(body, place, arrays, grid, in_specs, out_shape, out_specs, name, **more):
    size = sum(math.prod(a.shape) * a.dtype.itemsize for a in arrays)
    return pl.pallas_call(
        body,
        out_shape=out_shape,
        grid_spec=pltpu.PrefetchScalarGridSpec(
            num_scalar_prefetch=1, grid=grid, in_specs=in_specs, out_specs=out_specs
        ),
        cost_estimate=pl.CostEstimate(flops=0, transcendentals=0, bytes_accessed=2 * size),
        name=name,
        **more,
    )(place, *arrays)


def layers_order(v, place):
    z = v.shape[0]

    def body(place_ref, source, out):
        out[...] = source[...]

    block = (1,) + v.shape[1:]
    return call(
        body,
        place,
        [v],
        (z,),
        [pl.BlockSpec(block, lambda d, at: (d, 0, 0))],
        jax.ShapeDtypeStruct(v.shape, v.dtype),
        pl.BlockSpec(block, lambda d, at: (lax.rem(at[1] - d + z, z), 0, 0)),
        "layers_order",
    )


def pair_order(pair, place):
    near, other = pair
    z, rows, columns = near.shape[1:]

    def body(place_ref, near_ref, other_ref, out):
        @pl.when(pl.program_id(0) == 0)
        def _():
            out[0, 0] = near_ref[0, 0]

        @pl.when(pl.program_id(0) == 1)
        def _():
            out[0, 0] = other_ref[0, 0]

    block = (1, 1, rows, columns)
    return call(
        body,
        place,
        [near, other],
        (2, 4, z),
        [
            pl.BlockSpec(block, lambda c, i, d, at: (jnp.where(c == 0, i, 3), jnp.where(c == 0, d, z - 1), 0, 0)),
            pl.BlockSpec(block, lambda c, i, d, at: (jnp.where(c == 1, i, 0), jnp.where(c == 1, d, 0), 0, 0)),
        ],
        jax.ShapeDtypeStruct((z, 8, rows, columns), near.dtype),
        pl.BlockSpec(block, lambda c, i, d, at: (lax.rem(at[1] - d + z, z), at[0] ^ (2 * i + c), 0, 0)),
        "pair_order",
    )


MAIN, REST = 128, 32


def unit_columns(matrix, place):
    rows, columns = matrix.shape
    groups = 8
    span = columns // groups // LANES
    block = 128

    def body(place_ref, *refs):
        out = refs[-1]
        lanes = lax.broadcasted_iota(jnp.int32, (block, LANES), 1) // REST
        turn = lax.rem(place_ref[0], 4)
        for side in range(2):
            rest = jnp.zeros((block, LANES), F32)
            for k in range(4):
                g = side * 4 + k
                out[:, side * 640 + k * MAIN : side * 640 + (k + 1) * MAIN] = refs[2 * g][...]
                turned = pltpu.roll(refs[2 * g + 1][...].astype(F32), lax.rem(k - turn + 4, 4) * REST, 1)
                rest = jnp.where(lanes == k, turned, rest)
            out[:, side * 640 + 4 * MAIN : (side + 1) * 640] = rest.astype(out.dtype)

    def main(g):
        return pl.BlockSpec((block, LANES), lambda i, at: (i, g * span + at[0]))

    def rest(g):
        return pl.BlockSpec((block, LANES), lambda i, at: (i, g * span + 8 + at[0] // 4))

    return call(
        body,
        place,
        [matrix] * (2 * groups),
        (rows // block,),
        [spec(g) for g in range(groups) for spec in (main, rest)],
        jax.ShapeDtypeStruct((rows, 1280), matrix.dtype),
        pl.BlockSpec((block, 1280), lambda i, at: (i, 0)),
        "unit_columns",
    )


def joint_columns_of(matrix, place):
    rows, columns = matrix.shape
    last = columns // LANES - 1
    block = 256

    def body(place_ref, left, right, out):
        out[:, :LANES] = left[...]
        out[:, LANES:] = right[...]

    return call(
        body,
        place,
        [matrix, matrix],
        (rows // block,),
        [
            pl.BlockSpec((block, LANES), lambda i, at: (i, 2 * at[0])),
            pl.BlockSpec((block, LANES), lambda i, at: (i, jnp.minimum(2 * at[0] + 1, last))),
        ],
        jax.ShapeDtypeStruct((rows, 2 * LANES), matrix.dtype),
        pl.BlockSpec((block, 2 * LANES), lambda i, at: (i, 0)),
        "joint_columns",
    )


def unit_merge(pair, place, side, into):
    rows = pair[0].shape[1]
    block = 64

    def body(place_ref, near, other, *refs):
        out = refs[-1]
        rank = place_ref[0]
        lanes = lax.broadcasted_iota(jnp.int32, (block, LANES), 1) // REST

        def fill(even, odd):
            def piece(k, start):
                source = odd if k % 2 else even
                index = lax.shift_right_logical(jnp.bitwise_xor(rank, k), 1)
                return source[index, :, start : start + LANES].astype(F32)

            for k in range(8):
                for g in range(4):
                    start = g * 1280 + k * MAIN
                    out[:, start : start + MAIN] = piece(k, g * MAIN)
            for b in range(2):
                rests = [piece(4 * b + q, 4 * MAIN) for q in range(4)]
                for g in range(4):
                    total = jnp.zeros((block, LANES), F32)
                    for q in range(4):
                        turned = rests[q] if q == g else pltpu.roll(rests[q], (q - g) % 4 * REST, 1)
                        total = jnp.where(lanes == q, turned, total)
                    start = g * 1280 + 8 * MAIN + b * LANES
                    out[:, start : start + LANES] = total

        @pl.when(lax.rem(rank, 2) == 0)
        def _():
            fill(near, other)

        @pl.when(lax.rem(rank, 2) == 1)
        def _():
            fill(other, near)

    source = pl.BlockSpec((4, block, 640), lambda i, at: (0, i, 0))
    arrays, specs, more = list(pair), [source, source], {}
    if into is not None:
        arrays.append(into)
        specs.append(pl.BlockSpec(memory_space=pl.ANY))
        more["input_output_aliases"] = {3: 0}
    return call(
        body,
        place,
        arrays,
        (rows // block,),
        specs,
        jax.ShapeDtypeStruct((rows, 10240), F32),
        pl.BlockSpec((block, 5120), lambda i, at: (i, side)),
        "unit_merge",
        **more,
    )


def unit_rows_merge(pair, place):
    near, other = pair
    columns = near.shape[2]
    steps = (MAIN + REST) // REST

    def body(place_ref, near_ref, other_ref, out):
        @pl.when(pl.program_id(0) == 0)
        def _():
            out[...] = near_ref[0].astype(F32)

        @pl.when(pl.program_id(0) == 1)
        def _():
            out[...] = other_ref[0].astype(F32)

    block = (1, REST, columns)

    def target(c, i, b, at):
        rank = at[0] ^ (2 * i + c)
        return (jnp.where(b < 4, 4 * rank + b, 32 + rank), 0)

    return call(
        body,
        place,
        [near, other],
        (2, 4, steps),
        [
            pl.BlockSpec(block, lambda c, i, b, at: (jnp.where(c == 0, i, 3), jnp.where(c == 0, b, steps - 1), 0)),
            pl.BlockSpec(block, lambda c, i, b, at: (jnp.where(c == 1, i, 0), jnp.where(c == 1, b, 0), 0)),
        ],
        jax.ShapeDtypeStruct((8 * (MAIN + REST), columns), F32),
        pl.BlockSpec((REST, columns), target),
        "unit_rows_merge",
    )


def rows_merge(pair, place):
    near, other = pair
    rows, columns = near.shape[1:]

    def body(place_ref, near_ref, other_ref, out):
        @pl.when(pl.program_id(0) == 0)
        def _():
            out[...] = near_ref[0].astype(F32)

        @pl.when(pl.program_id(0) == 1)
        def _():
            out[...] = other_ref[0].astype(F32)

    block = (1, rows, columns)
    return call(
        body,
        place,
        [near, other],
        (2, 4),
        [
            pl.BlockSpec(block, lambda c, i, at: (jnp.where(c == 0, i, 3), 0, 0)),
            pl.BlockSpec(block, lambda c, i, at: (jnp.where(c == 1, i, 0), 0, 0)),
        ],
        jax.ShapeDtypeStruct((8 * rows, columns), F32),
        pl.BlockSpec((rows, columns), lambda c, i, at: (at[0] ^ (2 * i + c), 0)),
        "rows_merge",
    )


def joint_merge(pair, place, columns):
    near, other = pair
    rows = near.shape[1]
    block = 128

    def body(place_ref, near_ref, other_ref, out):
        rank = place_ref[0]

        def fill(even, odd):
            for k in range(8):
                source = odd if k % 2 else even
                index = lax.shift_right_logical(jnp.bitwise_xor(rank, k), 1)
                width = min(256, columns - 256 * k)
                out[:, 256 * k : 256 * k + width] = source[index, :, :width].astype(F32)

        @pl.when(lax.rem(rank, 2) == 0)
        def _():
            fill(near_ref, other_ref)

        @pl.when(lax.rem(rank, 2) == 1)
        def _():
            fill(other_ref, near_ref)

    source = pl.BlockSpec((4, block, 256), lambda i, at: (0, i, 0))
    return call(
        body,
        place,
        [near, other],
        (rows // block,),
        [source, source],
        jax.ShapeDtypeStruct((rows, columns), F32),
        pl.BlockSpec((block, columns), lambda i, at: (i, 0)),
        "joint_merge",
    )


def after(value, *earlier):
    return lax.optimization_barrier((value, *earlier))[0]


def shards(
    tokens,
    cotangent,
    lengths,
    first_gain,
    joint_matrix,
    query_gain,
    key_gain,
    out_weight,
    second_gain,
    expand_weight,
    contract_weight,
):
    plane = Plane()
    cube, members, layers, rank, at_place = plane.cube, plane.size, plane.z, plane.rank, plane.place
    rows_here = tokens.shape[1]
    model = tokens.shape[2]
    place_ctx = lax.axis_index("ctx")
    contexts = lax.axis_size("ctx")
    span = rows_here * contexts
    slot_length_value = lengths[0]
    positions = place_ctx * rows_here + jnp.arange(rows_here, dtype=jnp.int32)
    valid = (positions < slot_length_value).astype(F32)[:, None]
    query_width = QUERY_HEADS * HEAD_SIZE
    key_width = KEY_VALUE_HEADS * HEAD_SIZE
    head_group = QUERY_HEADS // KEY_VALUE_HEADS
    scale = HEAD_SIZE ** (-0.5)
    joint_columns = joint_matrix.shape[1]

    rows = tokens[0].astype(F32)
    tokens_all = plane.gather_rows(tokens[0])

    sizes = [first_gain.shape[0], second_gain.shape[0], query_gain.shape[0], key_gain.shape[0]]
    joint_width = 2048 // members
    if cube:
        joint_share = joint_columns_of(joint_matrix, at_place)
    else:
        padded = jnp.pad(joint_matrix, ((0, 0), (0, joint_width * members - joint_columns)))
        joint_share = lax.dynamic_slice_in_dim(padded, rank * joint_width, joint_width, 1)
    packed = jnp.concatenate([first_gain, second_gain, query_gain, key_gain])
    fill = -packed.shape[0] % (8 * joint_width)
    packed = jnp.pad(packed, (0, fill)).reshape(-1, joint_width)
    joint_sent = jnp.concatenate([joint_share, packed], axis=0)
    if cube:
        joint_got = layers_order(plane.layers_gather(joint_sent), at_place)
    else:
        joint_got = lax.all_gather(joint_sent, "fsdp", axis=0, tiled=False)
    joint_rows = joint_share.shape[0]
    joint_part = joint_got[:, :joint_rows].reshape(model, joint_width)
    packed = joint_got[:, joint_rows:].reshape(layers, -1)
    gains, at = [], 0
    for size in sizes:
        gains.append(packed[:, at : at + size].reshape(-1).astype(F32))
        at += size
    gain_one, gain_two, query_scale, key_scale = gains

    out_rows = out_weight.shape[0] // members
    out_share = lax.dynamic_slice_in_dim(out_weight, rank * out_rows, out_rows, 0)
    if cube:
        out_share = after(out_share, joint_got)
        out_full = pair_order(plane.gather_pair(plane.layers_gather(out_share)), at_place)
        out_full = out_full.reshape(query_width, model)
    else:
        out_full = lax.all_gather(out_weight, "fsdp", axis=0, tiled=True)

    units = contract_weight.shape[0] // members
    width = units * layers
    if cube:
        expand_share = unit_columns(after(expand_weight, joint_sent), at_place)
        main_share = lax.dynamic_slice_in_dim(contract_weight, rank * MAIN, MAIN, 0)
        rest_share = lax.dynamic_slice_in_dim(contract_weight, members * MAIN + rank * REST, REST, 0)
        contract_share = jnp.concatenate([main_share, rest_share], axis=0)
    else:
        share = expand_weight.reshape(-1, 2 * layers, members, units)
        expand_share = lax.dynamic_index_in_dim(share, rank, 2, keepdims=False).reshape(-1, 2 * width)
        contract_share = lax.dynamic_slice_in_dim(contract_weight, rank * units, units, 0)
    expand_part = lax.all_gather(expand_share, "fsdp", axis=0, tiled=True)
    contract_part = lax.all_gather(contract_share, "fsdp", axis=0, tiled=False)
    if cube:
        contract_part = jnp.concatenate(
            [contract_part[:, :MAIN].reshape(-1, model), contract_part[:, MAIN:].reshape(-1, model)], axis=0
        )
    else:
        contract_part = contract_part.reshape(width, model)

    upstream = cotangent[0].astype(F32) * valid
    upstream_all = plane.gather_rows(after(upstream.astype(BF), tokens_all))

    entry_one_all = (rms_parts(tokens_all.astype(F32))[0] * gain_one).astype(BF)
    normed_one, inverse_one = rms_parts(rows)
    joint_columns_all = plane.to_ranks(dot(entry_one_all, joint_part, ((1,), (0,))))
    joint_projection = plane.exchange(joint_columns_all).reshape(members, rows_here, joint_width)
    joint_projection = jnp.swapaxes(joint_projection, 0, 1).reshape(rows_here, members * joint_width)
    query_raw = joint_projection[:, :query_width].reshape(rows_here, QUERY_HEADS, HEAD_SIZE)
    key_raw = joint_projection[:, query_width : query_width + key_width].reshape(
        rows_here, KEY_VALUE_HEADS, HEAD_SIZE
    )
    value_part = joint_projection[:, query_width + key_width : joint_columns]
    cosine_table, sine_table = tables(positions, HEAD_SIZE)
    query_normed, query_inverse = rms_parts(query_raw)
    rotated_query = rotate(query_normed * query_scale, cosine_table, sine_table).astype(BF)
    key_normed, key_inverse = rms_parts(key_raw)
    key_rot = rotate(key_normed * key_scale, cosine_table, sine_table).astype(BF)
    local_pair = jnp.concatenate([key_rot.reshape(rows_here, key_width), value_part.astype(BF)], axis=1)
    if contexts == 2:
        earlier = lax.ppermute(local_pair, "ctx", [(0, 1)])
        first = place_ctx == 0
        pair_all = jnp.concatenate(
            [jnp.where(first, local_pair, earlier), jnp.where(first, 0, local_pair).astype(BF)], axis=0
        )
    else:
        pair_all = lax.all_gather(local_pair, "ctx", axis=0, tiled=True)
    key_all = pair_all[:, :key_width].reshape(span, KEY_VALUE_HEADS, HEAD_SIZE)
    value_all = pair_all[:, key_width:].reshape(span, KEY_VALUE_HEADS, HEAD_SIZE)
    grouped_query = rotated_query.reshape(rows_here, KEY_VALUE_HEADS, head_group, HEAD_SIZE)
    key_pos = jnp.arange(span, dtype=jnp.int32)
    allowed = (key_pos[None, :] <= positions[:, None]) & (key_pos[None, :] < slot_length_value)
    scores = jnp.einsum("qgrd,kgd->grqk", grouped_query, key_all, preferred_element_type=F32) * scale
    scores = jnp.where(allowed, scores, masked_fill_value)
    powers = jnp.where(allowed, jnp.exp(scores - jnp.max(scores, axis=-1, keepdims=True)), 0.0)
    shares = powers / jnp.sum(powers, axis=-1, keepdims=True)
    shares_b = shares.astype(BF)
    mixed = jnp.einsum("grqk,kgd->qgrd", shares_b, value_all, preferred_element_type=F32)
    mixed_output = mixed.reshape(rows_here, query_width).astype(BF)
    hidden = rows + dot(mixed_output, out_full, ((1,), (0,)))

    normed_two, inverse_two = rms_parts(hidden)
    entry_two = (normed_two * gain_two).astype(BF)
    entry_all = plane.gather_rows(entry_two)
    expanded = dot(entry_all, expand_part, ((1,), (0,)))
    gate, upward = expanded[:, :width], expanded[:, width:]
    sigma = jax.nn.sigmoid(gate)
    activated = gate * sigma
    product = (activated * upward).astype(BF)
    contract_grad = cross_product(product, upstream_all, BF)
    if cube:
        contract_grad = jnp.concatenate(
            [
                contract_grad[: layers * MAIN].reshape(layers, MAIN, model),
                contract_grad[layers * MAIN :].reshape(layers, REST, model),
            ],
            axis=1,
        )
    else:
        contract_grad = contract_grad.reshape(layers, units, model)
    contract_owned = lax.psum_scatter(contract_grad, "fsdp", scatter_dimension=0, tiled=False)
    back_product = against(upstream_all, contract_part)
    grad_gate = (back_product * upward * sigma * (1.0 + gate * (1.0 - sigma))).astype(BF)
    grad_upward = (back_product * activated).astype(BF)
    grad_expanded = jnp.concatenate([grad_gate, grad_upward], axis=1)
    back_entry_two = plane.scatter_rows(against(grad_expanded, expand_part))
    gate_grad = cross_product(entry_all, grad_gate, BF)
    up_grad = cross_product(entry_all, grad_upward, BF)
    gate_owned = lax.psum_scatter(gate_grad, "fsdp", scatter_dimension=0, tiled=True)
    up_owned = lax.psum_scatter(up_grad, "fsdp", scatter_dimension=0, tiled=True)
    branch_two = plane.scatter_rows(dot(product, contract_part, ((1,), (0,))))
    layer_output = ((hidden + branch_two) * valid).astype(BF)

    second_grad = jnp.sum(back_entry_two * normed_two, axis=0)
    back_hidden = upstream + rms_back(back_entry_two * gain_two, normed_two, inverse_two)

    back_hidden_b = back_hidden.astype(BF)
    out_grad = cross_product(mixed_output, back_hidden_b, BF)
    out_mine = plane.scatter(out_grad.reshape(layers, members, out_rows, model))
    mixed_backward = against(back_hidden_b, out_full, BF)
    group_backward = mixed_backward.reshape(rows_here, KEY_VALUE_HEADS, head_group, HEAD_SIZE)
    back_shares = jnp.einsum("qgrd,kgd->grqk", group_backward, value_all, preferred_element_type=F32)
    offset = jnp.sum(shares * back_shares, axis=-1, keepdims=True)
    back_scores = (shares * (back_shares - offset)).astype(BF)
    grad_query = jnp.einsum("grqk,kgd->qgrd", back_scores, key_all, preferred_element_type=F32)
    grad_keys = jnp.einsum("grqk,qgrd->kgd", back_scores, grouped_query, preferred_element_type=F32) * scale
    grad_values = jnp.einsum("grqk,qgrd->kgd", shares_b, group_backward, preferred_element_type=F32)
    pair_grads = jnp.concatenate(
        [grad_keys.reshape(span, key_width), grad_values.reshape(span, key_width)], axis=1
    )
    if contexts == 2:
        later = lax.ppermute(pair_grads[:rows_here], "ctx", [(1, 0)])
        pair_mine = jnp.where(first, pair_grads[:rows_here] + later, pair_grads[rows_here:])
    else:
        pair_mine = lax.psum_scatter(pair_grads, "ctx", scatter_dimension=0, tiled=True)
    back_query_rot = reverse_rotation(
        grad_query.reshape(rows_here, QUERY_HEADS, HEAD_SIZE) * scale, cosine_table, sine_table
    )
    query_gain_grad = jnp.sum(back_query_rot * query_normed, axis=(0, 1))
    grad_query_raw = rms_back(back_query_rot * query_scale, query_normed, query_inverse)
    back_key_rot = reverse_rotation(
        pair_mine[:, :key_width].reshape(rows_here, KEY_VALUE_HEADS, HEAD_SIZE), cosine_table, sine_table
    )
    key_gain_grad = jnp.sum(back_key_rot * key_normed, axis=(0, 1))
    grad_key_raw = rms_back(back_key_rot * key_scale, key_normed, key_inverse)
    grad_joint = jnp.concatenate(
        [
            grad_query_raw.reshape(rows_here, query_width),
            grad_key_raw.reshape(rows_here, key_width),
            pair_mine[:, key_width:],
            jnp.zeros((rows_here, members * joint_width - joint_columns), F32),
        ],
        axis=1,
    ).astype(BF)
    grad_joint = jnp.swapaxes(grad_joint.reshape(rows_here, members, joint_width), 0, 1)
    grad_columns = plane.from_ranks(plane.exchange(grad_joint.reshape(members * rows_here, joint_width)))
    joint_grad = cross_product(entry_one_all, grad_columns, BF).reshape(layers, -1, joint_width)
    back_entry_one = plane.scatter_rows(against(grad_columns, joint_part))
    first_grad = jnp.sum(back_entry_one * normed_one, axis=0)
    input_gradient = back_hidden + rms_back(back_entry_one * gain_one, normed_one, inverse_one)

    small = plane.total(jnp.concatenate([first_grad, second_grad, query_gain_grad, key_gain_grad]))
    out_owned = plane.layers_scatter(out_mine).astype(BF)
    joint_owned = plane.layers_scatter(joint_grad).astype(BF)
    if cube:
        contract_gradient = unit_rows_merge(plane.gather_pair(contract_owned), at_place)
        half = unit_merge(plane.gather_pair(gate_owned), at_place, 0, None)
        out_gradient = rows_merge(plane.gather_pair(out_owned), at_place)
        joint_gradient = joint_merge(plane.gather_pair(joint_owned), at_place, joint_columns)
        expand_gradient = unit_merge(plane.gather_pair(up_owned), at_place, 1, half)
    else:
        every = lambda v: lax.all_gather(v, PLANE, axis=0, tiled=False)
        contract_gradient = every(contract_owned).reshape(members * units, model).astype(F32)
        both = jnp.concatenate([every(gate_owned), every(up_owned)], axis=2)
        both = both.reshape(members, -1, 2 * layers, units).transpose(1, 2, 0, 3)
        expand_gradient = both.reshape(-1, 2 * layers * members * units).astype(F32)
        out_gradient = every(out_owned).reshape(members * out_rows, model).astype(F32)
        joint_gradient = jnp.moveaxis(every(joint_owned), 0, 1).reshape(joint_rows, -1)[:, :joint_columns].astype(F32)
    owned, at = [], 0
    for size in sizes:
        owned.append(lax.dynamic_slice_in_dim(small, at + plane.layer * size, size))
        at += size * layers
    return (
        layer_output[None],
        input_gradient[None],
        owned[0],
        joint_gradient,
        owned[2],
        owned[3],
        out_gradient,
        owned[1],
        expand_gradient,
        contract_gradient,
    )


def solution(mesh):
    return jax.shard_map(
        shards,
        mesh=mesh,
        in_specs=(
            P(("fsdp", "rep"), "ctx", None),
            P(("fsdp", "rep"), "ctx", None),
            P(("fsdp", "rep")),
            P("fsdp"),
            P("fsdp", None),
            P("fsdp"),
            P("fsdp"),
            P("fsdp", None),
            P("fsdp"),
            P("fsdp", None),
            P("fsdp", None),
        ),
        out_specs=(
            P(("fsdp", "rep"), "ctx", None),
            P(("fsdp", "rep"), "ctx", None),
            P("fsdp"),
            P("fsdp", None),
            P("fsdp"),
            P("fsdp"),
            P("fsdp", None),
            P("fsdp"),
            P("fsdp", None),
            P("fsdp", None),
        ),
        check_vma=False,
    )
```

time: 679 us -> 705 us (1.038)
  Pallas kernels: 21.5 us -> 83.9 us
  blocking collectives: 43.2 us -> 0 us
  starting transfers between devices: 79.7 us -> 109 us
  local copies, waits for them, and re-layouts: 114 us -> 99.9 us
  other arithmetic: 46.7 us -> 57.1 us
  waiting for transfers between devices: 272 us -> 262 us
    pallas_call x2 -> x9, Pallas kernels: 21.5 us -> 83.9 us  [call(): pl.pallas_call(body, out_shape=out_shape, grid_spec=pltpu.PrefetchScalarG...]
    dynamic_update_slice x49 -> x0, local copies, waits for them, and re-layouts: 45.5 us -> none  [place(): lax.dynamic_update_index_in_dim(total, jnp.expand_dims(part, axis), index...]
    ppermute x24 -> x27, waiting for transfers between devices: 134 us -> 90.5 us  [over_y(): return lax.ppermute(v, 'ctx', [(0, 1), (1, 0)])]
    psum x1 -> x0, blocking collectives: 43.2 us -> none  [shards(): lax.psum(jnp.concatenate([first_grad, second_grad, query_gain_grad, key_g...]
    unnamed x147 -> x221, local copies, waits for them, and re-layouts: 12.1 us -> 54.2 us
    all_gather x1, waiting for transfers between devices: 38.4 us -> 0.01 us  [shards(): contract_part = lax.all_gather(contract_share, 'fsdp', axis=0, tiled=False)]
    ppermute x15, waiting for transfers between devices: 60.9 us -> 92.5 us  [from_layers(): lax.ppermute(get(d), 'fsdp', [(i, (i + d) % z) for i in range(z)])]
    slice x27 -> x38, local copies, waits for them, and re-layouts: 2.73 us -> 20.5 us  [the longest x9 5.15 us: gather_pair(): far_a = self.over_y(from_x[:half])]
  transfers between devices with their start and end apart: 81 -> 92, of which waited for: 41 -> 38; matrix products, arithmetic and copies ran while one was open for 30% -> 27% of each run, Pallas kernels for 1% -> 11%
where the time goes in v3:
time: 705 us; the launch traced here: 696 us
  waiting for transfers between devices  262 us (37%)
  starting transfers between devices  109 us (15%)
  local copies, waits for them, and re-layouts  99.9 us (14%)
  Pallas kernels  83.9 us (12%)
  matrix products  68 us (10%)
  other arithmetic  57.1 us (8%)
  between operations  16.5 us (2%)
    ppermute x15, waiting for transfers between devices, from_layers(): lax.ppermute(get(d), 'fsdp', [(i, (i + d) % z) for i in range(z)])  92.5 us
    ppermute x27, waiting for transfers between devices, over_y(): return lax.ppermute(v, 'ctx', [(0, 1), (1, 0)])  90.5 us
    pallas_call x9, Pallas kernels, call(): pl.pallas_call(body, out_shape=out_shape, grid_spec=pltpu.PrefetchScalarG...  83.9 us
    dot_general x13, matrix products, dot(): lax.dot_general(left, right, (dims, ((), ())), preferred_element_type=F32)  58.4 us
    unnamed x221, local copies, waits for them, and re-layouts  54.2 us
    ppermute x27, waiting for transfers between devices, over_x(): return lax.ppermute(v, 'rep', [(i, i ^ 2) for i in range(4)])  53.6 us
    ppermute x27, starting transfers between devices, over_y(): return lax.ppermute(v, 'ctx', [(0, 1), (1, 0)])  36.1 us
    ppermute x15, starting transfers between devices, from_layers(): lax.ppermute(get(d), 'fsdp', [(i, (i + d) % z) for i in range(z)])  29.9 us
  transfers between devices with their start and end apart: 92, of which 38 were waited for; matrix products, arithmetic and copies ran while one was open for 27% of the time, Pallas kernels for 11%

profile of v3, /device:TPU:0, one launch (start us, length us, event | category | flops | bytes accessed | tf_op | source)
XLA Modules:
  0.0 696.0 jit_solution(137592603034002372)
XLA Ops:
  14.5 5.1 collective-permute-start.7
  23.7 4.7 unit_columns.1
  32.9 28.6 %collective-permute-done.6 = bf16[520,256]{1,0:T(8,128)(2,1)} collective-permute-done((bf16[520,256]{1,0:T(8,128)(2,1)S(1)}, bf16[520,256]{1,0:T(8,128)(2,1)}, u32[]{:S(2)}, u32[]{:S(2)}) %collective-permute-start.6) | collective-permute-done | bytes 266272 | tf_op jit(solution)/shard_map/ppermute | solution.py:169
  63.8 4.0 layers_order.1
  69.9 8.7 %collective-permute-start.9 = (bf16[40,2048]{1,0:T(8,128)(2,1)S(1)}, bf16[40,2048]{1,0:T(8,128)(2,1)S(1)}, u32[]{:S(2)}, u32[]{:S(2)}) collective-permute-start(bf16[40,2048]{1,0:T(8,128)(2,1)S(1)} %constant_dynamic-slice_fusion.4), channel_id=1, source_target_pairs={{0,4},{4,8},{8,12},{12,0},{1,5},{5,9},{9,13},{13,1},{2,6},{6,10},{... | collective-permute-start | bytes 491528 | tf_op jit(solution)/shard_map/ppermute | solution.py:169
  78.6 4.0 collective-permute-start.10
  118.5 7.6 %collective-permute-done.13 = bf16[4,40,2048]{2,1,0:T(8,128)(2,1)S(1)} collective-permute-done((bf16[4,40,2048]{2,1,0:T(8,128)(2,1)S(1)}, bf16[4,40,2048]{2,1,0:T(8,128)(2,1)S(1)}, u32[]{:S(2)}, u32[]{:S(2)}) %collective-permute-start.13) | collective-permute-done | bytes 655392 | tf_op jit(solution)/shard_map/ppermute | solution.py:89
  135.5 3.6 all-to-all-start
  144.7 9.7 %all-to-all-done = f32[8,128,256]{2,1,0:T(8,128)S(1)} async-done(((f32[8,128,256]{2,1,0:T(8,128)}), f32[8,128,256]{2,1,0:T(8,128)S(1)}, u32[]{:S(2)}, u32[]{:S(2)}) %all-to-all-start) | async-done | bytes 1048608 | tf_op jit(solution)/shard_map/all_to_all | solution.py:155
  160.5 3.6 fusion.103
  166.3 19.1 %pair_order.1 = bf16[4,8,40,2048]{3,2,1,0:T(8,128)(2,1)} custom-call(s32[2]{0:T(128)} %pad_add_fusion.place_ref, bf16[4,4,40,2048]{3,2,1,0:T(8,128)(2,1)} %bitcast.295, bf16[4,4,40,2048]{3,2,1,0:T(8,128)(2,1)} %bitcast.37.other_ref), custom_call_target="tpu_custom_call" | custom-call | bytes 10485760 | tf_op jit(solution)/shard_map/pair_order/pallas_call | solution.py:184
  185.5 3.5 multiply_reduce_fusion.2
  198.0 4.4 collective-permute-done.17
  212.8 4.0 pad_maximum_fusion.2
  221.1 4.6 pad_maximum_fusion.1
  225.6 9.0 %fusion.105 = f32[1024,1280]{1,0:T(8,128)S(1)} fusion(bf16[1024,2048]{1,0:T(8,128)(2,1)} %bitcast.289, bf16[2048,1280]{1,0:T(8,128)(2,1)} %all-gather.4.cloned.1.call-done), kind=kOutput, calls=%fused_computation.307 | convolution fusion | flops 5368709120 | bytes 14680064 | tf_op jit(solution)/shard_map/dot_general | solution.py:59
  234.7 5.8 multiply_convert_fusion.1
  245.8 7.6 %convolution_convert_fusion.3 = bf16[2048,640]{1,0:T(8,128)(2,1)} fusion(bf16[1024,2048]{1,0:T(8,128)(2,1)} %bitcast.290, bf16[1024,640]{1,0:T(8,128)(2,1)} %get-tuple-element.34), kind=kOutput, calls=%fused_computation.16 | convolution fusion | flops 2685665280 | bytes 8126464 | tf_op jit(solution)/shard_map/dot_general | solution.py:59
  253.4 8.4 %fusion.4 = f32[1024,2048]{1,0:T(8,128)S(1)} fusion(bf16[2048,1280]{1,0:T(8,128)(2,1)} %all-gather.4.cloned.1.call-done, bf16[1024,640]{1,0:T(8,128)(2,1)} %get-tuple-element.34, bf16[1024,640]{1,0:T(8,128)(2,1)} %get-tuple-element.33), kind=kOutput, calls=%fused_computation.18 | convolution fusion | flops 5373952000 | bytes 16252928 | tf_op jit(solution)/shard_map/dot_general | solution.py:59
  266.3 3.4 fusion.14
  277.9 7.7 %convolution_convert_fusion.2 = bf16[2048,640]{1,0:T(8,128)(2,1)} fusion(bf16[1024,2048]{1,0:T(8,128)(2,1)} %bitcast.291, bf16[1024,640]{1,0:T(8,128)(2,1)} %get-tuple-element.33), kind=kOutput, calls=%fused_computation.15 | convolution fusion | flops 2685665280 | bytes 8126464 | tf_op jit(solution)/shard_map/dot_general | solution.py:59
  301.9 3.5 collective-permute-done.25
  307.6 10.3 %collective-permute-done.36 = bf16[128,2048]{1,0:T(8,128)(2,1)S(1)} collective-permute-done((bf16[128,2048]{1,0:T(8,128)(2,1)S(1)}, bf16[128,2048]{1,0:T(8,128)(2,1)S(1)}, u32[]{:S(2)}, u32[]{:S(2)}) %collective-permute-start.36) | collective-permute-done | bytes 524320 | tf_op jit(solution)/shard_map/ppermute | solution.py:89
  320.3 7.5 %collective-permute-done.26 = bf16[128,2048]{1,0:T(8,128)(2,1)S(1)} collective-permute-done((bf16[128,2048]{1,0:T(8,128)(2,1)S(1)}, bf16[128,2048]{1,0:T(8,128)(2,1)S(1)}, u32[]{:S(2)}, u32[]{:S(2)}) %collective-permute-start.26) | collective-permute-done | bytes 524320 | tf_op jit(solution)/shard_map/ppermute | solution.py:89
  340.1 8.1 %collective-permute-done.37 = f32[128,640]{0,1:T(8,128)S(1)} collective-permute-done((f32[128,640]{0,1:T(8,128)S(1)}, f32[128,640]{0,1:T(8,128)S(1)}, u32[]{:S(2)}, u32[]{:S(2)}) %collective-permute-start.37) | collective-permute-done | bytes 327712 | tf_op jit(solution)/shard_map/ppermute | solution.py:644
  350.3 3.5 all-to-all-start.1
  359.8 3.7 all-to-all-done.1
  364.0 3.6 convolution_convert_fusion.4
  374.8 12.6 %collective-permute-done.51 = bf16[512,256]{1,0:T(8,128)(2,1)} collective-permute-done((bf16[512,256]{1,0:T(8,128)(2,1)}, bf16[512,256]{1,0:T(8,128)(2,1)}, u32[]{:S(2)}, u32[]{:S(2)}) %collective-permute-start.51) | collective-permute-done | bytes 262176 | tf_op jit(solution)/shard_map/ppermute | solution.py:169
  387.4 34.2 %collective-permute-done.50 = bf16[512,256]{1,0:T(8,128)(2,1)} collective-permute-done((bf16[512,256]{1,0:T(8,128)(2,1)}, bf16[512,256]{1,0:T(8,128)(2,1)}, u32[]{:S(2)}, u32[]{:S(2)}) %collective-permute-start.50) | collective-permute-done | bytes 262176 | tf_op jit(solution)/shard_map/ppermute | solution.py:169
  451.2 9.2 %collective-permute-done.58 = bf16[2,40,2048]{2,1,0:T(8,128)(2,1)S(1)} collective-permute-done((bf16[2,40,2048]{2,1,0:T(8,128)(2,1)S(1)}, bf16[2,40,2048]{2,1,0:T(8,128)(2,1)S(1)}, u32[]{:S(2)}, u32[]{:S(2)}) %collective-permute-start.58) | collective-permute-done | bytes 327712 | tf_op jit(solution)/shard_map/ppermute | solution.py:89
  461.3 12.0 %collective-permute-done.60 = bf16[2,40,2048]{2,1,0:T(8,128)(2,1)S(1)} collective-permute-done((bf16[2,40,2048]{2,1,0:T(8,128)(2,1)S(1)}, bf16[2,40,2048]{2,1,0:T(8,128)(2,1)S(1)}, u32[]{:S(2)}, u32[]{:S(2)}) %collective-permute-start.60) | collective-permute-done | bytes 327712 | tf_op jit(solution)/shard_map/ppermute | solution.py:83
  480.9 6.1 collective-permute-done.75
  495.2 9.8 %collective-permute-done.81 = bf16[160,2048]{1,0:T(8,128)(2,1)S(1)} collective-permute-done((bf16[160,2048]{1,0:T(8,128)(2,1)S(1)}, bf16[160,2048]{1,0:T(8,128)(2,1)S(1)}, u32[]{:S(2)}, u32[]{:S(2)}) %collective-permute-start.81) | collective-permute-done | bytes 655392 | tf_op jit(solution)/shard_map/ppermute | solution.py:89
  508.3 5.2 collective-permute-done.39
  514.8 19.8 %collective-permute-done.72 = bf16[256,640]{1,0:T(8,128)(2,1)S(1)} collective-permute-done((bf16[256,640]{1,0:T(8,128)(2,1)S(1)}, bf16[256,640]{1,0:T(8,128)(2,1)S(1)}, u32[]{:S(2)}, u32[]{:S(2)}) %collective-permute-start.72) | collective-permute-done | bytes 327712 | tf_op jit(solution)/shard_map/ppermute | solution.py:89
  548.6 16.1 %collective-permute-done.83 = bf16[80,2048]{1,0:T(8,128)(2,1)S(1)} collective-permute-done((bf16[80,2048]{1,0:T(8,128)(2,1)S(1)}, bf16[80,2048]{1,0:T(8,128)(2,1)S(1)}, u32[]{:S(2)}, u32[]{:S(2)}) %collective-permute-start.83) | collective-permute-done | bytes 327712 | tf_op jit(solution)/shard_map/ppermute | solution.py:83
  568.5 5.3 collective-permute-done.42
  586.7 6.4 collective-permute-done.63
  593.2 7.6 %collective-permute-done.62 = bf16[40,2048]{1,0:T(8,128)(2,1)S(1)} collective-permute-done((bf16[40,2048]{1,0:T(8,128)(2,1)S(1)}, bf16[40,2048]{1,0:T(8,128)(2,1)S(1)}, u32[]{:S(2)}, u32[]{:S(2)}) %collective-permute-start.62) | collective-permute-done | bytes 163872 | tf_op jit(solution)/shard_map/ppermute | solution.py:169
  606.1 3.7 collective-permute-done.65
  611.6 4.1 collective-permute-done.66
  621.7 4.9 joint_merge.1
  627.9 3.8 concatenate.160
  640.4 6.5 rows_merge.1
  646.9 9.2 %unit_merge.2.refs_0_ = f32[512,10240]{1,0:T(8,128)} custom-call(s32[2]{0:T(128)} %pad_add_fusion.place_ref, bf16[4,512,640]{2,1,0:T(8,128)(2,1)} %bitcast.107.near, bf16[4,512,640]{2,1,0:T(8,128)(2,1)} %bitcast.108.other), custom_call_target="tpu_custom_call" | custom-call | bytes 10485760 | tf_op jit(solution)/shard_map/unit_merge/pallas_call | solution.py:184
  656.1 23.8 %unit_rows_merge.1 = f32[1280,2048]{1,0:T(8,128)} custom-call(s32[2]{0:T(128)} %pad_add_fusion.place_ref, bf16[4,160,2048]{2,1,0:T(8,128)(2,1)} %bitcast.112.near_ref, bf16[4,160,2048]{2,1,0:T(8,128)(2,1)} %bitcast.113.other_ref), custom_call_target="tpu_custom_call" | custom-call | bytes 10485760 | tf_op jit(solution)/shard_map/unit_rows_merge/pallas_call | solution.py:184
  679.9 9.3 %unit_merge.3 = f32[512,10240]{1,0:T(8,128)} custom-call(s32[2]{0:T(128)} %pad_add_fusion.place_ref, bf16[4,512,640]{2,1,0:T(8,128)(2,1)} %bitcast.105.near, bf16[4,512,640]{2,1,0:T(8,128)(2,1)} %bitcast.106.other, f32[512,10240]{1,0:T(8,128)} %unit_merge.2.refs_0_), custom_call_target="tpu_custom_call", output_to_operand_aliasing={{}: (3, {})} | custom-call | bytes 52428800 | tf_op jit(solution)/shard_map/unit_merge/pallas_call | solution.py:184
  (565 shorter events, 272.4 us)
Async XLA Ops:
  7.2 209.6 %all-gather.6.cloned.1.call-start = ((), (), s32[]{:S(2)}) async-start(), calls=%async_computation.9 | async-start | bytes 3276800 | tf_op jit(solution)/shard_map/all_gather | solution.py:545
  10.4 215.3 %all-gather.4.cloned.1.call-start = ((), (), s32[]{:S(2)}) async-start(), calls=%async_computation.5 | async-start | bytes 6553600 | tf_op jit(solution)/shard_map/all_gather | solution.py:544
  14.5 17.9 %collective-permute-start.7 = (bf16[520,256]{1,0:T(8,128)(2,1)S(1)}, bf16[520,256]{1,0:T(8,128)(2,1)}, u32[]{:S(2)}, u32[]{:S(2)}) collective-permute-start(bf16[520,256]{1,0:T(8,128)(2,1)S(1)} %get-tuple-element.71), channel_id=1, source_target_pairs={{0,12},{4,0},{8,4},{12,8},{1,13},{5,1},{9,5},{13,9},{2,14},{6,2},{... | collective-permute-start | bytes 798728 | tf_op jit(solution)/shard_map/ppermute | solution.py:169
  19.6 41.9 %collective-permute-start.6 = (bf16[520,256]{1,0:T(8,128)(2,1)S(1)}, bf16[520,256]{1,0:T(8,128)(2,1)}, u32[]{:S(2)}, u32[]{:S(2)}) collective-permute-start(bf16[520,256]{1,0:T(8,128)(2,1)S(1)} %get-tuple-element.71), channel_id=1, source_target_pairs={{0,8},{4,12},{8,0},{12,4},{1,9},{5,13},{9,1},{13,5},{2,10},{6,14},... | collective-permute-start | bytes 798728 | tf_op jit(solution)/shard_map/ppermute | solution.py:169
  19.6 41.9 %collective-permute-start.5 = (bf16[520,256]{1,0:T(8,128)(2,1)S(1)}, bf16[520,256]{1,0:T(8,128)(2,1)}, u32[]{:S(2)}, u32[]{:S(2)}) collective-permute-start(bf16[520,256]{1,0:T(8,128)(2,1)S(1)} %get-tuple-element.71), channel_id=1, source_target_pairs={{0,4},{4,8},{8,12},{12,0},{1,5},{5,9},{9,13},{13,1},{2,6},{6,10},{... | collective-permute-start | bytes 798728 | tf_op jit(solution)/shard_map/ppermute | solution.py:169
  20.6 62.6 %collective-permute-start = (bf16[128,2048]{1,0:T(8,128)(2,1)S(1)}, bf16[128,2048]{1,0:T(8,128)(2,1)}, u32[]{:S(2)}, u32[]{:S(2)}) collective-permute-start(bf16[128,2048]{1,0:T(8,128)(2,1)S(1)} %bitcast.272), channel_id=1, source_target_pairs={{0,2},{1,3},{2,0},{3,1},{4,6},{5,7},{6,4},{7,5},{8,10},{9,11},{10,... | collective-permute-start | bytes 1572872 | tf_op jit(solution)/shard_map/ppermute | solution.py:83
  22.1 63.7 %collective-permute-start.1 = (bf16[128,2048]{1,0:T(8,128)(2,1)S(1)}, bf16[128,2048]{1,0:T(8,128)(2,1)}, u32[]{:S(2)}, u32[]{:S(2)}) collective-permute-start(bf16[128,2048]{1,0:T(8,128)(2,1)S(1)} %bitcast.273), channel_id=1, source_target_pairs={{0,16},{16,0},{1,17},{17,1},{2,18},{18,2},{3,19},{19,3},{4,20},{20... | collective-permute-start | bytes 1572872 | tf_op jit(solution)/shard_map/ppermute | solution.py:89
  32.4 74.0 %collective-permute-start.27 = (bf16[128,2048]{1,0:T(8,128)(2,1)S(1)}, bf16[128,2048]{1,0:T(8,128)(2,1)}, u32[]{:S(2)}, u32[]{:S(2)}) collective-permute-start(bf16[128,2048]{1,0:T(8,128)(2,1)S(1)} %fusion.44), channel_id=1, source_target_pairs={{0,2},{1,3},{2,0},{3,1},{4,6},{5,7},{6,4},{7,5},{8,10},{9,11},{10,... | collective-permute-start | bytes 1572872 | tf_op jit(solution)/shard_map/ppermute | solution.py:83
  69.9 27.4 %collective-permute-start.9 = (bf16[40,2048]{1,0:T(8,128)(2,1)S(1)}, bf16[40,2048]{1,0:T(8,128)(2,1)S(1)}, u32[]{:S(2)}, u32[]{:S(2)}) collective-permute-start(bf16[40,2048]{1,0:T(8,128)(2,1)S(1)} %constant_dynamic-slice_fusion.4), channel_id=1, source_target_pairs={{0,4},{4,8},{8,12},{12,0},{1,5},{5,9},{9,13},{13,1},{2,6},{6,10},{... | collective-permute-start | bytes 491528 | tf_op jit(solution)/shard_map/ppermute | solution.py:169
  78.6 19.2 %collective-permute-start.10 = (bf16[40,2048]{1,0:T(8,128)(2,1)S(1)}, bf16[40,2048]{1,0:T(8,128)(2,1)S(1)}, u32[]{:S(2)}, u32[]{:S(2)}) collective-permute-start(bf16[40,2048]{1,0:T(8,128)(2,1)S(1)} %constant_dynamic-slice_fusion.4), channel_id=1, source_target_pairs={{0,8},{4,12},{8,0},{12,4},{1,9},{5,13},{9,1},{13,5},{2,10},{6,14},... | collective-permute-start | bytes 491528 | tf_op jit(solution)/shard_map/ppermute | solution.py:169
  96.4 31.0 %collective-permute-start.4 = (bf16[512,2048]{1,0:T(8,128)(2,1)}, bf16[512,2048]{1,0:T(8,128)(2,1)}, u32[]{:S(2)}, u32[]{:S(2)}) collective-permute-start(bf16[512,2048]{1,0:T(8,128)(2,1)} %constant_dynamic-update-slice_fusion), channel_id=1, source_target_pairs={{0,1},{1,0},{2,3},{3,2},{4,5},{5,4},{6,7},{7,6},{8,9},{9,8},{10,11... | collective-permute-start | bytes 6291464 | tf_op jit(solution)/shard_map/ppermute | solution.py:86
  100.2 25.9 %collective-permute-start.13 = (bf16[4,40,2048]{2,1,0:T(8,128)(2,1)S(1)}, bf16[4,40,2048]{2,1,0:T(8,128)(2,1)S(1)}, u32[]{:S(2)}, u32[]{:S(2)}) collective-permute-start(bf16[4,40,2048]{2,1,0:T(8,128)(2,1)S(1)} %pad_maximum_fusion.8), channel_id=1, source_target_pairs={{0,16},{16,0},{1,17},{17,1},{2,18},{18,2},{3,19},{19,3},{4,20},{20... | collective-permute-start | bytes 1966088 | tf_op jit(solution)/shard_map/ppermute | solution.py:89
  108.0 86.6 %collective-permute-start.29 = (bf16[64,2048]{1,0:T(8,128)(2,1)}, bf16[64,2048]{1,0:T(8,128)(2,1)}, u32[]{:S(2)}, u32[]{:S(2)}) collective-permute-start(bf16[64,2048]{1,0:T(8,128)(2,1)} %slice.470), channel_id=1, source_target_pairs={{0,16},{16,0},{1,17},{17,1},{2,18},{18,2},{3,19},{19,3},{4,20},{20... | collective-permute-start | bytes 786440 | tf_op jit(solution)/shard_map/ppermute | solution.py:89
  112.8 83.5 %collective-permute-start.30 = (bf16[64,2048]{1,0:T(8,128)(2,1)}, bf16[64,2048]{1,0:T(8,128)(2,1)}, u32[]{:S(2)}, u32[]{:S(2)}) collective-permute-start(bf16[64,2048]{1,0:T(8,128)(2,1)} %slice.471), channel_id=1, source_target_pairs={{0,2},{1,3},{2,0},{3,1},{4,6},{5,7},{6,4},{7,5},{8,10},{9,11},{10,... | collective-permute-start | bytes 786440 | tf_op jit(solution)/shard_map/ppermute | solution.py:83
  116.4 24.5 %collective-permute-start.14 = (bf16[2,40,2048]{2,1,0:T(8,128)(2,1)}, bf16[2,40,2048]{2,1,0:T(8,128)(2,1)}, u32[]{:S(2)}, u32[]{:S(2)}) collective-permute-start(bf16[2,40,2048]{2,1,0:T(8,128)(2,1)} %slice.446), channel_id=1, source_target_pairs={{0,16},{16,0},{1,17},{17,1},{2,18},{18,2},{3,19},{19,3},{4,20},{20... | collective-permute-start | bytes 983048 | tf_op jit(solution)/shard_map/ppermute | solution.py:89
  135.5 18.9 %all-to-all-start = ((f32[8,128,256]{2,1,0:T(8,128)}), f32[8,128,256]{2,1,0:T(8,128)S(1)}, u32[]{:S(2)}, u32[]{:S(2)}) async-start(f32[8,128,256]{2,1,0:T(8,128)} %bitcast.14), calls=%async_computation | async-start | bytes 2097152 | tf_op jit(solution)/shard_map/all_to_all | solution.py:155
  139.1 295.5 %reduce-scatter.8.cloned.1.call-start = ((), (), s32[]{:S(2)}) async-start(), calls=%async_computation.8 | async-start | bytes 3276800 | tf_op jit(solution)/shard_map/reduce_scatter | solution.py:613
  144.4 22.0 %collective-permute-start.16 = (bf16[16,40,2048]{2,1,0:T(8,128)(2,1)}, bf16[16,40,2048]{2,1,0:T(8,128)(2,1)}, u32[]{:S(2)}, u32[]{:S(2)}) collective-permute-start(bf16[16,40,2048]{2,1,0:T(8,128)(2,1)} %constant_dynamic-update-slice_fusion.5), channel_id=1, source_target_pairs={{0,1},{1,0},{2,3},{3,2},{4,5},{5,4},{6,7},{7,6},{8,9},{9,8},{10,11... | collective-permute-start | bytes 7864328 | tf_op jit(solution)/shard_map/ppermute | solution.py:86
  245.5 190.0 %reduce-scatter.4.cloned.1.call-start = ((), (), s32[]{:S(2)}) async-start(), calls=%async_computation.6 | async-start | bytes 3276800 | tf_op jit(solution)/shard_map/reduce_scatter | solution.py:622
  253.4 186.4 %reduce-scatter.6.cloned.1.call-start = ((), (), s32[]{:S(2)}) async-start(), calls=%async_computation.7 | async-start | bytes 3276800 | tf_op jit(solution)/shard_map/reduce_scatter | solution.py:621
  263.5 22.1 %collective-permute-start.32 = (bf16[512,2048]{1,0:T(8,128)(2,1)}, bf16[512,2048]{1,0:T(8,128)(2,1)}, u32[]{:S(2)}, u32[]{:S(2)}) collective-permute-start(bf16[512,2048]{1,0:T(8,128)(2,1)} %slice.653), channel_id=1, source_target_pairs={{0,1},{1,0},{2,3},{3,2},{4,5},{5,4},{6,7},{7,6},{8,9},{9,8},{10,11... | collective-permute-start | bytes 6291464 | tf_op jit(solution)/shard_map/ppermute | solution.py:86
  299.9 18.0 %collective-permute-start.36 = (bf16[128,2048]{1,0:T(8,128)(2,1)S(1)}, bf16[128,2048]{1,0:T(8,128)(2,1)S(1)}, u32[]{:S(2)}, u32[]{:S(2)}) collective-permute-start(bf16[128,2048]{1,0:T(8,128)(2,1)S(1)} %pad_maximum_fusion.16), channel_id=1, source_target_pairs={{0,16},{16,0},{1,17},{17,1},{2,18},{18,2},{3,19},{19,3},{4,20},{20... | collective-permute-start | bytes 1572872 | tf_op jit(solution)/shard_map/ppermute | solution.py:89
  305.6 22.2 %collective-permute-start.26 = (bf16[128,2048]{1,0:T(8,128)(2,1)S(1)}, bf16[128,2048]{1,0:T(8,128)(2,1)S(1)}, u32[]{:S(2)}, u32[]{:S(2)}) collective-permute-start(bf16[128,2048]{1,0:T(8,128)(2,1)S(1)} %pad_maximum_fusion.14), channel_id=1, source_target_pairs={{0,16},{16,0},{1,17},{17,1},{2,18},{18,2},{3,19},{19,3},{4,20},{20... | collective-permute-start | bytes 1572872 | tf_op jit(solution)/shard_map/ppermute | solution.py:89
  307.5 20.3 %collective-permute-start.24 = (bf16[128,2048]{1,0:T(8,128)(2,1)S(1)}, bf16[128,2048]{1,0:T(8,128)(2,1)S(1)}, u32[]{:S(2)}, u32[]{:S(2)}) collective-permute-start(bf16[128,2048]{1,0:T(8,128)(2,1)S(1)} %pad_maximum_fusion.13), channel_id=1, source_target_pairs={{0,2},{1,3},{2,0},{3,1},{4,6},{5,7},{6,4},{7,5},{8,10},{9,11},{10,... | collective-permute-start | bytes 1572872 | tf_op jit(solution)/shard_map/ppermute | solution.py:83
  359.4 83.4 %collective-permute-start.57 = (bf16[4,2,2,40,2048]{4,3,0,2,1:T(8,128)(2,1)}, bf16[4,2,2,40,2048]{4,3,0,2,1:T(8,128)(2,1)}, u32[]{:S(2)}, u32[]{:S(2)}) collective-permute-start(bf16[4,2,2,40,2048]{4,3,0,2,1:T(8,128)(2,1)} %bitcast.262), channel_id=1, source_target_pairs={{0,1},{1,0},{2,3},{3,2},{4,5},{5,4},{6,7},{7,6},{8,9},{9,8},{10,11... | collective-permute-start | bytes 7864328 | tf_op jit(solution)/shard_map/ppermute | solution.py:86
  369.5 17.8 %collective-permute-start.51 = (bf16[512,256]{1,0:T(8,128)(2,1)}, bf16[512,256]{1,0:T(8,128)(2,1)}, u32[]{:S(2)}, u32[]{:S(2)}) collective-permute-start(bf16[512,256]{1,0:T(8,128)(2,1)} %get-tuple-element.52), channel_id=1, source_target_pairs={{0,12},{4,0},{8,4},{12,8},{1,13},{5,1},{9,5},{13,9},{2,14},{6,2},{... | collective-permute-start | bytes 786440 | tf_op jit(solution)/shard_map/ppermute | solution.py:169
  370.8 50.7 %collective-permute-start.50 = (bf16[512,256]{1,0:T(8,128)(2,1)}, bf16[512,256]{1,0:T(8,128)(2,1)}, u32[]{:S(2)}, u32[]{:S(2)}) collective-permute-start(bf16[512,256]{1,0:T(8,128)(2,1)} %get-tuple-element.53), channel_id=1, source_target_pairs={{0,8},{4,12},{8,0},{12,4},{1,9},{5,13},{9,1},{13,5},{2,10},{6,14},... | collective-permute-start | bytes 786440 | tf_op jit(solution)/shard_map/ppermute | solution.py:169
  370.8 50.7 %collective-permute-start.49 = (bf16[512,256]{1,0:T(8,128)(2,1)}, bf16[512,256]{1,0:T(8,128)(2,1)}, u32[]{:S(2)}, u32[]{:S(2)}) collective-permute-start(bf16[512,256]{1,0:T(8,128)(2,1)} %get-tuple-element.51), channel_id=1, source_target_pairs={{0,4},{4,8},{8,12},{12,0},{1,5},{5,9},{9,13},{13,1},{2,6},{6,10},{... | collective-permute-start | bytes 786440 | tf_op jit(solution)/shard_map/ppermute | solution.py:169
  434.6 54.3 %collective-permute-start.80 = (bf16[160,2048]{1,0:T(8,128)(2,1)}, bf16[160,2048]{1,0:T(8,128)(2,1)S(1)}, u32[]{:S(2)}, u32[]{:S(2)}) collective-permute-start(bf16[160,2048]{1,0:T(8,128)(2,1)} %bitcast.328), channel_id=1, source_target_pairs={{0,2},{1,3},{2,0},{3,1},{4,6},{5,7},{6,4},{7,5},{8,10},{9,11},{10,... | collective-permute-start | bytes 1966088 | tf_op jit(solution)/shard_map/ppermute | solution.py:83
  435.5 39.3 %collective-permute-start.70 = (bf16[512,640]{1,0:T(8,128)(2,1)}, bf16[512,640]{1,0:T(8,128)(2,1)}, u32[]{:S(2)}, u32[]{:S(2)}) collective-permute-start(bf16[512,640]{1,0:T(8,128)(2,1)} %reduce-scatter.4.cloned.1.call-done), channel_id=1, source_target_pairs={{0,2},{1,3},{2,0},{3,1},{4,6},{5,7},{6,4},{7,5},{8,10},{9,11},{10,... | collective-permute-start | bytes 1966088 | tf_op jit(solution)/shard_map/ppermute | solution.py:83
  436.6 41.2 %collective-permute-start.71 = (bf16[512,640]{1,0:T(8,128)(2,1)}, bf16[512,640]{1,0:T(8,128)(2,1)}, u32[]{:S(2)}, u32[]{:S(2)}) collective-permute-start(bf16[512,640]{1,0:T(8,128)(2,1)} %reduce-scatter.4.cloned.1.call-done), channel_id=1, source_target_pairs={{0,16},{16,0},{1,17},{17,1},{2,18},{18,2},{3,19},{19,3},{4,20},{20... | collective-permute-start | bytes 1966088 | tf_op jit(solution)/shard_map/ppermute | solution.py:89
  447.3 26.0 %collective-permute-start.60 = (bf16[2,40,2048]{2,1,0:T(8,128)(2,1)S(1)}, bf16[2,40,2048]{2,1,0:T(8,128)(2,1)S(1)}, u32[]{:S(2)}, u32[]{:S(2)}) collective-permute-start(bf16[2,40,2048]{2,1,0:T(8,128)(2,1)S(1)} %get-tuple-element.59), channel_id=1, source_target_pairs={{0,2},{1,3},{2,0},{3,1},{4,6},{5,7},{6,4},{7,5},{8,10},{9,11},{10,... | collective-permute-start | bytes 983048 | tf_op jit(solution)/shard_map/ppermute | solution.py:83
  460.4 26.6 %collective-permute-start.75 = (bf16[512,640]{1,0:T(8,128)(2,1)S(1)}, bf16[512,640]{1,0:T(8,128)(2,1)S(1)}, u32[]{:S(2)}, u32[]{:S(2)}) collective-permute-start(bf16[512,640]{1,0:T(8,128)(2,1)S(1)} %copy-done.38), channel_id=1, source_target_pairs={{0,2},{1,3},{2,0},{3,1},{4,6},{5,7},{6,4},{7,5},{8,10},{9,11},{10,... | collective-permute-start | bytes 1966088 | tf_op jit(solution)/shard_map/ppermute | solution.py:83
  474.8 30.2 %collective-permute-start.81 = (bf16[160,2048]{1,0:T(8,128)(2,1)S(1)}, bf16[160,2048]{1,0:T(8,128)(2,1)S(1)}, u32[]{:S(2)}, u32[]{:S(2)}) collective-permute-start(bf16[160,2048]{1,0:T(8,128)(2,1)S(1)} %bitcast.329), channel_id=1, source_target_pairs={{0,16},{16,0},{1,17},{17,1},{2,18},{18,2},{3,19},{19,3},{4,20},{20... | collective-permute-start | bytes 1966088 | tf_op jit(solution)/shard_map/ppermute | solution.py:89
  477.8 100.2 %collective-permute-start.54 = (bf16[256,256]{1,0:T(8,128)(2,1)}, bf16[256,256]{1,0:T(8,128)(2,1)}, u32[]{:S(2)}, u32[]{:S(2)}) collective-permute-start(bf16[256,256]{1,0:T(8,128)(2,1)} %slice.510), channel_id=1, source_target_pairs={{0,16},{16,0},{1,17},{17,1},{2,18},{18,2},{3,19},{19,3},{4,20},{20... | collective-permute-start | bytes 393224 | tf_op jit(solution)/shard_map/ppermute | solution.py:89
  487.0 20.1 %collective-permute-start.41 = (bf16[64,2048]{1,0:T(8,128)(2,1)S(1)}, bf16[64,2048]{1,0:T(8,128)(2,1)S(1)}, u32[]{:S(2)}, u32[]{:S(2)}) collective-permute-start(bf16[64,2048]{1,0:T(8,128)(2,1)S(1)} %get-tuple-element.63), channel_id=1, source_target_pairs={{0,2},{1,3},{2,0},{3,1},{4,6},{5,7},{6,4},{7,5},{8,10},{9,11},{10,... | collective-permute-start | bytes 786440 | tf_op jit(solution)/shard_map/ppermute | solution.py:83
  488.9 24.6 %collective-permute-start.39 = (bf16[64,2048]{1,0:T(8,128)(2,1)S(1)}, bf16[64,2048]{1,0:T(8,128)(2,1)S(1)}, u32[]{:S(2)}, u32[]{:S(2)}) collective-permute-start(bf16[64,2048]{1,0:T(8,128)(2,1)S(1)} %get-tuple-element.62), channel_id=1, source_target_pairs={{0,16},{16,0},{1,17},{17,1},{2,18},{18,2},{3,19},{19,3},{4,20},{20... | collective-permute-start | bytes 786440 | tf_op jit(solution)/shard_map/ppermute | solution.py:89
  491.0 75.8 %collective-permute-start.61 = (bf16[4,40,2048]{2,1,0:T(8,128)(2,1)S(1)}, bf16[4,40,2048]{2,1,0:T(8,128)(2,1)S(1)}, u32[]{:S(2)}, u32[]{:S(2)}) collective-permute-start(bf16[4,40,2048]{2,1,0:T(8,128)(2,1)S(1)} %pad_maximum_fusion.12), channel_id=1, source_target_pairs={{0,16},{16,0},{1,17},{17,1},{2,18},{18,2},{3,19},{19,3},{4,20},{20... | collective-permute-start | bytes 1966088 | tf_op jit(solution)/shard_map/ppermute | solution.py:89
  505.1 29.5 %collective-permute-start.72 = (bf16[256,640]{1,0:T(8,128)(2,1)S(1)}, bf16[256,640]{1,0:T(8,128)(2,1)S(1)}, u32[]{:S(2)}, u32[]{:S(2)}) collective-permute-start(bf16[256,640]{1,0:T(8,128)(2,1)S(1)} %slice.516), channel_id=1, source_target_pairs={{0,16},{16,0},{1,17},{17,1},{2,18},{18,2},{3,19},{19,3},{4,20},{20... | collective-permute-start | bytes 983048 | tf_op jit(solution)/shard_map/ppermute | solution.py:89
  507.2 29.1 %collective-permute-start.73 = (bf16[256,640]{1,0:T(8,128)(2,1)S(1)}, bf16[256,640]{1,0:T(8,128)(2,1)S(1)}, u32[]{:S(2)}, u32[]{:S(2)}) collective-permute-start(bf16[256,640]{1,0:T(8,128)(2,1)S(1)} %slice.517), channel_id=1, source_target_pairs={{0,2},{1,3},{2,0},{3,1},{4,6},{5,7},{6,4},{7,5},{8,10},{9,11},{10,... | collective-permute-start | bytes 983048 | tf_op jit(solution)/shard_map/ppermute | solution.py:83
  513.5 28.1 %collective-permute-start.77 = (bf16[256,640]{1,0:T(8,128)(2,1)S(1)}, bf16[256,640]{1,0:T(8,128)(2,1)S(1)}, u32[]{:S(2)}, u32[]{:S(2)}) collective-permute-start(bf16[256,640]{1,0:T(8,128)(2,1)S(1)} %slice.518), channel_id=1, source_target_pairs={{0,16},{16,0},{1,17},{17,1},{2,18},{18,2},{3,19},{19,3},{4,20},{20... | collective-permute-start | bytes 983048 | tf_op jit(solution)/shard_map/ppermute | solution.py:89
  541.6 26.5 %collective-permute-start.59 = (bf16[4,40,2048]{2,1,0:T(8,128)(2,1)S(1)}, bf16[4,40,2048]{2,1,0:T(8,128)(2,1)S(1)}, u32[]{:S(2)}, u32[]{:S(2)}) collective-permute-start(bf16[4,40,2048]{2,1,0:T(8,128)(2,1)S(1)} %pad_maximum_fusion.11), channel_id=1, source_target_pairs={{0,2},{1,3},{2,0},{3,1},{4,6},{5,7},{6,4},{7,5},{8,10},{9,11},{10,... | collective-permute-start | bytes 1966088 | tf_op jit(solution)/shard_map/ppermute | solution.py:83
  543.3 21.4 %collective-permute-start.83 = (bf16[80,2048]{1,0:T(8,128)(2,1)S(1)}, bf16[80,2048]{1,0:T(8,128)(2,1)S(1)}, u32[]{:S(2)}, u32[]{:S(2)}) collective-permute-start(bf16[80,2048]{1,0:T(8,128)(2,1)S(1)} %slice.523), channel_id=1, source_target_pairs={{0,2},{1,3},{2,0},{3,1},{4,6},{5,7},{6,4},{7,5},{8,10},{9,11},{10,... | collective-permute-start | bytes 983048 | tf_op jit(solution)/shard_map/ppermute | solution.py:83
  546.9 31.0 %collective-permute-start.55 = (bf16[256,256]{1,0:T(8,128)(2,1)S(1)}, bf16[256,256]{1,0:T(8,128)(2,1)}, u32[]{:S(2)}, u32[]{:S(2)}) collective-permute-start(bf16[256,256]{1,0:T(8,128)(2,1)S(1)} %copy-done.55), channel_id=1, source_target_pairs={{0,2},{1,3},{2,0},{3,1},{4,6},{5,7},{6,4},{7,5},{8,10},{9,11},{10,... | collective-permute-start | bytes 393224 | tf_op jit(solution)/shard_map/ppermute | solution.py:83
  568.1 111.8 %collective-permute-start.74 = (bf16[2048,640]{1,0:T(8,128)(2,1)}, bf16[2048,640]{1,0:T(8,128)(2,1)}, u32[]{:S(2)}, u32[]{:S(2)}) collective-permute-start(bf16[2048,640]{1,0:T(8,128)(2,1)} %constant_dynamic-update-slice_fusion.28), channel_id=1, source_target_pairs={{0,1},{1,0},{2,3},{3,2},{4,5},{5,4},{6,7},{7,6},{8,9},{9,8},{10,11... | collective-permute-start | bytes 7864328 | tf_op jit(solution)/shard_map/ppermute | solution.py:86
  573.8 73.1 %collective-permute-start.79 = (bf16[2048,640]{1,0:T(8,128)(2,1)}, bf16[2048,640]{1,0:T(8,128)(2,1)}, u32[]{:S(2)}, u32[]{:S(2)}) collective-permute-start(bf16[2048,640]{1,0:T(8,128)(2,1)} %constant_dynamic-update-slice_fusion.33), channel_id=1, source_target_pairs={{0,1},{1,0},{2,3},{3,2},{4,5},{5,4},{6,7},{7,6},{8,9},{9,8},{10,11... | collective-permute-start | bytes 7864328 | tf_op jit(solution)/shard_map/ppermute | solution.py:86
  576.8 79.3 %collective-permute-start.84 = (bf16[640,2048]{1,0:T(8,128)(2,1)}, bf16[640,2048]{1,0:T(8,128)(2,1)}, u32[]{:S(2)}, u32[]{:S(2)}) collective-permute-start(bf16[640,2048]{1,0:T(8,128)(2,1)} %constant_dynamic-update-slice_fusion.38), channel_id=1, source_target_pairs={{0,1},{1,0},{2,3},{3,2},{4,5},{5,4},{6,7},{7,6},{8,9},{9,8},{10,11... | collective-permute-start | bytes 7864328 | tf_op jit(solution)/shard_map/ppermute | solution.py:86
  586.7 31.5 %collective-permute-start.56 = (bf16[2048,256]{1,0:T(8,128)(2,1)}, bf16[2048,256]{1,0:T(8,128)(2,1)}, u32[]{:S(2)}, u32[]{:S(2)}) collective-permute-start(bf16[2048,256]{1,0:T(8,128)(2,1)} %constant_dynamic-update-slice_fusion.23), channel_id=1, source_target_pairs={{0,1},{1,0},{2,3},{3,2},{4,5},{5,4},{6,7},{7,6},{8,9},{9,8},{10,11... | collective-permute-start | bytes 3145736 | tf_op jit(solution)/shard_map/ppermute | solution.py:86
  (136 other events, 1481.3 us)
Sparse Core Ops, SparseCore 0:
  10.5 87.0 all-gather.5
  99.2 96.8 all-gather.3
  245.6 50.5 reduce-scatter.7
  298.4 51.7 reduce-scatter.3
  352.4 69.7 reduce-scatter.5
